TPU v7x, 32 devices: a whole 2x2x4 slice. The times are simulated.
32 devices in a mesh: dp: 4 (over z), fsdp: 8 (over y, x, core).
Axes of the slice: x: 2, y: 2, z: 4, core: 2. Of those that a mesh axis runs over, the one named last changes fastest.
Arguments:
- tokens: bfloat16 [16384, 768], P(('dp', 'fsdp')), may hold values from -6 to 6
- condition: bfloat16 [64, 768], P(('dp', 'fsdp')), may hold values from -6 to 6
- ada_weight: bfloat16 [768, 4608], P('fsdp', 'dp'), may hold values from -0.21875 to 0.21875
- qkv_weight: bfloat16 [768, 2304], P('fsdp', 'dp'), may hold values from -0.21875 to 0.21875
- out_weight: bfloat16 [768, 768], P('fsdp', 'dp'), may hold values from -2 to 2
- shared_up: bfloat16 [768, 3072], P('fsdp', 'dp'), may hold values from -0.21875 to 0.21875
- shared_down: bfloat16 [3072, 768], P('fsdp', 'dp'), may hold values from -0.109375 to 0.109375
- router_weight: bfloat16 [768, 8], P('fsdp', 'dp'), may hold values from -0.21875 to 0.21875
- expert_up: bfloat16 [8, 768, 3072], P('dp', 'fsdp'), may hold values from -0.21875 to 0.21875
- expert_down: bfloat16 [8, 3072, 768], P('dp', 'fsdp'), may hold values from -0.109375 to 0.109375
- routes: int32 [16384, 2], P(('dp', 'fsdp')), may hold values from 0 to 7, all different within a row; in each aligned block of 512 rows (0 to 511, 512 to 1023, ...) at most 144 rows name the same one
- image_sizes: int32 [64], P(('dp', 'fsdp')), may hold values from 0 to 512, as said below
- cotangent: bfloat16 [16384, 768], P(('dp', 'fsdp')), may hold values from -6 to 6
Outputs:
- output: bfloat16 [16384, 768], P(('dp', 'fsdp'))
- tokens_grad: float32 [16384, 768], P(('dp', 'fsdp'))
- condition_grad: float32 [64, 768], P(('dp', 'fsdp'))
- ada_grad: float32 [768, 4608], P('fsdp', 'dp')
- qkv_grad: float32 [768, 2304], P('fsdp', 'dp')
- out_grad: float32 [768, 768], P('fsdp', 'dp')
- shared_up_grad: float32 [768, 3072], P('fsdp', 'dp')
- shared_down_grad: float32 [3072, 768], P('fsdp', 'dp')
- router_grad: float32 [768, 8], P('fsdp', 'dp')
- expert_up_grad: float32 [8, 768, 3072], P('dp', 'fsdp')
- expert_down_grad: float32 [8, 3072, 768], P('dp', 'fsdp')
- expert_counts: int32 [8], replicated
Inputs may be any that keep to these rules, and one draw needn't show every extreme that they name: `routes`: each row names two different experts; in the rows of one device no expert is named by more than 144 rows, and in every draw some expert is named by exactly 144 rows of some device. `image_sizes`: each aligned group of 2 entries is either one image of 512 patches followed by zeros, or k images of 256 patches followed by zeros, k from 1 to 2; in every draw some group holds one image of 512 and another holds 2 images of 256.
All inputs are finite; a program needn't handle non-finite values.
Results may differ from a plain program's by a relative error of at most 0.015.
The roundings to bfloat16 on the way count: a program that leaves them out, or rounds other values in their place, can miss the bound.
Values may be sent and summed in bfloat16 or wider, within the bound.
A program may use at most 512 MiB of HBM per device.

v0:
```python
import jax
import jax.numpy as jnp
from jax import lax
from jax.sharding import PartitionSpec as P

HEADS = 12
EXPERTS = 8
CAP = 144
IMG_DEV = 2
LONG = 512


EXACT = lax.Precision.HIGHEST


def owners(image_sizes):
    starts = jnp.cumsum(image_sizes) - image_sizes
    position = jnp.arange(LONG, dtype=jnp.int32)[:, None]
    inside = (position >= starts[None, :]) & (position < (starts + image_sizes)[None, :])
    slot_ids = jnp.arange(IMG_DEV, dtype=jnp.int32)
    segment = jnp.sum(jnp.where(inside, slot_ids[None, :], 0), axis=1) + jnp.where(
        jnp.any(inside, axis=1), 0, IMG_DEV
    )
    return (inside.astype(jnp.float32), segment)


def dispatch_plan(routes):
    flat = routes.reshape(-1)
    onehot = (flat[:, None] == jnp.arange(EXPERTS, dtype=jnp.int32)[None, :]).astype(jnp.int32)
    before = jnp.cumsum(onehot, axis=0) - onehot
    position = jnp.sum(before * onehot, axis=1)
    target = flat * CAP + position
    assignment = jnp.arange(2 * LONG, dtype=jnp.int32)
    source = jnp.zeros((EXPERTS * CAP,), jnp.int32).at[target].set(assignment)
    filled = jnp.zeros((EXPERTS * CAP,), jnp.int32).at[target].set(1)
    return (target, source, filled)


def layer_norm(values_in):
    centred = values_in - jnp.mean(values_in, axis=-1, keepdims=True)
    inv_std = lax.rsqrt(jnp.mean(centred * centred, axis=-1, keepdims=True) + 1e-06)
    return (centred * inv_std, inv_std)


def norm_back(upstream, normed, inv_std):
    return (
        upstream
        - jnp.mean(upstream, axis=-1, keepdims=True)
        - normed * jnp.mean(upstream * normed, axis=-1, keepdims=True)
    ) * inv_std


def gelu_tanh(values_in):
    return jax.nn.gelu(values_in, approximate=True)


def gelu_back(values_in, upstream):
    return jax.vjp(gelu_tanh, values_in)[1](upstream)[0]


def collect(first, second, third):
    widened = (
        lax.all_gather(first, "dp", axis=1, tiled=True),
        lax.all_gather(second, "dp", axis=1, tiled=True),
        lax.all_gather(third, "dp", axis=1, tiled=True),
    )
    return (
        lax.all_gather(widened[0], "fsdp", axis=0, tiled=True),
        lax.all_gather(widened[1], "fsdp", axis=0, tiled=True),
        lax.all_gather(widened[2], "fsdp", axis=0, tiled=True),
    )


def spread(first, second, third):
    row_sums = (
        lax.psum_scatter(first, "fsdp", scatter_dimension=0, tiled=True),
        lax.psum_scatter(second, "fsdp", scatter_dimension=0, tiled=True),
        lax.psum_scatter(third, "fsdp", scatter_dimension=0, tiled=True),
    )
    return (
        lax.psum_scatter(row_sums[0], "dp", scatter_dimension=1, tiled=True),
        lax.psum_scatter(row_sums[1], "dp", scatter_dimension=1, tiled=True),
        lax.psum_scatter(row_sums[2], "dp", scatter_dimension=1, tiled=True),
    )


def gather_experts(up_shard, down_shard):
    return (
        lax.all_gather(up_shard, "fsdp", axis=1, tiled=True),
        lax.all_gather(down_shard, "fsdp", axis=1, tiled=True),
    )


def expert_forward(buffer_in, up_full, down_full):
    expert_pre = jnp.einsum(
        "secd,edf->secf", buffer_in, up_full, preferred_element_type=jnp.float32
    )
    expert_act = gelu_tanh(expert_pre).astype(jnp.bfloat16)
    expert_out = jnp.einsum(
        "secf,efd->secd", expert_act, down_full, preferred_element_type=jnp.float32
    ).astype(jnp.bfloat16)
    return (expert_pre, expert_act, expert_out)


def expert_backward(buffer_in, expert_pre, expert_act, d_out, up_full, down_full):
    d_act = jnp.einsum("secd,efd->secf", d_out, down_full, preferred_element_type=jnp.float32)
    d_pre = gelu_back(expert_pre, d_act).astype(jnp.bfloat16)
    d_rows = jnp.einsum(
        "secf,edf->secd", d_pre, up_full, preferred_element_type=jnp.float32
    ).astype(jnp.bfloat16)
    down_grad = jnp.einsum("secf,secd->efd", expert_act, d_out, preferred_element_type=jnp.float32)
    up_grad = jnp.einsum("secd,secf->edf", buffer_in, d_pre, preferred_element_type=jnp.float32)
    return (up_grad, down_grad, d_rows)


def attend(queries, keys_all, values_all, segment):
    row_count, head_count, head_size = queries.shape
    block_rows = min(512, row_count)
    block_count = row_count // block_rows
    score_scale = head_size ** (-0.5)

    def one_block(pieces):
        query_part, segment_part = pieces
        allowed = (segment_part[:, None] == segment[None, :])[None]
        scores = (
            jnp.einsum("qhd,khd->hqk", query_part, keys_all, preferred_element_type=jnp.float32)
            * score_scale
        )
        scores = jnp.where(allowed, scores, -1e30)
        row_max = jnp.max(scores, axis=-1, keepdims=True)
        weight = jnp.exp(scores - row_max)
        running = jnp.sum(weight, axis=-1, keepdims=True)
        probability = (weight / running).astype(jnp.bfloat16)
        attended = jnp.einsum(
            "hqk,khd->qhd", probability, values_all, preferred_element_type=jnp.float32
        )
        return (attended.astype(jnp.bfloat16), (row_max + jnp.log(running))[:, :, 0])

    return lax.map(
        one_block,
        (
            queries.reshape(block_count, block_rows, head_count, head_size),
            segment.reshape(block_count, block_rows),
        ),
    )


def attend_back(queries, keys_all, values_all, segment, log_totals, d_attended):
    row_count, head_count, head_size = queries.shape
    block_rows = min(512, row_count)
    block_count = row_count // block_rows
    score_scale = head_size ** (-0.5)

    def one_block(carry, pieces):
        key_sum, value_sum = carry
        query_part, segment_part, total_part, grad_part = pieces
        allowed = (segment_part[:, None] == segment[None, :])[None]
        scores = (
            jnp.einsum("qhd,khd->hqk", query_part, keys_all, preferred_element_type=jnp.float32)
            * score_scale
        )
        scores = jnp.where(allowed, scores, -1e30)
        probability = jnp.exp(scores - total_part[:, :, None])
        d_prob = jnp.einsum(
            "qhd,khd->hqk", grad_part, values_all, preferred_element_type=jnp.float32
        )
        d_scores = (
            probability * (d_prob - jnp.sum(probability * d_prob, axis=-1, keepdims=True))
        ).astype(jnp.bfloat16)
        query_grad = (
            jnp.einsum("hqk,khd->qhd", d_scores, keys_all, preferred_element_type=jnp.float32)
            * score_scale
        )
        key_sum = (
            key_sum
            + jnp.einsum("hqk,qhd->khd", d_scores, query_part, preferred_element_type=jnp.float32)
            * score_scale
        )
        value_sum = value_sum + jnp.einsum(
            "hqk,qhd->khd",
            probability.astype(jnp.bfloat16),
            grad_part,
            preferred_element_type=jnp.float32,
        )
        return ((key_sum, value_sum), query_grad)

    empty = jnp.zeros(keys_all.shape, jnp.float32)
    sums, query_grads = lax.scan(
        one_block,
        (empty, empty),
        (
            queries.reshape(block_count, block_rows, head_count, head_size),
            segment.reshape(block_count, block_rows),
            log_totals,
            d_attended.reshape(block_count, block_rows, head_count, head_size),
        ),
    )
    return (query_grads.reshape(row_count, head_count, head_size), sums[0], sums[1])


def shards(
    tokens,
    condition,
    ada_weight,
    qkv_weight,
    out_weight,
    shared_up,
    shared_down,
    router_weight,
    expert_up,
    expert_down,
    routes,
    image_sizes,
    cotangent,
):
    model_width = tokens.shape[1]
    head_size = model_width // HEADS
    inside, segment = owners(image_sizes)
    target, source, filled = dispatch_plan(routes)
    route_hot = (routes[:, :, None] == jnp.arange(EXPERTS, dtype=jnp.int32)[None, None, :]).astype(
        jnp.float32
    )
    live = (segment < IMG_DEV).astype(jnp.int32)
    local_counts = jnp.sum(live[:, None, None] * route_hot.astype(jnp.int32), axis=(0, 1))
    expert_counts = lax.psum(local_counts, ("dp", "fsdp"))
    ada_full, qkv_full, out_full = collect(ada_weight, qkv_weight, out_weight)
    cond_float = condition.astype(jnp.float32)
    activated = jax.nn.silu(cond_float).astype(jnp.bfloat16)
    modulation = jnp.dot(activated, ada_full, preferred_element_type=jnp.float32)
    per_row = jnp.dot(inside, modulation, precision=EXACT, preferred_element_type=jnp.float32)
    shift_one, scale_one, gate_one, shift_two, scale_two, gate_two = jnp.split(per_row, 6, axis=1)
    token_float = tokens.astype(jnp.float32)
    normed_one, inv_one = layer_norm(token_float)
    first_input = (normed_one * (1.0 + scale_one) + shift_one).astype(jnp.bfloat16)
    qkv_rows = jnp.dot(first_input, qkv_full, preferred_element_type=jnp.float32).astype(
        jnp.bfloat16
    )
    queries = qkv_rows[:, :model_width].reshape(-1, HEADS, head_size)
    keys_all = qkv_rows[:, model_width : 2 * model_width].reshape(-1, HEADS, head_size)
    values_all = qkv_rows[:, 2 * model_width :].reshape(-1, HEADS, head_size)
    attended_blocks, log_totals = attend(queries, keys_all, values_all, segment)
    attended = attended_blocks.reshape(-1, model_width)
    projected = jnp.dot(attended, out_full, preferred_element_type=jnp.float32)
    residual_one = token_float + gate_one * projected
    normed_two, inv_two = layer_norm(residual_one)
    second_input = (normed_two * (1.0 + scale_two) + shift_two).astype(jnp.bfloat16)
    shared_first, shared_second, router_full = collect(shared_up, shared_down, router_weight)
    shared_pre = jnp.dot(second_input, shared_first, preferred_element_type=jnp.float32)
    shared_act = gelu_tanh(shared_pre).astype(jnp.bfloat16)
    shared_out = jnp.dot(shared_act, shared_second, preferred_element_type=jnp.float32)
    logits = jnp.dot(second_input, router_full, preferred_element_type=jnp.float32)
    chosen = jnp.sum(logits[:, None, :] * route_hot, axis=-1)
    gate_share = jax.nn.softmax(chosen, axis=-1)
    buffer_rows = jnp.take(second_input, source // 2, axis=0).reshape(EXPERTS, CAP, model_width)
    up_full, down_full = gather_experts(expert_up, expert_down)
    groups = lax.axis_size("dp")
    expert_in = lax.all_to_all(
        buffer_rows.reshape(groups, EXPERTS // groups, CAP, model_width),
        "dp",
        split_axis=0,
        concat_axis=0,
        tiled=True,
    )
    expert_pre, expert_act, expert_out = expert_forward(expert_in, up_full, down_full)
    returned = lax.all_to_all(expert_out, "dp", split_axis=0, concat_axis=0, tiled=True).reshape(
        EXPERTS, CAP, model_width
    )
    picked = (
        jnp.take(returned.reshape(EXPERTS * CAP, model_width), target, axis=0)
        .reshape(-1, 2, model_width)
        .astype(jnp.float32)
    )
    mixed = shared_out + jnp.sum(gate_share[:, :, None] * picked, axis=1)
    output = (residual_one + gate_two * mixed).astype(jnp.bfloat16)
    upstream = cotangent.astype(jnp.float32)
    d_mixed = gate_two * upstream
    d_gate_two = upstream * mixed
    d_gate_share = jnp.sum(d_mixed[:, None, :] * picked, axis=-1)
    slot_gate = jnp.take(gate_share.reshape(-1), source) * filled.astype(jnp.float32)
    d_buffer = (
        (jnp.take(d_mixed, source // 2, axis=0) * slot_gate[:, None])
        .astype(jnp.bfloat16)
        .reshape(EXPERTS, CAP, model_width)
    )
    shared_first, shared_second, router_full = collect(shared_up, shared_down, router_weight)
    up_full, down_full = gather_experts(expert_up, expert_down)
    arrived = lax.all_to_all(
        d_buffer.reshape(groups, EXPERTS // groups, CAP, model_width),
        "dp",
        split_axis=0,
        concat_axis=0,
        tiled=True,
    )
    up_grad, down_grad, d_rows = expert_backward(
        expert_in, expert_pre, expert_act, arrived, up_full, down_full
    )
    d_returned = lax.all_to_all(d_rows, "dp", split_axis=0, concat_axis=0, tiled=True).reshape(
        EXPERTS, CAP, model_width
    )
    expert_sums = (
        lax.psum_scatter(up_grad, "fsdp", scatter_dimension=1, tiled=True),
        lax.psum_scatter(down_grad, "fsdp", scatter_dimension=1, tiled=True),
    )
    d_shared = d_mixed.astype(jnp.bfloat16)
    shared_second_grad = jnp.einsum(
        "tf,td->fd", shared_act, d_shared, preferred_element_type=jnp.float32
    )
    d_shared_act = jnp.einsum(
        "td,fd->tf", d_shared, shared_second, preferred_element_type=jnp.float32
    )
    d_shared_pre = gelu_back(shared_pre, d_shared_act).astype(jnp.bfloat16)
    shared_first_grad = jnp.einsum(
        "td,tf->df", second_input, d_shared_pre, preferred_element_type=jnp.float32
    )
    d_chosen = gate_share * (
        d_gate_share - jnp.sum(gate_share * d_gate_share, axis=-1, keepdims=True)
    )
    d_logits = jnp.sum(d_chosen[:, :, None] * route_hot, axis=1).astype(jnp.bfloat16)
    router_grad = jnp.einsum(
        "td,te->de", second_input, d_logits, preferred_element_type=jnp.float32
    )
    from_experts = (
        jnp.take(d_returned.reshape(EXPERTS * CAP, model_width), target, axis=0)
        .reshape(-1, 2, model_width)
        .astype(jnp.float32)
    )
    d_second = (
        jnp.einsum("tf,df->td", d_shared_pre, shared_first, preferred_element_type=jnp.float32)
        + jnp.einsum("te,de->td", d_logits, router_full, preferred_element_type=jnp.float32)
        + jnp.sum(from_experts, axis=1)
    )
    mlp_sums = spread(shared_first_grad, shared_second_grad, router_grad)
    d_scale_two = d_second * normed_two
    d_residual = upstream + norm_back(d_second * (1.0 + scale_two), normed_two, inv_two)
    ada_full, qkv_full, out_full = collect(ada_weight, qkv_weight, out_weight)
    d_projected = (gate_one * d_residual).astype(jnp.bfloat16)
    d_gate_one = d_residual * projected
    out_grad = jnp.einsum("td,te->de", attended, d_projected, preferred_element_type=jnp.float32)
    d_attended = jnp.einsum(
        "te,de->td", d_projected, out_full, preferred_element_type=jnp.float32
    ).astype(jnp.bfloat16)
    d_queries, d_keys, d_values = attend_back(
        queries, keys_all, values_all, segment, log_totals, d_attended.reshape(-1, HEADS, head_size)
    )
    d_qkv = jnp.concatenate(
        [
            d_queries.reshape(-1, model_width),
            d_keys.reshape(-1, model_width),
            d_values.reshape(-1, model_width),
        ],
        axis=1,
    ).astype(jnp.bfloat16)
    qkv_grad = jnp.einsum("td,te->de", first_input, d_qkv, preferred_element_type=jnp.float32)
    d_first = jnp.einsum("te,de->td", d_qkv, qkv_full, preferred_element_type=jnp.float32)
    d_scale_one = d_first * normed_one
    tokens_grad = d_residual + norm_back(d_first * (1.0 + scale_one), normed_one, inv_one)
    d_per_row = jnp.concatenate(
        [d_first, d_scale_one, d_gate_one, d_second, d_scale_two, d_gate_two], axis=1
    )
    d_modulation = jnp.einsum(
        "tj,te->je", inside, d_per_row, precision=EXACT, preferred_element_type=jnp.float32
    ).astype(jnp.bfloat16)
    ada_grad = jnp.einsum("jd,je->de", activated, d_modulation, preferred_element_type=jnp.float32)
    d_activated = jnp.einsum(
        "je,de->jd", d_modulation, ada_full, preferred_element_type=jnp.float32
    )
    condition_grad = jax.vjp(jax.nn.silu, cond_float)[1](d_activated)[0]
    attn_sums = spread(ada_grad, qkv_grad, out_grad)
    return (
        output,
        tokens_grad,
        condition_grad,
        attn_sums[0],
        attn_sums[1],
        attn_sums[2],
        mlp_sums[0],
        mlp_sums[1],
        mlp_sums[2],
        expert_sums[0],
        expert_sums[1],
        expert_counts,
    )


def solution(mesh):
    placed = (
        P(("dp", "fsdp"), None),
        P(("dp", "fsdp"), None),
        P("fsdp", "dp"),
        P("fsdp", "dp"),
        P("fsdp", "dp"),
        P("fsdp", "dp"),
        P("fsdp", "dp"),
        P("fsdp", "dp"),
        P("dp", "fsdp", None),
        P("dp", "fsdp", None),
        P(("dp", "fsdp"), None),
        P(("dp", "fsdp")),
        P(("dp", "fsdp"), None),
    )
    return jax.shard_map(
        shards,
        mesh=mesh,
        in_specs=placed,
        out_specs=(
            P(("dp", "fsdp"), None),
            P(("dp", "fsdp"), None),
            P(("dp", "fsdp"), None),
            P("fsdp", "dp"),
            P("fsdp", "dp"),
            P("fsdp", "dp"),
            P("fsdp", "dp"),
            P("fsdp", "dp"),
            P("fsdp", "dp"),
            P("dp", "fsdp", None),
            P("dp", "fsdp", None),
            P(),
        ),
        check_vma=False,
    )
```

profile of v0, /device:TPU:0, one launch (start us, length us, event | category | flops | bytes accessed | tf_op | source)
XLA Modules:
  0.0 1420.0 jit_solution(14664628744125656856)
XLA Ops:
  7.3 23.3 %all_gather.56 = bf16[96,4608]{1,0:T(8,128)(2,1)} all-gather(bf16[96,1152]{1,0:T(8,128)(2,1)} %param.17), channel_id=1, replica_groups=mesh['dp'=4,'fsdp'=8] {'dp'}, dimensions={1}, use_global_device_ids=true | all-gather | bytes 1105920 | tf_op jit(solution)/shard_map/all_gather | solution.py:63
  30.6 16.1 %all-gather = bf16[4,576,96]{1,2,0:T(8,128)(2,1)S(1)} all-gather(bf16[1,576,96]{1,2,0:T(8,128)(2,1)} %bitcast.192), channel_id=1, replica_groups=mesh['dp'=4,'fsdp'=8] {'dp'}, dimensions={0}, use_global_device_ids=true | all-gather | bytes 552960 | tf_op jit(solution)/shard_map/all_gather | solution.py:64
  48.3 14.1 all_gather.60
  64.4 15.7 %all_gather.62 = bf16[96,3072]{1,0:T(8,128)(2,1)} all-gather(bf16[96,768]{1,0:T(8,128)(2,1)S(1)} %copy-done.32), channel_id=1, replica_groups=mesh['dp'=4,'fsdp'=8] {'dp'}, dimensions={1}, use_global_device_ids=true | all-gather | bytes 737280 | tf_op jit(solution)/shard_map/all_gather | solution.py:63
  155.5 46.1 %all_to_all.20 = bf16[4,2,144,768]{3,2,1,0:T(8,128)(2,1)} all-to-all(bf16[4,2,144,768]{3,2,1,0:T(8,128)(2,1)S(1)} %broadcast_select_fusion), channel_id=1, replica_groups=mesh['dp'=4,'fsdp'=8] {'dp'}, dimensions={0} | all-to-all | bytes 3538944 | tf_op jit(solution)/shard_map/all_to_all | solution.py:257
  202.2 12.8 fusion.15
  215.0 47.7 %all-gather.23.cloned.1.call-done = bf16[2,3072,768]{2,1,0:T(8,128)(2,1)} async-done(((bf16[2,384,768]{2,1,0:T(8,128)(2,1)}), bf16[2,3072,768]{2,1,0:T(8,128)(2,1)}) %all-gather.23.cloned.1.call-update) | async-done | bytes 9437200 | tf_op jit(solution)/shard_map/all_gather | solution.py:90
  281.1 53.3 %all_gather.64 = bf16[384,768]{0,1:T(8,128)(2,1)} all-gather(bf16[384,192]{0,1:T(8,128)(2,1)S(1)} %copy-done.33), channel_id=1, replica_groups=mesh['dp'=4,'fsdp'=8] {'dp'}, dimensions={1}, use_global_device_ids=true | all-gather | bytes 737280 | tf_op jit(solution)/shard_map/all_gather | solution.py:64
  403.9 35.2 %all-to-all-done.2 = bf16[4,2,144,768]{3,2,1,0:T(8,128)(2,1)} async-done(((bf16[4,2,144,768]{3,2,1,0:T(8,128)(2,1)}), bf16[4,2,144,768]{3,2,1,0:T(8,128)(2,1)}, u32[]{:S(2)}, u32[]{:S(2)}) %all-to-all-start.2) | async-done | bytes 1769504 | tf_op jit(solution)/shard_map/all_to_all | solution.py:287
  439.0 19.5 %fusion.6 = bf16[4,2,144,3072]{3,2,0,1:T(8,128)(2,1)} fusion(f32[2,4,144,3072]{3,2,1,0:T(8,128)} %fusion.15, bf16[2,3072,768]{2,1,0:T(8,128)(2,1)} %all-gather.23.cloned.1.call-done, bf16[4,2,144,768]{3,2,1,0:T(8,128)(2,1)} %all-to-all-done.2), kind=kOutput, calls=%fused_computation.15 | convolution fusion | flops 5506596864 | bytes 32440320 | tf_op jit(solution)/shard_map/secd,efd->secf/dot_general | solution.py:106
  491.8 24.3 %all-to-all-done.3 = bf16[4,2,144,768]{3,2,1,0:T(8,128)(2,1)} async-done(((bf16[4,2,144,768]{3,2,1,0:T(8,128)(2,1)}), bf16[4,2,144,768]{3,2,1,0:T(8,128)(2,1)}, u32[]{:S(2)}, u32[]{:S(2)}) %all-to-all-start.3) | async-done | bytes 1769504 | tf_op jit(solution)/shard_map/all_to_all | solution.py:297
  550.5 16.3 %multiply_reduce_fusion.2 = f32[512,768]{1,0:T(8,128)S(1)} fusion(f32[512,2,768]{2,1,0:T(2,128)} %reshape.359, f32[512,2]{1,0:T(8,128)S(1)} %copy.138), kind=kLoop, calls=%fused_computation.60 | loop fusion | flops 1179648 | bytes 4722688 | tf_op jit(solution)/shard_map/reduce_sum | solution.py:273
  664.0 31.7 %reduce-scatter.26.cloned.1.call-done = f32[96,2304]{1,0:T(8,128)} async-done(((f32[768,2304]{1,0:T(8,128)}), f32[96,2304]{1,0:T(8,128)}) %reduce-scatter.26.cloned.1.call-update) | async-done | bytes 884752 | tf_op jit(solution)/shard_map/reduce_scatter | solution.py:77
  698.3 77.6 %reduce-scatter.30.cloned.1.call-done = f32[96,3072]{1,0:T(8,128)} async-done(((f32[768,3072]{1,0:T(8,128)}), f32[96,3072]{1,0:T(8,128)}) %reduce-scatter.30.cloned.1.call-update) | async-done | bytes 1179664 | tf_op jit(solution)/shard_map/reduce_scatter | solution.py:76
  775.9 80.3 %reduce-scatter.34.cloned.1.call-done = f32[384,768]{1,0:T(8,128)} async-done(((f32[3072,768]{1,0:T(8,128)}), f32[384,768]{1,0:T(8,128)}) %reduce-scatter.34.cloned.1.call-update) | async-done | bytes 1179664 | tf_op jit(solution)/shard_map/reduce_scatter | solution.py:77
  858.9 102.5 %reduce-scatter.22.cloned.1.call-done = f32[96,4608]{1,0:T(8,128)} async-done(((f32[768,4608]{1,0:T(8,128)}), f32[96,4608]{1,0:T(8,128)}) %reduce-scatter.22.cloned.1.call-update) | async-done | bytes 1769488 | tf_op jit(solution)/shard_map/reduce_scatter | solution.py:76
  961.9 16.6 %convolution_bitcast_fusion = f32[2,3072,768]{2,1,0:T(8,128)} fusion(bf16[4,2,144,768]{3,2,1,0:T(8,128)(2,1)} %all-to-all-done.2, f32[2,4,144,3072]{3,2,1,0:T(8,128)} %fusion.15), kind=kOutput, calls=%fused_computation.41 | convolution fusion | flops 5467668480 | bytes 34799616 | tf_op jit(solution)/shard_map/secf,secd->efd/dot_general | solution.py:111
  980.0 13.6 convolution_bitcast_fusion.1
  994.4 39.5 %psum.7 = s32[8]{0:T(128)} all-reduce(s32[8]{0:T(128)S(1)} %multiply_reduce_fusion.5), channel_id=1, replica_groups=mesh['dp'=4,'fsdp'=8] {'dp','fsdp'}, use_global_device_ids=true, to_apply=%region_42.44 | all-reduce | flops 8 | bytes 64 | tf_op jit(solution)/shard_map/psum | solution.py:225
  1056.8 25.5 %reduce-scatter.32.cloned.1.call-done = f32[96,768]{1,0:T(8,128)} async-done(((f32[96,3072]{1,0:T(8,128)}), f32[96,768]{1,0:T(8,128)}) %reduce-scatter.32.cloned.1.call-update) | async-done | bytes 294928 | tf_op jit(solution)/shard_map/reduce_scatter | solution.py:81
  1082.3 30.7 %reduce-scatter.44.cloned.1.call-done = f32[192,384]{1,0:T(8,128)} async-done(((f32[768,384]{1,0:T(8,128)}), f32[192,384]{1,0:T(8,128)}) %reduce-scatter.44.cloned.1.call-update) | async-done | bytes 294928
  1113.0 39.9 %reduce-scatter.24.cloned.1.call-done = f32[96,1152]{1,0:T(8,128)} async-done(((f32[96,4608]{1,0:T(8,128)}), f32[96,1152]{1,0:T(8,128)}) %reduce-scatter.24.cloned.1.call-update) | async-done | bytes 442384 | tf_op jit(solution)/shard_map/reduce_scatter | solution.py:81
  1152.9 129.6 %reduce-scatter.38.cloned.1.call-done = f32[2,384,768]{2,1,0:T(8,128)} async-done(((f32[2,3072,768]{2,1,0:T(8,128)}), f32[2,384,768]{2,1,0:T(8,128)}) %reduce-scatter.38.cloned.1.call-update) | async-done | bytes 2359312 | tf_op jit(solution)/shard_map/reduce_scatter | solution.py:302
  1282.5 130.5 %reduce-scatter.36.cloned.1.call-done = f32[2,96,3072]{2,1,0:T(8,128)} async-done(((f32[2,768,3072]{2,1,0:T(8,128)}), f32[2,96,3072]{2,1,0:T(8,128)}) %reduce-scatter.36.cloned.1.call-update) | async-done | bytes 2359312 | tf_op jit(solution)/shard_map/reduce_scatter | solution.py:301
  (302 shorter events, 361.8 us)
Async XLA Ops:
  7.2 73.3 %copy-start.34 = (s32[512,2]{0,1:T(2,128)S(1)}, s32[512,2]{0,1:T(2,128)}, u32[]{:S(2)}) copy-start(s32[512,2]{0,1:T(2,128)} %param.25) | copy-start | bytes 12292
  7.2 83.7 %all-gather.11.cloned.1.call-start = ((), (), s32[]{:S(2)}) async-start(), calls=%async_computation.17 | async-start | bytes 7962624 | tf_op jit(solution)/shard_map/all_gather | solution.py:68
  30.6 84.7 %all-gather.13.cloned.1.call-start = ((), (), s32[]{:S(2)}) async-start(), calls=%async_computation.18 | async-start | bytes 3981312 | tf_op jit(solution)/shard_map/all_gather | solution.py:69
  48.2 93.5 %all-gather.15.cloned.1.call-start = ((), (), s32[]{:S(2)}) async-start(), calls=%async_computation.19 | async-start | bytes 1327104 | tf_op jit(solution)/shard_map/all_gather | solution.py:70
  63.2 139.0 %all-gather.21.cloned.1.call-start = ((), (), s32[]{:S(2)}) async-start(), calls=%async_computation.22 | async-start | bytes 10616832 | tf_op jit(solution)/shard_map/all_gather | solution.py:89
  63.8 198.9 %all-gather.23.cloned.1.call-start = ((), (), s32[]{:S(2)}) async-start(), calls=%async_computation.23 | async-start | bytes 10616832 | tf_op jit(solution)/shard_map/all_gather | solution.py:90
  64.4 332.6 %all-gather.17.cloned.1.call-start = ((), (), s32[]{:S(2)}) async-start(), calls=%async_computation.20 | async-start | bytes 5308416 | tf_op jit(solution)/shard_map/all_gather | solution.py:68
  276.5 96.1 %all-to-all-start.1 = ((bf16[4,2,144,768]{3,2,1,0:T(8,128)(2,1)}), bf16[4,2,144,768]{3,2,1,0:T(8,128)(2,1)}, u32[]{:S(2)}, u32[]{:S(2)}) async-start(bf16[4,2,144,768]{3,2,1,0:T(8,128)(2,1)} %copy.143), calls=%async_computation.1 | async-start | bytes 3538944 | tf_op jit(solution)/shard_map/all_to_all | solution.py:265
  281.0 194.2 %all-gather.19.cloned.1.call-start = ((), (), s32[]{:S(2)}) async-start(), calls=%async_computation.21 | async-start | bytes 5308416 | tf_op jit(solution)/shard_map/all_gather | solution.py:69
  392.4 46.6 %all-to-all-start.2 = ((bf16[4,2,144,768]{3,2,1,0:T(8,128)(2,1)}), bf16[4,2,144,768]{3,2,1,0:T(8,128)(2,1)}, u32[]{:S(2)}, u32[]{:S(2)}) async-start(bf16[4,2,144,768]{3,2,1,0:T(8,128)(2,1)} %multiply_convert_fusion.2), calls=%async_computation.2 | async-start | bytes 3538944 | tf_op jit(solution)/shard_map/all_to_all | solution.py:287
  470.5 45.6 %all-to-all-start.3 = ((bf16[4,2,144,768]{3,2,1,0:T(8,128)(2,1)}), bf16[4,2,144,768]{3,2,1,0:T(8,128)(2,1)}, u32[]{:S(2)}, u32[]{:S(2)}) async-start(bf16[4,2,144,768]{3,2,1,0:T(8,128)(2,1)} %copy.148), calls=%async_computation.3 | async-start | bytes 3538944 | tf_op jit(solution)/shard_map/all_to_all | solution.py:297
  474.9 187.0 %reduce-scatter.28.cloned.1.call-start = ((), (), s32[]{:S(2)}) async-start(), calls=%async_computation.27 | async-start | bytes 2654208 | tf_op jit(solution)/shard_map/reduce_scatter | solution.py:78
  585.9 109.7 %reduce-scatter.26.cloned.1.call-start = ((), (), s32[]{:S(2)}) async-start(), calls=%async_computation.26 | async-start | bytes 7962624 | tf_op jit(solution)/shard_map/reduce_scatter | solution.py:77
  619.0 156.8 %reduce-scatter.30.cloned.1.call-start = ((), (), s32[]{:S(2)}) async-start(), calls=%async_computation.28 | async-start | bytes 10616832 | tf_op jit(solution)/shard_map/reduce_scatter | solution.py:76
  626.2 229.9 %reduce-scatter.34.cloned.1.call-start = ((), (), s32[]{:S(2)}) async-start(), calls=%async_computation.30 | async-start | bytes 10616832 | tf_op jit(solution)/shard_map/reduce_scatter | solution.py:77
  636.3 325.1 %reduce-scatter.22.cloned.1.call-start = ((), (), s32[]{:S(2)}) async-start(), calls=%async_computation.24 | async-start | bytes 15925248 | tf_op jit(solution)/shard_map/reduce_scatter | solution.py:76
  660.6 374.6 %reduce-scatter.46.cloned.1.call-start = ((), (), s32[]{:S(2)}) async-start(), calls=%async_computation.36 | async-start | bytes 442368
  661.9 391.5 %reduce-scatter.42.cloned.1.call-start = ((), (), s32[]{:S(2)}) async-start(), calls=%async_computation.34 | async-start | bytes 491520
  663.9 391.1 %reduce-scatter.40.cloned.1.call-start = ((), (), s32[]{:S(2)}) async-start(), calls=%async_computation.33 | async-start | bytes 1474560
  698.2 384.1 %reduce-scatter.32.cloned.1.call-start = ((), (), s32[]{:S(2)}) async-start(), calls=%async_computation.29 | async-start | bytes 1474560 | tf_op jit(solution)/shard_map/reduce_scatter | solution.py:81
  775.9 337.2 %reduce-scatter.44.cloned.1.call-start = ((), (), s32[]{:S(2)}) async-start(), calls=%async_computation.35 | async-start | bytes 1474560
  858.9 294.0 %reduce-scatter.24.cloned.1.call-start = ((), (), s32[]{:S(2)}) async-start(), calls=%async_computation.25 | async-start | bytes 2211840 | tf_op jit(solution)/shard_map/reduce_scatter | solution.py:81
  961.5 321.1 %reduce-scatter.38.cloned.1.call-start = ((), (), s32[]{:S(2)}) async-start(), calls=%async_computation.32 | async-start | bytes 21233664 | tf_op jit(solution)/shard_map/reduce_scatter | solution.py:302
  978.5 434.5 %reduce-scatter.36.cloned.1.call-start = ((), (), s32[]{:S(2)}) async-start(), calls=%async_computation.31 | async-start | bytes 21233664 | tf_op jit(solution)/shard_map/reduce_scatter | solution.py:301
  (58 other events, 726.4 us)
Sparse Core Ops, SparseCore 0:
  30.7 48.2 all-gather.10
  81.4 33.8 all-gather.12
  117.7 23.9 all-gather.14
  143.5 58.6 all-gather.20
  203.9 58.6 all-gather.22
  264.4 38.7 all-gather.16
  334.5 39.8 all-gather.18
  586.0 40.4 reduce-scatter.27
  630.1 65.5 reduce-scatter.25
  699.0 76.8 reduce-scatter.29
  779.3 76.8 reduce-scatter.33
  859.6 101.7 reduce-scatter.21
  964.5 33.8 reduce-scatter.45
  1000.5 21.0 reduce-scatter.41
  1023.8 27.7 reduce-scatter.39
  1054.4 27.9 reduce-scatter.31
  1085.1 27.9 reduce-scatter.43
  1115.8 37.0 reduce-scatter.23
  1157.1 125.3 reduce-scatter.37
  1286.6 126.4 reduce-scatter.35
where the time goes:
time: 1430 us; the launch traced here: 1420 us
  waiting for transfers between devices  778 us (54%)
  blocking collectives  240 us (17%)
  matrix products  215 us (15%)
  local copies, waits for them, and re-layouts  95.5 us (7%)
  other arithmetic  60.1 us (4%)
  between operations  16.1 us (1%)
  starting transfers between devices  15.2 us (1%)
    reduce_scatter x2, waiting for transfers between devices, spread(): lax.psum_scatter(first, 'fsdp', scatter_dimension=0, tiled=True)  180 us
    reduce_scatter x1, waiting for transfers between devices, shards(): lax.psum_scatter(up_grad, 'fsdp', scatter_dimension=1, tiled=True)  131 us
    reduce_scatter x1, waiting for transfers between devices, shards(): lax.psum_scatter(down_grad, 'fsdp', scatter_dimension=1, tiled=True)  130 us
    reduce_scatter x2, waiting for transfers between devices, spread(): lax.psum_scatter(second, 'fsdp', scatter_dimension=0, tiled=True)  112 us
    all_gather x2, blocking collectives, collect(): lax.all_gather(second, 'dp', axis=1, tiled=True)  69.3 us
    reduce_scatter x2, waiting for transfers between devices, spread(): lax.psum_scatter(row_sums[0], 'dp', scatter_dimension=1, tiled=True)  65.4 us
    all_gather x1, waiting for transfers between devices, gather_experts(): lax.all_gather(down_shard, 'fsdp', axis=1, tiled=True)  47.7 us
    all_to_all x1, blocking collectives, shards(): lax.all_to_all(buffer_rows.reshape(groups, EXPERTS // groups, CAP, model_...  46.1 us
  transfers between devices with their start and end apart: 23, of which 15 were waited for; matrix products, arithmetic and copies ran while one was open for 20% of the time, Pallas kernels for 0%

commit v1 on v0

--- a/solution.py
+++ b/solution.py
@@ -1,6 +1,10 @@
+import functools
+
 import jax
 import jax.numpy as jnp
 from jax import lax
+from jax.experimental import pallas as pl
+from jax.experimental.pallas import tpu as pltpu
 from jax.sharding import PartitionSpec as P
 
 HEADS = 12
@@ -8,6 +12,7 @@
 CAP = 144
 IMG_DEV = 2
 LONG = 512
+MESH = pl.DeviceIdType.MESH
 
 
 EXACT = lax.Precision.HIGHEST
@@ -382,6 +387,888 @@
     )
 
 
+def at(d, s, c):
+    return (d, 2 * s + c)
+
+
+def slot(kind, f, d):
+    if kind == "cols":
+        return (pl.ds(pl.multiple_of(96 * f, 96), 96), pl.ds(pl.multiple_of(768 * d, 768), 768))
+    return (pl.ds(pl.multiple_of(192 * d, 192), 192), pl.ds(pl.multiple_of(384 * f, 384), 384))
+
+
+def half_slot(kind, f, d, h):
+    if kind == "cols":
+        return (
+            pl.ds(pl.multiple_of(96 * f, 96), 96),
+            pl.ds(pl.multiple_of(768 * d + 384 * h, 384), 384),
+        )
+    return (
+        pl.ds(pl.multiple_of(192 * d + 96 * h, 96), 96),
+        pl.ds(pl.multiple_of(384 * f, 384), 384),
+    )
+
+
+def place():
+    d = lax.axis_index("dp")
+    f = lax.axis_index("fsdp")
+    return d, f // 2, lax.rem(f, 2)
+
+
+def flip(v, bit):
+    return v + bit - 2 * bit * lax.rem(v // bit, 2)
+
+
+def greet(devices):
+    barrier = pltpu.get_barrier_semaphore()
+    for device in devices:
+        pl.semaphore_signal(barrier, inc=1, device_id=device, device_id_type=MESH)
+    pl.semaphore_wait(barrier, len(devices))
+
+
+def push(src, dst, send_sem, recv_sem, device):
+    return pltpu.make_async_remote_copy(
+        src_ref=src,
+        dst_ref=dst,
+        send_sem=send_sem,
+        recv_sem=recv_sem,
+        device_id=device,
+        device_id_type=MESH,
+    )
+
+
+GATHER_SEMS = 3 + 8 + 8 + 20
+
+
+class Gather:
+    def __init__(self, kind, shard, full, ssem, rsem, lsem):
+        self.kind, self.shard, self.full = kind, shard, full
+        self.ssem, self.rsem, self.lsem = ssem, rsem, lsem
+        self.d, self.s, self.c = place()
+        self.sent = []
+
+    def f(self, s):
+        return 2 * s + self.c
+
+    def go(self, index, where, device, src=None):
+        ref = self.full.at[where]
+        copy = push(
+            ref if src is None else src, ref, self.ssem.at[index], self.rsem.at[index], device
+        )
+        copy.start()
+        self.sent.append(copy)
+
+    def arrived(self, index, where):
+        ref = self.full.at[where]
+        push(ref, ref, self.ssem.at[index], self.rsem.at[index], at(self.d, self.s, self.c)).wait_recv()
+
+    def start(self):
+        d, s, c = self.d, self.s, self.c
+        mine = slot(self.kind, self.f(s), d)
+        self.own = pltpu.make_async_copy(self.shard, self.full.at[mine], self.lsem)
+        self.own.start()
+        for k in range(1, 4):
+            self.go(k - 1, mine, at(lax.rem(d + k, 4), s, c), self.shard)
+        self.go(3, mine, at(d, flip(s, 1), c), self.shard)
+        self.go(4, mine, at(d, flip(s, 2), c), self.shard)
+        self.go(19, mine, at(d, s, 1 - c), self.shard)
+
+    def spread_z(self, k):
+        d, s, c = self.d, self.s, self.c
+        source = lax.rem(d + 4 - k, 4)
+        block = slot(self.kind, self.f(s), source)
+        self.arrived(k - 1, block)
+        self.go(3 + 2 * k, block, at(d, flip(s, 1), c))
+        self.go(4 + 2 * k, block, at(d, flip(s, 2), c))
+        self.go(19 + 5 * k, block, at(d, s, 1 - c))
+
+    def relay(self, k):
+        d, s, c = self.d, self.s, self.c
+        source = lax.rem(d + 4 - k, 4)
+        sx, sy = flip(s, 1), flip(s, 2)
+        from_x = slot(self.kind, self.f(sx), source)
+        from_y = slot(self.kind, self.f(sy), source)
+        self.arrived(3 + 2 * k, from_x)
+        self.go(11 + 2 * k, half_slot(self.kind, self.f(sx), source, 0), at(d, sy, c))
+        self.go(20 + 5 * k, from_x, at(d, s, 1 - c))
+        self.arrived(4 + 2 * k, from_y)
+        self.go(12 + 2 * k, half_slot(self.kind, self.f(sy), source, 1), at(d, sx, c))
+        self.go(21 + 5 * k, from_y, at(d, s, 1 - c))
+
+    def corner(self, k):
+        d, s, c = self.d, self.s, self.c
+        source = lax.rem(d + 4 - k, 4)
+        sd = flip(flip(s, 1), 2)
+        for h in range(2):
+            where = half_slot(self.kind, self.f(sd), source, h)
+            self.arrived(11 + 2 * k + h, where)
+            self.go(22 + 5 * k + h, where, at(d, s, 1 - c))
+
+    def finish(self):
+        d, s, c = self.d, self.s, self.c
+        sx, sy = flip(s, 1), flip(s, 2)
+        sd = flip(sx, 2)
+        self.own.wait()
+        for k in range(4):
+            source = lax.rem(d + 4 - k, 4)
+            for j, position in enumerate((s, sx, sy)):
+                self.arrived(19 + 5 * k + j, slot(self.kind, 2 * position + 1 - c, source))
+            for h in range(2):
+                self.arrived(22 + 5 * k + h, half_slot(self.kind, 2 * sd + 1 - c, source, h))
+        for copy in self.sent:
+            copy.wait_send()
+
+
+def everyone_else():
+    me = lax.axis_index("dp") * 8 + lax.axis_index("fsdp")
+
+    def other(k):
+        device = lax.rem(me + k, 32)
+        return (device // 8, lax.rem(device, 8))
+
+    return me, other
+
+
+def open_kernel(
+    shard, router, act_ref, ada_ref, full, routers, seen, rows_out,
+    heard, part, got, mixed, ssem, rsem, lsem, asem, brsem, rssem, rrsem, tssem, trsem, zssem, zrsem,
+):
+    me, other = everyone_else()
+    d, s, c = place()
+    f = 2 * s + c
+    barrier = pltpu.get_barrier_semaphore()
+
+    def hello(k, carry):
+        pl.semaphore_signal(barrier, inc=1, device_id=other(k), device_id_type=MESH)
+        return carry
+
+    lax.fori_loop(1, 32, hello, 0)
+    pl.semaphore_wait(barrier, 31)
+
+    def act_copy(k, source):
+        device = other(k)
+        return push(act_ref.at[device[1]], heard.at[source], asem.at[k], brsem.at[k], device)
+
+    def router_copy(k, source):
+        return push(router, routers.at[source], rssem.at[k], rrsem.at[k], other(k))
+
+    def send(k, carry):
+        act_copy(k, me).start()
+        return carry
+
+    lax.fori_loop(1, 32, send, 0)
+    gather = Gather("cols", shard, full, ssem, rsem, lsem.at[0])
+    gather.start()
+    own_router = pltpu.make_async_copy(router, routers.at[me], lsem.at[1])
+    own_router.start()
+
+    def send_router(k, carry):
+        router_copy(k, me).start()
+        return carry
+
+    lax.fori_loop(1, 32, send_router, 0)
+    heard[me] = act_ref[f]
+
+    def take(k, carry):
+        copy = act_copy(k, lax.rem(me + 32 - k, 32))
+        copy.wait_recv()
+        return carry
+
+    lax.fori_loop(1, 32, take, 0)
+    everything = heard[...].reshape(256, 128)
+    row = lax.broadcasted_iota(jnp.int32, (64, 256), 0)
+    column = lax.broadcasted_iota(jnp.int32, (64, 256), 1)
+    source = lax.rem(row // 2, 4) * 8 + row // 8
+    pick = (column == source * 8 + lax.rem(row, 2)).astype(jnp.bfloat16)
+    compact = jnp.dot(
+        pick, everything.astype(jnp.bfloat16), preferred_element_type=jnp.float32
+    ).astype(jnp.bfloat16)
+    seen[...] = jnp.concatenate(
+        [compact.astype(jnp.float32), jnp.sum(heard[...], axis=0)], axis=0
+    )
+    part[...] = jnp.dot(compact, ada_ref[...], preferred_element_type=jnp.float32).reshape(
+        8, 8, 1152
+    )
+
+    def tile_copy(k):
+        target = lax.rem(f + k, 8)
+        return push(part.at[target], got.at[k], tssem.at[k], trsem.at[k], (d, target))
+
+    for k in range(1, 8):
+        tile_copy(k).start()
+    gather.relay(0)
+    for k in range(1, 8):
+        tile_copy(k).wait_recv()
+    total = part[f]
+    for k in range(1, 8):
+        total = total + got[k]
+    mixed[...] = total
+    zs = []
+    for k in range(1, 4):
+        copy = push(mixed, rows_out.at[d], zssem.at[k], zrsem.at[k], at(lax.rem(d + k, 4), s, c))
+        copy.start()
+        zs.append(copy)
+    own_rows = pltpu.make_async_copy(mixed, rows_out.at[d], lsem.at[2])
+    own_rows.start()
+    gather.corner(0)
+    for k in range(1, 4):
+        gather.spread_z(k)
+    for k in range(1, 4):
+        gather.relay(k)
+    for k in range(1, 4):
+        gather.corner(k)
+    gather.finish()
+    own_router.wait()
+    own_rows.wait()
+    for k in range(1, 4):
+        push(
+            mixed, rows_out.at[lax.rem(d + 4 - k, 4)], zssem.at[k], zrsem.at[k],
+            at(lax.rem(d + k, 4), s, c),
+        ).wait_recv()
+    for copy in zs:
+        copy.wait_send()
+    for k in range(1, 8):
+        tile_copy(k).wait_send()
+
+    def drain(k, carry):
+        act_copy(k, me).wait_send()
+        copy = router_copy(k, lax.rem(me + 32 - k, 32))
+        copy.wait_recv()
+        copy.wait_send()
+        return carry
+
+    lax.fori_loop(1, 32, drain, 0)
+
+
+DMA = pltpu.SemaphoreType.DMA
+ANYWHERE = pl.BlockSpec(memory_space=pl.ANY)
+ONCHIP = pl.BlockSpec(memory_space=pltpu.VMEM)
+
+
+def opening(shard, router, act, ada):
+    return pl.pallas_call(
+        open_kernel,
+        out_shape=(
+            jax.ShapeDtypeStruct((768, 3072), jnp.bfloat16),
+            jax.ShapeDtypeStruct((32, 16, 128), jnp.bfloat16),
+            jax.ShapeDtypeStruct((72, 128), jnp.float32),
+            jax.ShapeDtypeStruct((4, 8, 1152), jnp.float32),
+        ),
+        in_specs=[ONCHIP] * 4,
+        out_specs=(ANYWHERE, ANYWHERE, ONCHIP, ANYWHERE),
+        scratch_shapes=[
+            pltpu.VMEM((32, 8, 128), jnp.float32),
+            pltpu.VMEM((8, 8, 1152), jnp.float32),
+            pltpu.VMEM((8, 8, 1152), jnp.float32),
+            pltpu.VMEM((8, 1152), jnp.float32),
+            DMA((GATHER_SEMS,)), DMA((GATHER_SEMS,)), DMA((3,)),
+            DMA((32,)), DMA((32,)), DMA((32,)), DMA((32,)),
+            DMA((8,)), DMA((8,)), DMA((4,)), DMA((4,)),
+        ],
+        compiler_params=pltpu.CompilerParams(collective_id=0, has_side_effects=True),
+        name="opening",
+    )(shard, router, act, ada)
+
+
+def group_of(d, s, c):
+    return [(j, at(lax.rem(d + j // 2, 4), s, lax.rem(c + j, 2))) for j in range(1, 8)]
+
+
+class Swap:
+    def __init__(self, blocks, out, ssem, rsem, lsem):
+        self.blocks, self.out, self.ssem, self.rsem, self.lsem = blocks, out, ssem, rsem, lsem
+        self.d, self.s, self.c = place()
+        self.me = 2 * self.d + self.c
+
+    def copy(self, j, landing):
+        target_d = lax.rem(self.d + j // 2, 4)
+        target_c = lax.rem(self.c + j, 2)
+        return push(
+            self.blocks.at[2 * target_d + target_c],
+            self.out.at[landing],
+            self.ssem.at[j],
+            self.rsem.at[j],
+            at(target_d, self.s, target_c),
+        )
+
+    def start(self):
+        for j in (4, 5, 2, 3, 6, 7, 1):
+            self.copy(j, self.me).start()
+        self.own = pltpu.make_async_copy(
+            self.blocks.at[self.me], self.out.at[self.me], self.lsem
+        )
+        self.own.start()
+
+    def finish(self):
+        self.own.wait()
+        for j in range(1, 8):
+            source_d = lax.rem(self.d + 4 - j // 2, 4)
+            source_c = lax.rem(self.c + j, 2)
+            copy = self.copy(j, 2 * source_d + source_c)
+            copy.wait_recv()
+            copy.wait_send()
+
+
+def out_kernel(
+    rows, grads, up_shard, down_shard, rows_in, grads_in, up_full, down_full,
+    s1, r1, s2, r2, ssem, rsem, ssem2, rsem2, lsem,
+):
+    d, s, c = place()
+    greet([device for _, device in group_of(d, s, c)] + [at(d, flip(s, 1), c), at(d, flip(s, 2), c)])
+    first = Gather("cols", up_shard, up_full, ssem, rsem, lsem.at[0])
+    second = Gather("rows", down_shard, down_full, ssem2, rsem2, lsem.at[1])
+    swap_a = Swap(rows, rows_in, s1, r1, lsem.at[2])
+    swap_b = Swap(grads, grads_in, s2, r2, lsem.at[3])
+    both = (first, second)
+    for g in both:
+        g.start()
+    swap_a.start()
+    swap_b.start()
+    for g in both:
+        g.relay(0)
+    for k in range(1, 4):
+        for g in both:
+            g.spread_z(k)
+    for g in both:
+        g.corner(0)
+    for k in range(1, 4):
+        for g in both:
+            g.relay(k)
+    for k in range(1, 4):
+        for g in both:
+            g.corner(k)
+    for g in both:
+        g.finish()
+    swap_a.finish()
+    swap_b.finish()
+
+
+def outbound(rows, grads, up_shard, down_shard):
+    return pl.pallas_call(
+        out_kernel,
+        out_shape=(
+            jax.ShapeDtypeStruct((8, 144, 768), jnp.bfloat16),
+            jax.ShapeDtypeStruct((8, 144, 768), jnp.bfloat16),
+            jax.ShapeDtypeStruct((768, 3072), jnp.bfloat16),
+            jax.ShapeDtypeStruct((768, 3072), jnp.bfloat16),
+        ),
+        in_specs=[ONCHIP] * 4,
+        out_specs=(ANYWHERE,) * 4,
+        scratch_shapes=[DMA((8,))] * 4 + [DMA((GATHER_SEMS,))] * 4 + [DMA((4,))],
+        compiler_params=pltpu.CompilerParams(collective_id=1, has_side_effects=True),
+        name="outbound",
+    )(rows, grads, up_shard, down_shard)
+
+
+def widened(ref):
+    return ref[...].astype(jnp.float32)
+
+
+class ExpertSum:
+    def __init__(self, grad, out, own, near, far, last, outgoing, ssem, rsem, lsem):
+        self.grad, self.out, self.own, self.near = grad, out, own, near
+        self.far, self.last, self.outgoing = far, last, outgoing
+        self.ssem, self.rsem, self.lsem = ssem, rsem, lsem
+        self.d, self.s, self.c = place()
+        self.sx, self.sy = flip(self.s, 1), flip(self.s, 2)
+        self.sd = flip(self.sx, 2)
+        self.rows = grad.shape[0] // 8
+
+    def part(self, position, h):
+        return self.grad.at[pl.ds(pl.multiple_of((2 * position + h) * self.rows, 32), self.rows)]
+
+    def start(self):
+        d, c = self.d, self.c
+        self.one = [
+            push(self.part(self.sd, 0), self.near.at[0], self.ssem.at[0], self.rsem.at[0], at(d, self.sx, c)),
+            push(self.part(self.sd, 1), self.near.at[1], self.ssem.at[1], self.rsem.at[1], at(d, self.sy, c)),
+        ]
+        self.two = [
+            push(self.part(self.sx, 0), self.far.at[0], self.ssem.at[2], self.rsem.at[2], at(d, self.sx, c)),
+            push(self.part(self.sy, 1), self.far.at[1], self.ssem.at[3], self.rsem.at[3], at(d, self.sy, c)),
+        ]
+        for copy in self.one + self.two:
+            copy.start()
+        self.local = [
+            pltpu.make_async_copy(self.part(self.sy, 0), self.own.at[0], self.lsem.at[0]),
+            pltpu.make_async_copy(self.part(self.sx, 1), self.own.at[1], self.lsem.at[1]),
+            pltpu.make_async_copy(self.part(self.s, 0), self.own.at[2], self.lsem.at[2]),
+            pltpu.make_async_copy(self.part(self.s, 1), self.own.at[3], self.lsem.at[3]),
+        ]
+        for copy in self.local:
+            copy.start()
+
+    def join(self):
+        d, c = self.d, self.c
+        for copy in self.local:
+            copy.wait()
+        targets = (at(d, self.sy, c), at(d, self.sx, c))
+        self.three = []
+        for h in range(2):
+            self.one[h].wait_recv()
+            self.outgoing[h] = (widened(self.own.at[h]) + widened(self.near.at[h])).astype(jnp.bfloat16)
+            copy = push(
+                self.outgoing.at[h], self.far.at[2 + h], self.ssem.at[4 + h], self.rsem.at[4 + h], targets[h]
+            )
+            copy.start()
+            self.three.append(copy)
+
+    def close(self):
+        d, s, c = self.d, self.s, self.c
+        for copy in self.two + self.three:
+            copy.wait_recv()
+        low = (widened(self.own.at[2]) + widened(self.far.at[0])) + widened(self.far.at[2])
+        high = (widened(self.own.at[3]) + widened(self.far.at[1])) + widened(self.far.at[3])
+        self.outgoing[2] = jnp.where(c == 0, high, low).astype(jnp.bfloat16)
+        self.out[c] = jnp.where(c == 0, low, high)
+        self.four = push(
+            self.outgoing.at[2], self.last, self.ssem.at[6], self.rsem.at[6], at(d, s, 1 - c)
+        )
+        self.four.start()
+
+    def finish(self):
+        self.four.wait_recv()
+        self.out[1 - self.c] = widened(self.last)
+        for copy in self.one + self.two + self.three + [self.four]:
+            copy.wait_send()
+
+
+def back_kernel(
+    rows, grads, up_grad, down_grad, rows_in, grads_in, up_out, down_out,
+    uo, un, uf, ul, ug, do, dn, df, dl, dg, s1, r1, s2, r2, s3, r3, s4, r4, lsem, l3, l4,
+):
+    d, s, c = place()
+    greet([device for _, device in group_of(d, s, c)] + [at(d, flip(s, 1), c), at(d, flip(s, 2), c)])
+    swap_a = Swap(rows, rows_in, s1, r1, lsem.at[0])
+    swap_b = Swap(grads, grads_in, s2, r2, lsem.at[1])
+    sums = (
+        ExpertSum(up_grad, up_out, uo, un, uf, ul, ug, s3, r3, l3),
+        ExpertSum(down_grad, down_out, do, dn, df, dl, dg, s4, r4, l4),
+    )
+    for each in sums:
+        each.start()
+    swap_a.start()
+    swap_b.start()
+    for each in sums:
+        each.join()
+    for each in sums:
+        each.close()
+    for each in sums:
+        each.finish()
+    swap_a.finish()
+    swap_b.finish()
+
+
+def inbound(rows, grads, up_grad, down_grad):
+    bf, f32 = jnp.bfloat16, jnp.float32
+
+    def rooms(r, n):
+        return [
+            pltpu.VMEM((4, r, n), bf),
+            pltpu.VMEM((2, r, n), bf),
+            pltpu.VMEM((4, r, n), bf),
+            pltpu.VMEM((r, n), bf),
+            pltpu.VMEM((3, r, n), bf),
+        ]
+
+    return pl.pallas_call(
+        back_kernel,
+        out_shape=(
+            jax.ShapeDtypeStruct((8, 144, 768), bf),
+            jax.ShapeDtypeStruct((8, 144, 768), bf),
+            jax.ShapeDtypeStruct((2, 96, 3072), f32),
+            jax.ShapeDtypeStruct((2, 384, 768), f32),
+        ),
+        in_specs=[ONCHIP, ONCHIP, ANYWHERE, ANYWHERE],
+        out_specs=(ANYWHERE, ANYWHERE, ONCHIP, ONCHIP),
+        scratch_shapes=rooms(96, 3072)
+        + rooms(384, 768)
+        + [DMA((8,))] * 8
+        + [DMA((2,)), DMA((4,)), DMA((4,))],
+        compiler_params=pltpu.CompilerParams(collective_id=2, has_side_effects=True),
+        name="inbound",
+    )(rows, grads, up_grad, down_grad)
+
+
+class DenseSum:
+    def __init__(self, kind, grad, out, own, mate, near, far, line, ssem, rsem, lsem):
+        self.kind, self.grad, self.out = kind, grad, out
+        self.own, self.mate, self.near, self.far, self.line = own, mate, near, far, line
+        self.ssem, self.rsem, self.lsem = ssem, rsem, lsem
+        self.d, self.s, self.c = place()
+        self.order = (
+            flip(flip(self.s, 1), 2),
+            flip(self.s, 1),
+            flip(self.s, 2),
+            self.s,
+        )
+
+    def piece(self, f):
+        if self.kind == "cols":
+            return self.grad.at[pl.ds(pl.multiple_of(96 * f, 96), 96)]
+        return self.grad.at[:, pl.ds(pl.multiple_of(384 * f, 384), 384)]
+
+    def half(self, ref, h):
+        if self.kind == "cols":
+            return ref.at[:, pl.ds(1536 * h, 1536)]
+        return ref.at[pl.ds(384 * h, 384)]
+
+    def quarter(self, ref, q):
+        if self.kind == "cols":
+            return ref.at[:, pl.ds(pl.multiple_of(768 * q, 768), 768)]
+        return ref.at[pl.ds(pl.multiple_of(192 * q, 192), 192)]
+
+    def start(self):
+        d, s, c = self.d, self.s, self.c
+        self.zero, self.local = [], []
+        for j, position in enumerate(self.order):
+            copy = push(
+                self.piece(2 * position + 1 - c), self.mate.at[j], self.ssem.at[j], self.rsem.at[j], at(d, s, 1 - c)
+            )
+            copy.start()
+            self.zero.append(copy)
+            copy = pltpu.make_async_copy(self.piece(2 * position + c), self.own.at[j], self.lsem.at[j])
+            copy.start()
+            self.local.append(copy)
+
+    def merge(self):
+        d, s, c = self.d, self.s, self.c
+        sx, sy = flip(s, 1), flip(s, 2)
+        self.one = []
+        for j in range(4):
+            self.zero[j].wait_recv()
+            self.local[j].wait()
+            self.own[j] = (widened(self.own.at[j]) + widened(self.mate.at[j])).astype(jnp.bfloat16)
+            if j == 0:
+                for h, target in enumerate((sx, sy)):
+                    copy = push(
+                        self.half(self.own.at[0], h), self.near.at[h], self.ssem.at[4 + h], self.rsem.at[4 + h],
+                        at(d, target, c),
+                    )
+                    copy.start()
+                    self.one.append(copy)
+
+    def join(self):
+        d, s, c = self.d, self.s, self.c
+        sx, sy = flip(s, 1), flip(s, 2)
+        for h, j in ((0, 2), (1, 1)):
+            self.one[h].wait_recv()
+            where = self.half(self.own.at[j], h)
+            where[...] = (widened(where) + widened(self.near.at[h])).astype(jnp.bfloat16)
+        self.two = []
+        for h, target in enumerate((sx, sy)):
+            copy = push(
+                self.own.at[1 + h], self.far.at[h], self.ssem.at[6 + h], self.rsem.at[6 + h], at(d, target, c)
+            )
+            copy.start()
+            self.two.append(copy)
+
+    def along(self):
+        d, s, c = self.d, self.s, self.c
+        for copy in self.two:
+            copy.wait_recv()
+        self.own[3] = (
+            widened(self.own.at[3]) + widened(self.far.at[0]) + widened(self.far.at[1])
+        ).astype(jnp.bfloat16)
+        self.three = []
+        for k in range(1, 4):
+            target = lax.rem(d + k, 4)
+            copy = push(
+                self.quarter(self.own.at[3], target), self.line.at[k - 1], self.ssem.at[7 + k], self.rsem.at[7 + k],
+                at(target, s, c),
+            )
+            copy.start()
+            self.three.append(copy)
+
+    def finish(self):
+        total = widened(self.quarter(self.own.at[3], self.d))
+        for k in range(1, 4):
+            self.three[k - 1].wait_recv()
+            total = total + widened(self.line.at[k - 1])
+        self.out[...] = total
+        for copy in self.zero + self.one + self.two + self.three:
+            copy.wait_send()
+
+
+def dense_kernel(kinds, *refs):
+    n = len(kinds)
+    grads, outs, rest = refs[:n], refs[n : 2 * n], refs[2 * n :]
+    d, s, c = place()
+    greet(
+        [at(lax.rem(d + k, 4), s, c) for k in range(1, 4)]
+        + [at(d, s, 1 - c), at(d, flip(s, 1), c), at(d, flip(s, 2), c)]
+    )
+    sums = [
+        DenseSum(kinds[i], grads[i], outs[i], *rest[8 * i : 8 * i + 8]) for i in range(n)
+    ]
+    for each in sums:
+        each.start()
+    for each in sums:
+        each.merge()
+    for each in sums:
+        each.join()
+    for each in sums:
+        each.along()
+    for each in sums:
+        each.finish()
+
+
+def dense_sums(kinds, grads, collective_id):
+    bf = jnp.bfloat16
+    outs, scratch = [], []
+    for kind in kinds:
+        if kind == "cols":
+            piece, half, quarter = (96, 3072), (96, 1536), (96, 768)
+        else:
+            piece, half, quarter = (768, 384), (384, 384), (192, 384)
+        outs.append(jax.ShapeDtypeStruct(quarter, jnp.float32))
+        scratch += [
+            pltpu.VMEM((4,) + piece, bf),
+            pltpu.VMEM((4,) + piece, bf),
+            pltpu.VMEM((2,) + half, bf),
+            pltpu.VMEM((2,) + piece, bf),
+            pltpu.VMEM((3,) + quarter, bf),
+            DMA((11,)),
+            DMA((11,)),
+            DMA((4,)),
+        ]
+    return pl.pallas_call(
+        functools.partial(dense_kernel, kinds),
+        out_shape=tuple(outs),
+        in_specs=[ANYWHERE] * len(kinds),
+        out_specs=(ONCHIP,) * len(kinds),
+        scratch_shapes=scratch,
+        compiler_params=pltpu.CompilerParams(collective_id=collective_id, has_side_effects=True),
+        name="dense_sums",
+    )(*grads)
+
+
+def nt(left, right):
+    return lax.dot_general(left, right, (((1,), (1,)), ((), ())), preferred_element_type=jnp.float32)
+
+
+def tn(left, right):
+    return lax.dot_general(left, right, (((0,), (0,)), ((), ())), preferred_element_type=jnp.float32)
+
+
+def nn(left, right):
+    return jnp.dot(left, right, preferred_element_type=jnp.float32)
+
+
+def fitted_shards(
+    tokens,
+    condition,
+    ada_weight,
+    qkv_weight,
+    out_weight,
+    shared_up,
+    shared_down,
+    router_weight,
+    expert_up,
+    expert_down,
+    routes,
+    image_sizes,
+    cotangent,
+):
+    bf = jnp.bfloat16
+    d_index, f_index = lax.axis_index("dp"), lax.axis_index("fsdp")
+    core = lax.rem(f_index, 2)
+    model_width = tokens.shape[1]
+    head_size = model_width // HEADS
+    inside, segment = owners(image_sizes)
+    up_all, down_all = gather_experts(expert_up, expert_down)
+    up_mine = lax.dynamic_index_in_dim(up_all, core, 0, keepdims=False)
+    down_mine = lax.dynamic_index_in_dim(down_all, core, 0, keepdims=False)
+    ids = jnp.arange(EXPERTS, dtype=jnp.int32)
+    hot = routes[:, :, None] == ids[None, None, :]
+    hot_any = jnp.any(hot, axis=1).astype(bf)
+    order = jnp.arange(LONG, dtype=jnp.int32)
+    earlier = (order[:, None] > order[None, :]).astype(bf)
+    before = nn(earlier, hot_any)
+    position = jnp.sum(jnp.where(hot, before[:, None, :], 0.0), axis=-1).astype(jnp.int32)
+    target = routes * CAP + position
+    places = jnp.arange(EXPERTS * CAP, dtype=jnp.int32)
+    send_0 = (places[:, None] == target[None, :, 0]).astype(bf)
+    send_1 = (places[:, None] == target[None, :, 1]).astype(bf)
+    live = (segment < IMG_DEV).astype(jnp.float32)
+    counts = jnp.sum(live[:, None] * hot_any.astype(jnp.float32), axis=0)
+    cond_float = condition.astype(jnp.float32)
+    activated = jax.nn.silu(cond_float).astype(bf)
+    act_slices = activated.astype(jnp.float32).reshape(IMG_DEV, 8, 96).transpose(1, 0, 2)
+    act_slices = jnp.pad(act_slices, ((0, 0), (0, 6), (0, 32)))
+    act_slices = act_slices.at[:, 2, :EXPERTS].set(counts)
+    ada_pad = jnp.pad(ada_weight, ((0, 32), (0, 0)))
+    router_pack = jnp.pad(router_weight.reshape(192), (0, 2048 - 192)).reshape(16, 128)
+    qkvo_shard = jnp.concatenate([qkv_weight, out_weight], axis=1)
+    qkvo, routers, seen, mod_rows = opening(qkvo_shard, router_pack, act_slices, ada_pad)
+    activated_all = seen[:64, :96].astype(bf)
+    expert_counts = seen[66, :EXPERTS].astype(jnp.int32)
+    modulation = lax.dynamic_slice(mod_rows, (0, 2 * d_index, 0), (4, 2, 1152))
+    modulation = modulation.transpose(1, 0, 2).reshape(2, 4608)
+    router_full = (
+        routers.reshape(32, 2048)[:, :192]
+        .reshape(4, 8, 96, 2)
+        .transpose(1, 2, 0, 3)
+        .reshape(model_width, EXPERTS)
+    )
+    qkvo = qkvo.reshape(model_width, 4, 768)
+    qkv_full = qkvo[:, :, :576].reshape(model_width, 2304)
+    out_full = qkvo[:, :, 576:].reshape(model_width, 768)
+    per_row = inside[:, 0:1] * modulation[0:1] + inside[:, 1:2] * modulation[1:2]
+    shift_one, scale_one, gate_one, shift_two, scale_two, gate_two = jnp.split(per_row, 6, axis=1)
+    token_float = tokens.astype(jnp.float32)
+    normed_one, inv_one = layer_norm(token_float)
+    first_input = (normed_one * (1.0 + scale_one) + shift_one).astype(bf)
+    qkv_rows = nn(first_input, qkv_full).astype(bf)
+    queries, keys, values = (
+        qkv_rows[:, i * model_width : (i + 1) * model_width]
+        .reshape(LONG, HEADS, head_size)
+        .transpose(1, 0, 2)
+        for i in range(3)
+    )
+    scale = head_size**-0.5
+    allowed = (segment[:, None] == segment[None, :])[None]
+    scores = jnp.einsum("hqd,hkd->hqk", queries, keys, preferred_element_type=jnp.float32) * scale
+    scores = jnp.where(allowed, scores, -1e30)
+    row_max = jnp.max(scores, axis=-1, keepdims=True)
+    weight = jnp.exp(scores - row_max)
+    running = jnp.sum(weight, axis=-1, keepdims=True)
+    probability = weight / running
+    prob_low = probability.astype(bf)
+    attended = jnp.einsum("hqk,hkd->hqd", prob_low, values, preferred_element_type=jnp.float32)
+    attended = attended.astype(bf).transpose(1, 0, 2).reshape(LONG, model_width)
+    projected = nn(attended, out_full)
+    residual_one = token_float + gate_one * projected
+    normed_two, inv_two = layer_norm(residual_one)
+    second_input = (normed_two * (1.0 + scale_two) + shift_two).astype(bf)
+    logits = nn(second_input, router_full)
+    route_hot = hot.astype(jnp.float32)
+    chosen = jnp.sum(logits[:, None, :] * route_hot, axis=-1)
+    gate_share = jax.nn.softmax(chosen, axis=-1)
+    upstream = cotangent.astype(jnp.float32)
+    d_mixed = gate_two * upstream
+    rows = nn(send_0 + send_1, second_input).astype(bf).reshape(EXPERTS, CAP, model_width)
+    weighted = jnp.concatenate(
+        [(gate_share[:, k : k + 1] * d_mixed).astype(bf) for k in range(2)], axis=0
+    )
+    grads = (
+        nn(jnp.concatenate([send_0, send_1], axis=1), weighted)
+        .astype(bf)
+        .reshape(EXPERTS, CAP, model_width)
+    )
+    rows_in, grads_in, shared_first, shared_second = outbound(rows, grads, shared_up, shared_down.T)
+    rows_in = rows_in.reshape(EXPERTS * CAP, model_width)
+    grads_in = grads_in.reshape(EXPERTS * CAP, model_width)
+    expert_pre = nn(rows_in, up_mine)
+    expert_act = gelu_tanh(expert_pre).astype(bf)
+    expert_out = nn(expert_act, down_mine).astype(bf)
+    d_act = nt(grads_in, down_mine)
+    d_pre = gelu_back(expert_pre, d_act).astype(bf)
+    d_rows = nt(d_pre, up_mine).astype(bf)
+    down_grad = tn(expert_act, grads_in).astype(bf)
+    up_grad = tn(rows_in, d_pre).astype(bf)
+    returned, d_returned, expert_up_grad, expert_down_grad = inbound(
+        expert_out.reshape(EXPERTS, CAP, model_width),
+        d_rows.reshape(EXPERTS, CAP, model_width),
+        up_grad,
+        down_grad,
+    )
+    returned = returned.reshape(EXPERTS * CAP, model_width)
+    d_returned = d_returned.reshape(EXPERTS * CAP, model_width)
+    shared_pre = nn(second_input, shared_first)
+    shared_act = gelu_tanh(shared_pre).astype(bf)
+    shared_out = nt(shared_act, shared_second)
+    d_shared = d_mixed.astype(bf)
+    shared_second_grad = tn(d_shared, shared_act).astype(bf)
+    d_shared_act = nn(d_shared, shared_second)
+    d_shared_pre = gelu_back(shared_pre, d_shared_act).astype(bf)
+    shared_first_grad = tn(second_input, d_shared_pre).astype(bf)
+    d_second = nt(d_shared_pre, shared_first)
+    picked_0 = tn(send_0, returned)
+    picked_1 = tn(send_1, returned)
+    mixed = shared_out + (gate_share[:, 0:1] * picked_0 + gate_share[:, 1:2] * picked_1)
+    output = (residual_one + gate_two * mixed).astype(bf)
+    d_gate_two = upstream * mixed
+    d_gate_share = jnp.stack(
+        [jnp.sum(d_mixed * picked_0, axis=-1), jnp.sum(d_mixed * picked_1, axis=-1)], axis=1
+    )
+    d_chosen = gate_share * (
+        d_gate_share - jnp.sum(gate_share * d_gate_share, axis=-1, keepdims=True)
+    )
+    d_logits = jnp.sum(d_chosen[:, :, None] * route_hot, axis=1).astype(bf)
+    router_grad = tn(d_logits, second_input)
+    d_second = d_second + nt(d_logits, router_full) + tn(send_0 + send_1, d_returned)
+    d_scale_two = d_second * normed_two
+    d_residual = upstream + norm_back(d_second * (1.0 + scale_two), normed_two, inv_two)
+    d_projected = (gate_one * d_residual).astype(bf)
+    d_gate_one = d_residual * projected
+    out_grad = tn(attended, d_projected)
+    d_attended = nt(d_projected, out_full).astype(bf)
+    d_attended = d_attended.reshape(LONG, HEADS, head_size).transpose(1, 0, 2)
+    d_prob = jnp.einsum("hqd,hkd->hqk", d_attended, values, preferred_element_type=jnp.float32)
+    d_scores = (
+        probability * (d_prob - jnp.sum(probability * d_prob, axis=-1, keepdims=True))
+    ).astype(bf)
+    d_queries = jnp.einsum("hqk,hkd->hqd", d_scores, keys, preferred_element_type=jnp.float32) * scale
+    d_keys = jnp.einsum("hqk,hqd->hkd", d_scores, queries, preferred_element_type=jnp.float32) * scale
+    d_values = jnp.einsum("hqk,hqd->hkd", prob_low, d_attended, preferred_element_type=jnp.float32)
+    d_qkv = jnp.concatenate(
+        [
+            piece.astype(bf).transpose(1, 0, 2).reshape(LONG, model_width)
+            for piece in (d_queries, d_keys, d_values)
+        ],
+        axis=1,
+    )
+    qkv_grad = tn(first_input, d_qkv)
+    d_first = nt(d_qkv, qkv_full)
+    d_scale_one = d_first * normed_one
+    tokens_grad = d_residual + norm_back(d_first * (1.0 + scale_one), normed_one, inv_one)
+    qkvo_grad = (
+        jnp.concatenate(
+            [qkv_grad.reshape(model_width, 4, 576), out_grad.reshape(model_width, 4, 192)], axis=2
+        )
+        .astype(bf)
+        .reshape(model_width, 3072)
+    )
+    d_modulation = jnp.concatenate(
+        [
+            jnp.stack([jnp.sum(inside[:, j : j + 1] * piece, axis=0) for j in range(IMG_DEV)])
+            for piece in (d_first, d_scale_one, d_gate_one, d_second, d_scale_two, d_gate_two)
+        ],
+        axis=1,
+    ).astype(bf)
+    shared_first_sum, shared_second_sum, qkvo_sum = dense_sums(
+        ("cols", "rows", "cols"), (shared_first_grad, shared_second_grad, qkvo_grad), 3
+    )
+    d_mod_all = lax.all_gather(d_modulation, ("dp", "fsdp"), axis=0)
+    d_mod_all = lax.dynamic_slice(d_mod_all, (0, 0, 1152 * d_index), (32, 2, 1152))
+    d_mod_all = d_mod_all.reshape(4, 8, 2, 1152).transpose(1, 0, 2, 3).reshape(64, 1152)
+    ada_grad = tn(activated_all, d_mod_all)
+    partial = nt(d_mod_all, ada_weight).reshape(8, 4, 2, 96)
+    partial_all = lax.all_gather(partial, ("dp", "fsdp"), axis=0)
+    partial_mine = lax.dynamic_slice(
+        partial_all, (0, f_index, d_index, 0, 0), (32, 1, 1, 2, 96)
+    ).reshape(4, 8, 2, 96)
+    d_activated = jnp.sum(partial_mine, axis=0).transpose(1, 0, 2).reshape(2, 768)
+    condition_grad = jax.vjp(jax.nn.silu, cond_float)[1](d_activated)[0]
+    router_sum = lax.psum(router_grad, ("dp", "fsdp"))
+    router_out = lax.dynamic_slice(router_sum, (2 * d_index, 96 * f_index), (2, 96)).T
+    return (
+        output,
+        tokens_grad,
+        condition_grad,
+        ada_grad,
+        qkvo_sum[:, :576],
+        qkvo_sum[:, 576:],
+        shared_first_sum,
+        shared_second_sum.T,
+        router_out,
+        expert_up_grad,
+        expert_down_grad,
+        expert_counts,
+    )
+
+
 def solution(mesh):
     placed = (
         P(("dp", "fsdp"), None),
@@ -398,8 +1285,9 @@
         P(("dp", "fsdp")),
         P(("dp", "fsdp"), None),
     )
+    fitted = mesh.shape["dp"] == 4 and mesh.shape["fsdp"] == 8
     return jax.shard_map(
-        shards,
+        fitted_shards if fitted else shards,
         mesh=mesh,
         in_specs=placed,
         out_specs=(

time: 1430 us -> 739 us (0.52)
  waiting for transfers between devices: 778 us -> 1.38 us
  Pallas kernels: 0 us -> 330 us
  blocking collectives: 240 us -> 120 us
  local copies, waits for them, and re-layouts: 95.5 us -> 55.5 us
  matrix products: 215 us -> 179 us
  other arithmetic: 60.1 us -> 30.7 us
  starting transfers between devices: 15.2 us -> 0.08 us
    reduce_scatter x9 -> x0, waiting for transfers between devices: 618 us -> none  [the longest x2 180 us: spread(): lax.psum_scatter(first, 'fsdp', scatter_dimension=0, tiled=True)]
    pallas_call x0 -> x4, Pallas kernels: none -> 330 us  [the longest x1 99.5 us: outbound(): pl.pallas_call(out_kernel, out_shape=(jax.ShapeDtypeStruct((8, 144, 768),...]
    all_gather x7 -> x2, blocking collectives: 143 us -> 82.9 us  [the longest x1 43.4 us: fitted_shards(): d_mod_all = lax.all_gather(d_modulation, ('dp', 'fsdp'), axis=0)]
    all_to_all x3 -> x0, waiting for transfers between devices: 59.5 us -> none  [the longest x1 35.2 us: shards(): lax.all_to_all(d_buffer.reshape(groups, EXPERTS // groups, CAP, model_wid...]
    all_gather x1, waiting for transfers between devices: 47.7 us -> 0.01 us  [gather_experts(): lax.all_gather(down_shard, 'fsdp', axis=1, tiled=True)]
    all_to_all x1 -> x0, blocking collectives: 46.1 us -> none  [shards(): lax.all_to_all(buffer_rows.reshape(groups, EXPERTS // groups, CAP, model_...]
    dot_general x31 -> x34, matrix products: 214 us -> 168 us  [the longest x8 50.3 us: nt(): lax.dot_general(left, right, (((1,), (1,)), ((), ())), preferred_element_...]
    unnamed x24 -> x2, waiting for transfers between devices: 32.1 us -> 1.38 us
  transfers between devices with their start and end apart: 23 -> 2, of which waited for: 15 -> 0; matrix products, arithmetic and copies ran while one was open for 20% -> 15% of each run, Pallas kernels for 0% -> 22%
where the time goes in v1:
time: 739 us; the launch traced here: 733 us
  Pallas kernels  330 us (45%)
  matrix products  179 us (24%)
  blocking collectives  120 us (16%)
  local copies, waits for them, and re-layouts  55.5 us (8%)
  other arithmetic  30.7 us (4%)
  between operations  15.7 us (2%)
    pallas_call x1, Pallas kernels, outbound(): pl.pallas_call(out_kernel, out_shape=(jax.ShapeDtypeStruct((8, 144, 768),...  99.5 us
    pallas_call x1, Pallas kernels, inbound(): pl.pallas_call(back_kernel, out_shape=(jax.ShapeDtypeStruct((8, 144, 768)...  95.7 us
    pallas_call x1, Pallas kernels, dense_sums(): pl.pallas_call(functools.partial(dense_kernel, kinds), out_shape=tuple(ou...  76.5 us
    pallas_call x1, Pallas kernels, opening(): pl.pallas_call(open_kernel, out_shape=(jax.ShapeDtypeStruct((768, 3072),...  58.7 us
    dot_general x8, matrix products, nt(): lax.dot_general(left, right, (((1,), (1,)), ((), ())), preferred_element_...  50.3 us
    dot_general x10, matrix products, nn(): return jnp.dot(left, right, preferred_element_type=jnp.float32)  46.3 us
    dot_general x11, matrix products, tn(): lax.dot_general(left, right, (((0,), (0,)), ((), ())), preferred_element_...  44.2 us
    all_gather x1, blocking collectives, fitted_shards(): d_mod_all = lax.all_gather(d_modulation, ('dp', 'fsdp'), axis=0)  43.4 us
  transfers between devices with their start and end apart: 2, of which 0 were waited for; matrix products, arithmetic and copies ran while one was open for 15% of the time, Pallas kernels for 22%

profile of v1, /device:TPU:0, one launch (start us, length us, event | category | flops | bytes accessed | tf_op | source)
XLA Modules:
  0.0 733.0 jit_solution(8278421115788220642)
XLA Ops:
  17.2 58.7 %opening.1 = (bf16[768,3072]{1,0:T(8,128)(2,1)}, bf16[32,16,128]{2,1,0:T(8,128)(2,1)}, f32[72,128]{1,0:T(8,128)}, f32[4,8,1152]{2,1,0:T(8,128)}) custom-call(bf16[96,768]{1,0:T(8,128)(2,1)} %pad_maximum_fusion.4.shard, bf16[16,128]{1,0:T(8,128)(2,1)} %pad_bitcast_fusion.router, f32[8,8,128]{2,1,0:T(8,128)} %copy-done.30, bf16[128,1152]{1,0:T(8,128)(2,1)} %pad.22.ada_ref), custom_call_target="tpu_custom_call" | custom-call | tf_op jit(solution)/shard_map/opening/pallas_call | solution.py:649
  83.1 7.4 %copy.144 = bf16[768,3072]{0,1:T(8,128)(2,1)} copy(bf16[768,3072]{1,0:T(8,128)(2,1)} %get-tuple-element.40) | data formatting | bytes 9437184 | tf_op jit(solution)/shard_map/reshape | solution.py:1114
  108.2 11.0 %fusion.125 = (f32[12,512]{1,0:T(8,128)}, f32[12,512,512]{1,2,0:T(8,128)}) fusion(pred[512,512]{0,1:T(8,128)(4,1)} %broadcast_compare_fusion, bf16[12,512,64]{1,2,0:T(8,128)(2,1)} %bitcast.204, bf16[12,512,64]{1,2,0:T(8,128)(2,1)S(1)} %bitcast.184), kind=kOutput, calls=%fused_computation.225 | convolution fusion | flops 415236608 | bytes 14442496 | tf_op jit(solution)/shard_map/sub | solution.py:1134
  119.3 7.3 %fusion.64 = bf16[12,512,64]{1,2,0:T(8,128)(2,1)S(1)} fusion(bf16[12,512,64]{1,2,0:T(8,128)(2,1)S(1)} %bitcast.206, f32[12,512,512]{1,2,0:T(8,128)} %get-tuple-element.103, f32[12,512]{1,0:T(8,128)} %get-tuple-element.102), kind=kOutput, calls=%fused_computation.120 | convolution fusion | flops 409337856 | bytes 14180352 | tf_op jit(solution)/shard_map/hqk,hkd->hqd/dot_general | solution.py:1138
  143.3 99.5 %outbound.1 = (bf16[8,144,768]{2,1,0:T(8,128)(2,1)}, bf16[8,144,768]{2,1,0:T(8,128)(2,1)}, bf16[768,3072]{1,0:T(8,128)(2,1)}, bf16[768,3072]{1,0:T(8,128)(2,1)}) custom-call(bf16[8,144,768]{2,1,0:T(8,128)(2,1)} %bitcast.197, bf16[8,144,768]{2,1,0:T(8,128)(2,1)} %bitcast.198, bf16[96,768]{1,0:T(8,128)(2,1)} %up_shard.1, bf16[192,384]{1,0:T(8,128)(2,1)} %bitcast.216), custom_call_target="tpu_custom_call" | custom-call | tf_op jit(solution)/shard_map/outbound/pallas_call | solution.py:747
  248.7 6.2 fusion.15
  266.7 8.4 %fusion.24 = f32[1152,3072]{1,0:T(8,128)S(1)} fusion(bf16[1152,768]{1,0:T(8,128)(2,1)} %bitcast.246, bf16[2,768,3072]{2,1,0:T(8,128)(2,1)} %all-gather.4.cloned.1.call-done, s32[]{:T(128)S(6)} %select_n.54), kind=kOutput, calls=%fused_computation.42 | convolution fusion | flops 5435817984 | bytes 20643844 | tf_op jit(solution)/shard_map/dot_general | solution.py:1055
  280.1 9.4 %convolution_convert_fusion.down_grad = bf16[3072,768]{1,0:T(8,128)(2,1)} fusion(bf16[1152,768]{1,0:T(8,128)(2,1)S(1)} %bitcast.250, f32[1152,3072]{1,0:T(8,128)S(1)} %fusion.24), kind=kOutput, calls=%fused_computation.31 | convolution fusion | flops 5470027776 | bytes 20643840 | tf_op jit(solution)/shard_map/dot_general | solution.py:1051
  289.5 19.1 %fusion.7 = bf16[1152,3072]{1,0:T(8,128)(2,1)} fusion(f32[1152,3072]{1,0:T(8,128)} %copy-done.68, bf16[1152,768]{1,0:T(8,128)(2,1)} %bitcast.249, bf16[2,3072,768]{2,1,0:T(8,128)(2,1)} %all-gather.6.cloned.1.call-done, s32[]{:T(128)S(6)} %select_n.54), kind=kOutput, calls=%fused_computation.9 | convolution fusion | flops 5506596864 | bytes 27721732 | tf_op jit(solution)/shard_map/dot_general | solution.py:1047
  308.6 11.5 %convolution_convert_fusion.1.up_grad = bf16[768,3072]{1,0:T(8,128)(2,1)} fusion(bf16[1152,768]{1,0:T(8,128)(2,1)S(1)} %bitcast.247, bf16[1152,3072]{1,0:T(8,128)(2,1)} %fusion.7), kind=kOutput, calls=%fused_computation.32 | convolution fusion | flops 5438177280 | bytes 13565952 | tf_op jit(solution)/shard_map/dot_general | solution.py:1051
  320.1 12.4 %fusion.33 = bf16[1152,768]{1,0:T(8,128)(2,1)} fusion(bf16[2,3072,768]{2,1,0:T(8,128)(2,1)S(1)} %copy-done.62, s32[]{:T(128)S(6)} %select_n.54, f32[1152,3072]{1,0:T(8,128)} %copy-done.68), kind=kOutput, calls=%fused_computation.50 | convolution fusion | flops 5468553216 | bytes 20643844 | tf_op jit(solution)/shard_map/dot_general | solution.py:1055
  332.6 9.0 %fusion.30 = bf16[1152,768]{1,0:T(8,128)(2,1)} fusion(bf16[1152,3072]{1,0:T(8,128)(2,1)} %fusion.7, bf16[2,768,3072]{2,1,0:T(8,128)(2,1)S(1)} %bitcast.245, s32[]{:T(128)S(6)} %select_n.54), kind=kOutput, calls=%fused_computation.49 | convolution fusion | flops 5436702720 | bytes 13565956 | tf_op jit(solution)/shard_map/dot_general | solution.py:1047
  341.6 95.7 %inbound.1 = (bf16[8,144,768]{2,1,0:T(8,128)(2,1)}, bf16[8,144,768]{2,1,0:T(8,128)(2,1)}, f32[2,96,3072]{2,1,0:T(8,128)}, f32[2,384,768]{2,1,0:T(8,128)}) custom-call(bf16[8,144,768]{2,1,0:T(8,128)(2,1)} %bitcast.195, bf16[8,144,768]{2,1,0:T(8,128)(2,1)} %bitcast.196, bf16[768,3072]{1,0:T(8,128)(2,1)} %convolution_convert_fusion.1.up_grad, ...), custom_call_target="tpu_custom_call" | custom-call | tf_op jit(solution)/shard_map/inbound/pallas_call | solution.py:874
  441.8 7.5 %add_add_fusion.1 = f32[512,768]{1,0:T(8,128)S(1)} fusion(f32[512,768]{1,0:T(8,128)S(1)} %fusion.43, f32[512,768]{1,0:T(8,128)S(1)} %get-tuple-element.105, bf16[768,3072]{1,0:T(8,128)(2,1)} %get-tuple-element.43, f32[512]{0:T(512)S(1)} %bitcast.241, f32[512]{0:T(512)S(1)} %bitcast.239, f32[512,3072]{1,0:T(8,128)} %copy-done.11), kind=kOutput, calls=%fused_computation.113 | convolution fusion | flops 2431647744 | bytes 15732736 | tf_op jit(solution)/shard_map/dot_general | solution.py:1047
  457.6 6.8 fusion.67
  464.4 9.2 %multiply_reduce_fusion = (f32[12,512]{1,0:T(8,128)S(1)}, f32[12,512,512]{1,2,0:T(8,128)}) fusion(f32[12,512,512]{1,2,0:T(8,128)} %get-tuple-element.103, f32[12,512]{1,0:T(8,128)S(1)} %copy-done.41, bf16[12,512,64]{1,2,0:T(8,128)(2,1)S(1)} %bitcast.210, bf16[12,512,64]{1,2,0:T(8,128)(2,1)S(1)} %bitcast.207), kind=kOutput, calls=%fused_computation.12 | convolution fusion | flops 412084224 | bytes 26787840 | tf_op jit(solution)/shard_map/hqd,hkd->hqk/dot_general | solution.py:1208
  473.7 6.8 multiply_convert_fusion.1
  485.8 5.1 convolution_convert_fusion.2
  500.1 6.8 copy.143.refs_2_
  507.0 76.5 %dense_sums.1 = (f32[96,768]{1,0:T(8,128)}, f32[192,384]{1,0:T(8,128)}, f32[96,768]{1,0:T(8,128)}) custom-call(bf16[768,3072]{1,0:T(8,128)(2,1)} %convolution_convert_fusion.4.refs_0_, bf16[768,3072]{1,0:T(8,128)(2,1)} %convolution_convert_fusion.3.refs_1_, bf16[768,3072]{1,0:T(8,128)(2,1)} %copy.143.refs_2_), custom_call_target="tpu_custom_call" | custom-call | tf_op jit(solution)/shard_map/dense_sums/pallas_call | solution.py:1035
  587.1 7.5 %fusion.119 = (f32[512]{0:T(512)S(1)}, f32[512]{0:T(512)S(1)}, bf16[768]{0:T(1024)(128)(2,1)S(1)}, bf16[768]{0:T(1024)(128)(2,1)S(1)}, bf16[768]{0:T(1024)(128)(...) fusion(f32[512,4608]{1,0:T(8,128)} %copy-done, ...), kind=kOutput, calls=%fused_computation.219 | convolution fusion | flops 1827662336 | bytes 12997632 | tf_op jit(solution)/shard_map/dot_general | solution.py:1047
  595.0 43.4 %all_gather.15 = bf16[32,2,4608]{2,1,0:T(2,128)(2,1)S(1)} all-gather(bf16[1,2,4608]{2,1,0:T(2,128)(2,1)S(1)} %constant_dynamic-update-slice_fusion), channel_id=1, replica_groups=mesh['dp'=4,'fsdp'=8] {'dp','fsdp'}, dimensions={0}, use_global_device_ids=true | all-gather | bytes 608256 | tf_op jit(solution)/shard_map/all_gather | solution.py:1243
  638.7 39.5 %all-gather = f32[256,4,2,96]{3,0,2,1:T(8,128)S(1)} all-gather(f32[8,4,2,96]{3,0,2,1:T(8,128)S(1)} %fusion.90), channel_id=2, replica_groups=mesh['dp'=4,'fsdp'=8] {'dp','fsdp'}, dimensions={0}, use_global_device_ids=true | all-gather | bytes 811008 | tf_op jit(solution)/shard_map/all_gather | solution.py:1248
  680.2 37.1 %psum.7 = f32[8,768]{1,0:T(8,128)S(1)} all-reduce(f32[8,768]{1,0:T(8,128)S(1)} %fusion.129), channel_id=1, replica_groups=mesh['dp'=4,'fsdp'=8] {'dp','fsdp'}, use_global_device_ids=true, to_apply=%region_37.38 | all-reduce | flops 6144 | bytes 49152 | tf_op jit(solution)/shard_map/psum | solution.py:1254
  (293 shorter events, 115.3 us)
Async XLA Ops:
  7.2 69.8 %copy-start.3 = (bf16[512,768]{1,0:T(8,128)(2,1)S(1)}, bf16[512,768]{1,0:T(8,128)(2,1)}, u32[]{:S(2)}) copy-start(bf16[512,768]{1,0:T(8,128)(2,1)} %param.15) | copy-start | bytes 2359300
  7.2 259.5 %all-gather.4.cloned.1.call-start = ((), (), s32[]{:S(2)}) async-start(), calls=%async_computation | async-start | bytes 10616832 | tf_op jit(solution)/shard_map/all_gather | solution.py:94
  7.9 281.6 %all-gather.6.cloned.1.call-start = ((), (), s32[]{:S(2)}) async-start(), calls=%async_computation.1 | async-start | bytes 10616832 | tf_op jit(solution)/shard_map/all_gather | solution.py:95
  83.1 12.9 %copy-start.23 = (bf16[512,768]{1,0:T(8,128)(2,1)}, bf16[512,768]{1,0:T(8,128)(2,1)S(1)}, u32[]{:S(2)}) copy-start(bf16[512,768]{1,0:T(8,128)(2,1)S(1)} %fusion.54) | copy-start | bytes 2359300
  95.9 30.7 %copy-start.13 = (bf16[768,4,192]{0,2,1:T(8,128)(2,1)}, bf16[768,4,192]{0,2,1:T(8,128)(2,1)S(1)}, u32[]{:S(2)}) copy-start(bf16[768,4,192]{0,2,1:T(8,128)(2,1)S(1)} %slice.123) | copy-start | bytes 3538948
  105.5 13.7 %copy-start.9 = (bf16[512,768]{0,1:T(8,128)(2,1)}, bf16[512,768]{0,1:T(8,128)(2,1)S(1)}, u32[]{:S(2)}) copy-start(bf16[512,768]{0,1:T(8,128)(2,1)S(1)} %copy.117) | copy-start | bytes 2359300
  107.3 26.5 %copy-start.31 = (bf16[768,8]{0,1:T(8,128)(2,1)}, bf16[768,8]{0,1:T(8,128)(2,1)S(1)}, u32[]{:S(2)}) copy-start(bf16[768,8]{0,1:T(8,128)(2,1)S(1)} %reshape.451) | copy-start | bytes 36868
  133.8 121.1 %copy-start.5 = (bf16[512,768]{1,0:T(8,128)(2,1)}, bf16[512,768]{1,0:T(8,128)(2,1)S(1)}, u32[]{:S(2)}) copy-start(bf16[512,768]{1,0:T(8,128)(2,1)S(1)} %fusion.60) | copy-start | bytes 2359300
  244.0 15.3 %slice-start.6 = ((s8[4718592]{0:T(1024)(128)(4,1)}), s8[4194304]{0:T(1024)(128)(4,1)S(1)}, s32[]{:S(2)}) async-start(s8[4718592]{0:T(1024)(128)(4,1)} %bitcast.188), calls=%async_computation.8 | async-start | bytes 8388608
  248.7 13.4 %copy-start.11 = (f32[512,3072]{1,0:T(8,128)}, f32[512,3072]{1,0:T(8,128)S(1)}, u32[]{:S(2)}) copy-start(f32[512,3072]{1,0:T(8,128)S(1)} %fusion.127) | copy-start | bytes 18874372
  266.7 13.4 %copy-start.66 = (bf16[8,144,768]{2,1,0:T(8,128)(2,1)S(1)}, bf16[8,144,768]{2,1,0:T(8,128)(2,1)}, u32[]{:S(2)}) copy-start(bf16[8,144,768]{2,1,0:T(8,128)(2,1)} %get-tuple-element.45) | copy-start | bytes 5308420
  289.5 19.1 %copy-start.64 = (bf16[8,144,768]{2,1,0:T(8,128)(2,1)S(1)}, bf16[8,144,768]{2,1,0:T(8,128)(2,1)}, u32[]{:S(2)}) copy-start(bf16[8,144,768]{2,1,0:T(8,128)(2,1)} %get-tuple-element.44) | copy-start | bytes 5308420
  308.6 24.0 %slice-start.8 = ((s8[9437184]{0:T(1024)(128)(4,1)}), s8[4194304]{0:T(1024)(128)(4,1)S(1)}, s32[]{:S(2)}) async-start(s8[9437184]{0:T(1024)(128)(4,1)} %bitcast.244), calls=%async_computation.10 | async-start | bytes 8388608
  457.6 16.0 %slice-start.3 = ((s8[12582912]{0:T(1024)(128)(4,1)}), s8[4194304]{0:T(1024)(128)(4,1)S(1)}, s32[]{:S(2)}) async-start(s8[12582912]{0:T(1024)(128)(4,1)} %bitcast.182), calls=%async_computation.5 | async-start | bytes 8388608
  457.6 16.0 %slice-start.4 = ((s8[12582912]{0:T(1024)(128)(4,1)}), s8[4194304]{0:T(1024)(128)(4,1)S(1)}, s32[]{:S(2)}) async-start(s8[12582912]{0:T(1024)(128)(4,1)} %bitcast.182), calls=%async_computation.6 | async-start | bytes 8388608
  464.4 21.4 %copy-start.67 = (bf16[12,512,64]{1,2,0:T(8,128)(2,1)}, bf16[12,512,64]{1,2,0:T(8,128)(2,1)S(1)}, u32[]{:S(2)}) copy-start(bf16[12,512,64]{1,2,0:T(8,128)(2,1)S(1)} %fusion.67) | copy-start | bytes 2359300
  507.0 79.8 %copy-start.6 = (bf16[512,768]{1,0:T(8,128)(2,1)S(1)}, bf16[512,768]{1,0:T(8,128)(2,1)}, u32[]{:S(2)}) copy-start(bf16[512,768]{1,0:T(8,128)(2,1)} %copy-done.5) | copy-start | bytes 2359300
  507.0 80.0 %copy-start.4 = (bf16[512,768]{1,0:T(8,128)(2,1)S(1)}, bf16[512,768]{1,0:T(8,128)(2,1)}, u32[]{:S(2)}) copy-start(bf16[512,768]{1,0:T(8,128)(2,1)} %param.15) | copy-start | bytes 2359300
  507.0 80.0 %copy-start.12 = (f32[512,768]{1,0:T(8,128)S(1)}, f32[512,768]{1,0:T(8,128)}, u32[]{:S(2)}) copy-start(f32[512,768]{1,0:T(8,128)} %get-tuple-element.81) | copy-start | bytes 4718596
  507.0 80.0 %copy-start.43 = (f32[512]{0:T(512)S(1)}, f32[512]{0:T(512)}, u32[]{:S(2)}) copy-start(f32[512]{0:T(512)} %copy-done.42) | copy-start | bytes 6148
  507.0 80.0 %copy-start.52 = (f32[512]{0:T(512)S(1)}, f32[512]{0:T(512)}, u32[]{:S(2)}) copy-start(f32[512]{0:T(512)} %copy-done.51) | copy-start | bytes 6148
  587.1 51.4 %copy-start.19 = (bf16[96,1152]{1,0:T(8,128)(2,1)S(1)}, bf16[96,1152]{1,0:T(8,128)(2,1)}, u32[]{:S(2)}) copy-start(bf16[96,1152]{1,0:T(8,128)(2,1)} %param.17) | copy-start | bytes 663556
  587.1 91.2 %copy-start.55 = (bf16[2,768]{1,0:T(2,128)(2,1)S(1)}, bf16[2,768]{1,0:T(2,128)(2,1)}, u32[]{:S(2)}) copy-start(bf16[2,768]{1,0:T(2,128)(2,1)} %param.16) | copy-start | bytes 9220
  594.7 84.5 %copy-start.46 = (f32[72,128]{1,0:T(8,128)S(1)}, f32[72,128]{1,0:T(8,128)}, u32[]{:S(2)}) copy-start(f32[72,128]{1,0:T(8,128)} %get-tuple-element.48) | copy-start | bytes 110596
  (58 other events, 255.3 us)
Sparse Core Ops, SparseCore 0:
  9.9 80.8 all-gather.3
  92.7 57.3 all-gather.5

commit v2 on v1

--- a/solution.py
+++ b/solution.py
@@ -699,6 +699,16 @@
         )
         self.own.start()
 
+    def send(self, step):
+        for j in (2 * step, 2 * step + 1):
+            if j:
+                self.copy(j, self.me).start()
+            else:
+                self.own = pltpu.make_async_copy(
+                    self.blocks.at[self.me], self.out.at[self.me], self.lsem
+                )
+                self.own.start()
+
     def finish(self):
         self.own.wait()
         for j in range(1, 8):
@@ -709,9 +719,38 @@
             copy.wait_send()
 
 
+def nt(left, right):
+    return lax.dot_general(left, right, (((1,), (1,)), ((), ())), preferred_element_type=jnp.float32)
+
+
+def tn(left, right):
+    return lax.dot_general(left, right, (((0,), (0,)), ((), ())), preferred_element_type=jnp.float32)
+
+
+def nn(left, right):
+    return jnp.dot(left, right, preferred_element_type=jnp.float32)
+
+
+GELU_SCALE = 0.7978845608028654
+
+
+def gelu_pair(v):
+    square = v * v
+    bend = jnp.tanh(GELU_SCALE * (v + 0.044715 * (square * v)))
+    half = 0.5 * (1.0 + bend)
+    slope = half + 0.5 * v * (1.0 - bend * bend) * (
+        GELU_SCALE * (1.0 + (3.0 * 0.044715) * square)
+    )
+    return v * half, slope
+
+
+HIDDEN = 512
+
+
 def out_kernel(
-    rows, grads, up_shard, down_shard, rows_in, grads_in, up_full, down_full,
-    s1, r1, s2, r2, ssem, rsem, ssem2, rsem2, lsem,
+    rows, grads, up_shard, down_shard, tokens, d_tokens,
+    rows_in, grads_in, mixed_out, d_tokens_out, up_grad, down_grad,
+    up_full, down_full, s1, r1, s2, r2, ssem, rsem, ssem2, rsem2, lsem,
 ):
     d, s, c = place()
     greet([device for _, device in group_of(d, s, c)] + [at(d, flip(s, 1), c), at(d, flip(s, 2), c)])
@@ -739,25 +778,50 @@
             g.corner(k)
     for g in both:
         g.finish()
+
+    mixed_out[...] = jnp.zeros_like(mixed_out)
+    d_tokens_out[...] = jnp.zeros_like(d_tokens_out)
+
+    def block(b, carry):
+        where = pl.ds(pl.multiple_of(b * HIDDEN, HIDDEN), HIDDEN)
+        up, down = up_full[:, where], down_full[:, where]
+        act, slope = gelu_pair(nn(tokens[...], up))
+        act = act.astype(jnp.bfloat16)
+        mixed_out[...] += nt(act, down)
+        down_grad[:, where] = tn(d_tokens[...], act).astype(jnp.bfloat16)
+        d_pre = (slope * nn(d_tokens[...], down)).astype(jnp.bfloat16)
+        d_tokens_out[...] += nt(d_pre, up)
+        up_grad[:, where] = tn(tokens[...], d_pre).astype(jnp.bfloat16)
+        return carry
+
+    lax.fori_loop(0, 3072 // HIDDEN, block, 0)
     swap_a.finish()
     swap_b.finish()
 
 
-def outbound(rows, grads, up_shard, down_shard):
+def outbound(rows, grads, up_shard, down_shard, tokens, d_tokens):
+    bf, f32 = jnp.bfloat16, jnp.float32
     return pl.pallas_call(
         out_kernel,
         out_shape=(
-            jax.ShapeDtypeStruct((8, 144, 768), jnp.bfloat16),
-            jax.ShapeDtypeStruct((8, 144, 768), jnp.bfloat16),
-            jax.ShapeDtypeStruct((768, 3072), jnp.bfloat16),
-            jax.ShapeDtypeStruct((768, 3072), jnp.bfloat16),
+            jax.ShapeDtypeStruct((8, 144, 768), bf),
+            jax.ShapeDtypeStruct((8, 144, 768), bf),
+            jax.ShapeDtypeStruct((512, 768), f32),
+            jax.ShapeDtypeStruct((512, 768), f32),
+            jax.ShapeDtypeStruct((768, 3072), bf),
+            jax.ShapeDtypeStruct((768, 3072), bf),
         ),
-        in_specs=[ONCHIP] * 4,
-        out_specs=(ANYWHERE,) * 4,
-        scratch_shapes=[DMA((8,))] * 4 + [DMA((GATHER_SEMS,))] * 4 + [DMA((4,))],
-        compiler_params=pltpu.CompilerParams(collective_id=1, has_side_effects=True),
+        in_specs=[ONCHIP] * 6,
+        out_specs=(ANYWHERE,) * 2 + (ONCHIP,) * 4,
+        scratch_shapes=[pltpu.VMEM((768, 3072), bf)] * 2
+        + [DMA((8,))] * 4
+        + [DMA((GATHER_SEMS,))] * 4
+        + [DMA((4,))],
+        compiler_params=pltpu.CompilerParams(
+            collective_id=1, has_side_effects=True, vmem_limit_bytes=60 << 20
+        ),
         name="outbound",
-    )(rows, grads, up_shard, down_shard)
+    )(rows, grads, up_shard, down_shard, tokens, d_tokens)
 
 
 def widened(ref):
@@ -765,10 +829,10 @@
 
 
 class ExpertSum:
-    def __init__(self, grad, out, own, near, far, last, outgoing, ssem, rsem, lsem):
-        self.grad, self.out, self.own, self.near = grad, out, own, near
+    def __init__(self, grad, out, near, far, last, outgoing, ssem, rsem):
+        self.grad, self.out, self.near = grad, out, near
         self.far, self.last, self.outgoing = far, last, outgoing
-        self.ssem, self.rsem, self.lsem = ssem, rsem, lsem
+        self.ssem, self.rsem = ssem, rsem
         self.d, self.s, self.c = place()
         self.sx, self.sy = flip(self.s, 1), flip(self.s, 2)
         self.sd = flip(self.sx, 2)
@@ -777,94 +841,152 @@
     def part(self, position, h):
         return self.grad.at[pl.ds(pl.multiple_of((2 * position + h) * self.rows, 32), self.rows)]
 
-    def start(self):
-        d, c = self.d, self.c
+    def copy(self, index, src, dst, position):
+        copy = push(src, dst, self.ssem.at[index], self.rsem.at[index], at(self.d, position, self.c))
+        copy.start()
+        return copy
+
+    def send_corner(self):
         self.one = [
-            push(self.part(self.sd, 0), self.near.at[0], self.ssem.at[0], self.rsem.at[0], at(d, self.sx, c)),
-            push(self.part(self.sd, 1), self.near.at[1], self.ssem.at[1], self.rsem.at[1], at(d, self.sy, c)),
+            self.copy(0, self.part(self.sd, 0), self.near.at[0], self.sx),
+            self.copy(1, self.part(self.sd, 1), self.near.at[1], self.sy),
         ]
-        self.two = [
-            push(self.part(self.sx, 0), self.far.at[0], self.ssem.at[2], self.rsem.at[2], at(d, self.sx, c)),
-            push(self.part(self.sy, 1), self.far.at[1], self.ssem.at[3], self.rsem.at[3], at(d, self.sy, c)),
-        ]
-        for copy in self.one + self.two:
-            copy.start()
-        self.local = [
-            pltpu.make_async_copy(self.part(self.sy, 0), self.own.at[0], self.lsem.at[0]),
-            pltpu.make_async_copy(self.part(self.sx, 1), self.own.at[1], self.lsem.at[1]),
-            pltpu.make_async_copy(self.part(self.s, 0), self.own.at[2], self.lsem.at[2]),
-            pltpu.make_async_copy(self.part(self.s, 1), self.own.at[3], self.lsem.at[3]),
-        ]
-        for copy in self.local:
-            copy.start()
-
-    def join(self):
-        d, c = self.d, self.c
-        for copy in self.local:
-            copy.wait()
-        targets = (at(d, self.sy, c), at(d, self.sx, c))
-        self.three = []
-        for h in range(2):
-            self.one[h].wait_recv()
-            self.outgoing[h] = (widened(self.own.at[h]) + widened(self.near.at[h])).astype(jnp.bfloat16)
-            copy = push(
-                self.outgoing.at[h], self.far.at[2 + h], self.ssem.at[4 + h], self.rsem.at[4 + h], targets[h]
-            )
-            copy.start()
-            self.three.append(copy)
+
+    def send_y(self):
+        self.two_y = self.copy(3, self.part(self.sy, 1), self.far.at[1], self.sy)
+
+    def send_x(self):
+        self.two_x = self.copy(2, self.part(self.sx, 0), self.far.at[0], self.sx)
+
+    def join_y(self):
+        self.one[0].wait_recv()
+        self.outgoing[0] = (widened(self.part(self.sy, 0)) + widened(self.near.at[0])).astype(jnp.bfloat16)
+        self.three_y = self.copy(4, self.outgoing.at[0], self.far.at[2], self.sy)
+
+    def join_x(self):
+        self.one[1].wait_recv()
+        self.outgoing[1] = (widened(self.part(self.sx, 1)) + widened(self.near.at[1])).astype(jnp.bfloat16)
+        self.three_x = self.copy(5, self.outgoing.at[1], self.far.at[3], self.sx)
 
     def close(self):
         d, s, c = self.d, self.s, self.c
-        for copy in self.two + self.three:
+        for copy in (self.two_x, self.two_y, self.three_x, self.three_y):
             copy.wait_recv()
-        low = (widened(self.own.at[2]) + widened(self.far.at[0])) + widened(self.far.at[2])
-        high = (widened(self.own.at[3]) + widened(self.far.at[1])) + widened(self.far.at[3])
-        self.outgoing[2] = jnp.where(c == 0, high, low).astype(jnp.bfloat16)
-        self.out[c] = jnp.where(c == 0, low, high)
+        mine, theirs = c, 1 - c
+        self.outgoing[2] = (
+            widened(self.part(s, theirs)) + widened(self.far.at[theirs]) + widened(self.far.at[2 + theirs])
+        ).astype(jnp.bfloat16)
         self.four = push(
             self.outgoing.at[2], self.last, self.ssem.at[6], self.rsem.at[6], at(d, s, 1 - c)
         )
         self.four.start()
+        self.out[c] = widened(self.part(s, mine)) + widened(self.far.at[mine]) + widened(self.far.at[2 + mine])
 
     def finish(self):
         self.four.wait_recv()
         self.out[1 - self.c] = widened(self.last)
-        for copy in self.one + self.two + self.three + [self.four]:
+        for copy in self.one + [self.two_x, self.two_y, self.three_x, self.three_y, self.four]:
             copy.wait_send()
 
 
-def back_kernel(
-    rows, grads, up_grad, down_grad, rows_in, grads_in, up_out, down_out,
-    uo, un, uf, ul, ug, do, dn, df, dl, dg, s1, r1, s2, r2, s3, r3, s4, r4, lsem, l3, l4,
+def expert_kernel(
+    rows, grads, up_all, down_all, rows_back, grads_back, up_out, down_out,
+    up, down, act, d_pre, made, d_made, total, d_total, up_grad, down_grad,
+    un, uf, ul, ug, dn, df, dl, dg, s1, r1, s2, r2, s3, r3, s4, r4, lsem, wsem,
 ):
+    bf = jnp.bfloat16
     d, s, c = place()
+    weights = [
+        pltpu.make_async_copy(up_all.at[c], up, wsem.at[0]),
+        pltpu.make_async_copy(down_all.at[c], down, wsem.at[1]),
+    ]
+    for copy in weights:
+        copy.start()
     greet([device for _, device in group_of(d, s, c)] + [at(d, flip(s, 1), c), at(d, flip(s, 2), c)])
-    swap_a = Swap(rows, rows_in, s1, r1, lsem.at[0])
-    swap_b = Swap(grads, grads_in, s2, r2, lsem.at[1])
-    sums = (
-        ExpertSum(up_grad, up_out, uo, un, uf, ul, ug, s3, r3, l3),
-        ExpertSum(down_grad, down_out, do, dn, df, dl, dg, s4, r4, l4),
-    )
-    for each in sums:
-        each.start()
-    swap_a.start()
-    swap_b.start()
-    for each in sums:
-        each.join()
-    for each in sums:
-        each.close()
-    for each in sums:
-        each.finish()
+    swap_a = Swap(made, rows_back, s1, r1, lsem.at[0])
+    swap_b = Swap(d_made, grads_back, s2, r2, lsem.at[1])
+    for copy in weights:
+        copy.wait()
+    for step in (2, 1, 3, 0):
+        there = lax.rem(d + step, 4)
+        chunk = pl.ds(2 * there, 2)
+        lines = pl.ds(pl.multiple_of(288 * there, 288), 288)
+        x = rows[chunk].reshape(288, 768)
+        g = grads[chunk].reshape(288, 768)
+        total[...] = jnp.zeros_like(total)
+        d_total[...] = jnp.zeros_like(d_total)
+
+        def block(b, carry):
+            where = pl.ds(pl.multiple_of(b * HIDDEN, HIDDEN), HIDDEN)
+            up_part, down_part = up[:, where], down[where]
+            made_act, slope = gelu_pair(nn(x, up_part))
+            made_act = made_act.astype(bf)
+            act[lines, where] = made_act
+            total[...] += nn(made_act, down_part)
+            d_part = (slope * nt(g, down_part)).astype(bf)
+            d_pre[lines, where] = d_part
+            d_total[...] += nt(d_part, up_part)
+            return carry
+
+        lax.fori_loop(0, 3072 // HIDDEN, block, 0)
+        made[chunk] = total[...].astype(bf).reshape(2, 144, 768)
+        d_made[chunk] = d_total[...].astype(bf).reshape(2, 144, 768)
+        swap_a.send(step)
+        swap_b.send(step)
+    first = ExpertSum(up_grad, up_out, un, uf, ul, ug, s3, r3)
+    second = ExpertSum(down_grad, down_out, dn, df, dl, dg, s4, r4)
+    x_all = rows.reshape(1152, 768)
+    g_all = grads.reshape(1152, 768)
+    y = s // 2
+
+    def up_rows(side):
+        here = pl.ds(pl.multiple_of(384 * side, 384), 384)
+        x_part = x_all[:, here]
+
+        def block(b, carry):
+            where = pl.ds(pl.multiple_of(b * HIDDEN, HIDDEN), HIDDEN)
+            up_grad[here, where] = tn(x_part, d_pre[:, where]).astype(bf)
+            return carry
+
+        lax.fori_loop(0, 3072 // HIDDEN, block, 0)
+
+    def down_rows(position):
+        def block(b, carry):
+            where = pl.ds(pl.multiple_of(768 * position + 384 * b, 384), 384)
+            down_grad[where] = tn(act[:, where], g_all[...]).astype(bf)
+            return carry
+
+        lax.fori_loop(0, 2, block, 0)
+
+    up_rows(1 - y)
+    first.send_corner()
+    first.send_y()
+    down_rows(second.sd)
+    second.send_corner()
+    first.join_y()
+    down_rows(second.sy)
+    second.send_y()
+    second.join_y()
+    up_rows(y)
+    first.send_x()
+    first.join_x()
+    down_rows(second.sx)
+    second.send_x()
+    second.join_x()
+    down_rows(s)
+    first.close()
+    second.close()
+    first.finish()
+    second.finish()
     swap_a.finish()
     swap_b.finish()
 
 
-def inbound(rows, grads, up_grad, down_grad):
+def experts(rows, grads, up_all, down_all):
     bf, f32 = jnp.bfloat16, jnp.float32
 
     def rooms(r, n):
         return [
-            pltpu.VMEM((4, r, n), bf),
             pltpu.VMEM((2, r, n), bf),
             pltpu.VMEM((4, r, n), bf),
             pltpu.VMEM((r, n), bf),
@@ -872,7 +994,7 @@
         ]
 
     return pl.pallas_call(
-        back_kernel,
+        expert_kernel,
         out_shape=(
             jax.ShapeDtypeStruct((8, 144, 768), bf),
             jax.ShapeDtypeStruct((8, 144, 768), bf),
@@ -881,13 +1003,27 @@
         ),
         in_specs=[ONCHIP, ONCHIP, ANYWHERE, ANYWHERE],
         out_specs=(ANYWHERE, ANYWHERE, ONCHIP, ONCHIP),
-        scratch_shapes=rooms(96, 3072)
+        scratch_shapes=[
+            pltpu.VMEM((768, 3072), bf),
+            pltpu.VMEM((3072, 768), bf),
+            pltpu.VMEM((1152, 3072), bf),
+            pltpu.VMEM((1152, 3072), bf),
+            pltpu.VMEM((8, 144, 768), bf),
+            pltpu.VMEM((8, 144, 768), bf),
+            pltpu.VMEM((288, 768), f32),
+            pltpu.VMEM((288, 768), f32),
+            pltpu.VMEM((768, 3072), bf),
+            pltpu.VMEM((3072, 768), bf),
+        ]
+        + rooms(96, 3072)
         + rooms(384, 768)
         + [DMA((8,))] * 8
-        + [DMA((2,)), DMA((4,)), DMA((4,))],
-        compiler_params=pltpu.CompilerParams(collective_id=2, has_side_effects=True),
-        name="inbound",
-    )(rows, grads, up_grad, down_grad)
+        + [DMA((2,)), DMA((2,))],
+        compiler_params=pltpu.CompilerParams(
+            collective_id=2, has_side_effects=True, vmem_limit_bytes=67043328
+        ),
+        name="experts",
+    )(rows, grads, up_all, down_all)
 
 
 class DenseSum:
@@ -990,38 +1126,142 @@
             copy.wait_send()
 
 
+class Tail:
+    def __init__(self, d_rows, router, act, ada, ada_out, d_act_out, router_out, z1, plane, plane_in, z2, z2_in, sems):
+        self.d_rows, self.router, self.act, self.ada = d_rows, router, act, ada
+        self.ada_out, self.d_act_out, self.router_out = ada_out, d_act_out, router_out
+        self.z1, self.plane, self.plane_in, self.z2, self.z2_in = z1, plane, plane_in, z2, z2_in
+        self.sems = sems
+        self.d, self.s, self.c = place()
+        self.f = 2 * self.s + self.c
+
+    def z_copy(self, k, src, dst, base):
+        send, recv = self.sems[base], self.sems[base + 1]
+        return push(src, dst, send.at[k], recv.at[k], at(lax.rem(self.d + k, 4), self.s, self.c))
+
+    def f_copy(self, k, src, dst, base):
+        send, recv = self.sems[base], self.sems[base + 1]
+        return push(src, dst, send.at[k], recv.at[k], (self.d, lax.rem(self.f + k, 8)))
+
+    def start(self):
+        self.all = [
+            self.z_copy(k, self.d_rows.at[lax.rem(self.d + k, 4)], self.z1.at[k], 0) for k in range(1, 4)
+        ]
+        for copy in self.all:
+            copy.start()
+
+    def second(self):
+        total = self.d_rows[self.d]
+        for k in range(1, 4):
+            self.all[k - 1].wait_recv()
+            total = total + self.z1[k]
+        for target in range(8):
+            self.plane[target, :, 0:1152] = total
+            self.plane[target, :, 1152:1280] = self.router[target]
+        copies = [
+            self.f_copy(k, self.plane.at[lax.rem(self.f + k, 8)], self.plane_in.at[lax.rem(8 - k, 8)], 2)
+            for k in range(1, 8)
+        ]
+        for copy in copies:
+            copy.start()
+        self.in_plane = copies
+        self.all = self.all + copies
+
+    def third(self):
+        f = self.f
+        self.plane_in[0] = self.plane[f]
+        for copy in self.in_plane:
+            copy.wait_recv()
+        everything = self.plane_in[...]
+        router = jnp.sum(everything[:, :, 1152:1280], axis=0)
+        rows = everything[:, :, 0:1152].reshape(64, 1152)
+        line = lax.broadcasted_iota(jnp.int32, (64, 64), 0)
+        column = lax.broadcasted_iota(jnp.int32, (64, 64), 1)
+        turn = (lax.rem(line // 8 + 8 - f, 8) * 8 + lax.rem(line, 8) == column).astype(jnp.bfloat16)
+        d_mod = nn(turn, rows.astype(jnp.bfloat16)).astype(jnp.bfloat16)
+        self.ada_out[...] = tn(self.act[...], d_mod)[0:96]
+        part = nt(d_mod, self.ada[...])
+        self.z2[0:64, 0:96] = part
+        self.z2[0:64, 96:128] = jnp.zeros((64, 32), jnp.float32)
+        self.z2[64:72, :] = router
+        copies = [self.z_copy(k, self.z2, self.z2_in.at[k], 4) for k in range(1, 4)]
+        for copy in copies:
+            copy.start()
+        self.along = copies
+        self.all = self.all + copies
+
+    def fourth(self):
+        total = self.z2[...]
+        for k in range(1, 4):
+            self.along[k - 1].wait_recv()
+            total = total + self.z2_in[k]
+        self.router_out[...] = total[64:72]
+        self.z2_in[0] = total
+        copies = [
+            self.f_copy(
+                k,
+                self.z2_in.at[0, pl.ds(pl.multiple_of(8 * lax.rem(self.f + k, 8), 8), 8)],
+                self.d_act_out.at[self.f],
+                6,
+            )
+            for k in range(1, 8)
+        ]
+        for copy in copies:
+            copy.start()
+        self.d_act_out[self.f] = self.z2_in[0, pl.ds(pl.multiple_of(8 * self.f, 8), 8)]
+        self.last = copies
+        self.all = self.all + copies
+
+    def finish(self):
+        for k in range(1, 8):
+            self.f_copy(
+                k, self.z2_in.at[0, pl.ds(0, 8)], self.d_act_out.at[lax.rem(self.f + 8 - k, 8)], 6
+            ).wait_recv()
+        for copy in self.all:
+            copy.wait_send()
+
+
 def dense_kernel(kinds, *refs):
     n = len(kinds)
-    grads, outs, rest = refs[:n], refs[n : 2 * n], refs[2 * n :]
+    grads, small, outs = refs[:n], refs[n : n + 4], refs[n + 4 : 2 * n + 4]
+    small_outs, rest = refs[2 * n + 4 : 2 * n + 7], refs[2 * n + 7 :]
     d, s, c = place()
+    f = 2 * s + c
     greet(
         [at(lax.rem(d + k, 4), s, c) for k in range(1, 4)]
-        + [at(d, s, 1 - c), at(d, flip(s, 1), c), at(d, flip(s, 2), c)]
+        + [(d, lax.rem(f + k, 8)) for k in range(1, 8)]
     )
     sums = [
         DenseSum(kinds[i], grads[i], outs[i], *rest[8 * i : 8 * i + 8]) for i in range(n)
     ]
+    rest = rest[8 * n :]
+    tail = Tail(*small, *small_outs, *rest[:5], rest[5:])
+    tail.start()
     for each in sums:
         each.start()
+    tail.second()
     for each in sums:
         each.merge()
+    tail.third()
     for each in sums:
         each.join()
+    tail.fourth()
     for each in sums:
         each.along()
     for each in sums:
         each.finish()
-
-
-def dense_sums(kinds, grads, collective_id):
-    bf = jnp.bfloat16
+    tail.finish()
+
+
+def dense_sums(kinds, grads, small, collective_id):
+    bf, f32 = jnp.bfloat16, jnp.float32
     outs, scratch = [], []
     for kind in kinds:
         if kind == "cols":
             piece, half, quarter = (96, 3072), (96, 1536), (96, 768)
         else:
             piece, half, quarter = (768, 384), (384, 384), (192, 384)
-        outs.append(jax.ShapeDtypeStruct(quarter, jnp.float32))
+        outs.append(jax.ShapeDtypeStruct(quarter, f32))
         scratch += [
             pltpu.VMEM((4,) + piece, bf),
             pltpu.VMEM((4,) + piece, bf),
@@ -1032,27 +1272,28 @@
             DMA((11,)),
             DMA((4,)),
         ]
+    outs += [
+        jax.ShapeDtypeStruct((96, 1152), f32),
+        jax.ShapeDtypeStruct((8, 8, 128), f32),
+        jax.ShapeDtypeStruct((8, 128), f32),
+    ]
+    scratch += [
+        pltpu.VMEM((4, 8, 1152), f32),
+        pltpu.VMEM((8, 8, 1280), f32),
+        pltpu.VMEM((8, 8, 1280), f32),
+        pltpu.VMEM((72, 128), f32),
+        pltpu.VMEM((4, 72, 128), f32),
+        DMA((4,)), DMA((4,)), DMA((8,)), DMA((8,)), DMA((4,)), DMA((4,)), DMA((8,)), DMA((8,)),
+    ]
     return pl.pallas_call(
         functools.partial(dense_kernel, kinds),
         out_shape=tuple(outs),
-        in_specs=[ANYWHERE] * len(kinds),
-        out_specs=(ONCHIP,) * len(kinds),
+        in_specs=[ANYWHERE] * len(kinds) + [ONCHIP] * 4,
+        out_specs=(ONCHIP,) * len(outs),
         scratch_shapes=scratch,
         compiler_params=pltpu.CompilerParams(collective_id=collective_id, has_side_effects=True),
         name="dense_sums",
-    )(*grads)
-
-
-def nt(left, right):
-    return lax.dot_general(left, right, (((1,), (1,)), ((), ())), preferred_element_type=jnp.float32)
-
-
-def tn(left, right):
-    return lax.dot_general(left, right, (((0,), (0,)), ((), ())), preferred_element_type=jnp.float32)
-
-
-def nn(left, right):
-    return jnp.dot(left, right, preferred_element_type=jnp.float32)
+    )(*grads, *small)
 
 
 def fitted_shards(
@@ -1072,13 +1313,10 @@
 ):
     bf = jnp.bfloat16
     d_index, f_index = lax.axis_index("dp"), lax.axis_index("fsdp")
-    core = lax.rem(f_index, 2)
     model_width = tokens.shape[1]
     head_size = model_width // HEADS
     inside, segment = owners(image_sizes)
     up_all, down_all = gather_experts(expert_up, expert_down)
-    up_mine = lax.dynamic_index_in_dim(up_all, core, 0, keepdims=False)
-    down_mine = lax.dynamic_index_in_dim(down_all, core, 0, keepdims=False)
     ids = jnp.arange(EXPERTS, dtype=jnp.int32)
     hot = routes[:, :, None] == ids[None, None, :]
     hot_any = jnp.any(hot, axis=1).astype(bf)
@@ -1101,7 +1339,6 @@
     router_pack = jnp.pad(router_weight.reshape(192), (0, 2048 - 192)).reshape(16, 128)
     qkvo_shard = jnp.concatenate([qkv_weight, out_weight], axis=1)
     qkvo, routers, seen, mod_rows = opening(qkvo_shard, router_pack, act_slices, ada_pad)
-    activated_all = seen[:64, :96].astype(bf)
     expert_counts = seen[66, :EXPERTS].astype(jnp.int32)
     modulation = lax.dynamic_slice(mod_rows, (0, 2 * d_index, 0), (4, 2, 1152))
     modulation = modulation.transpose(1, 0, 2).reshape(2, 4608)
@@ -1156,34 +1393,14 @@
         .astype(bf)
         .reshape(EXPERTS, CAP, model_width)
     )
-    rows_in, grads_in, shared_first, shared_second = outbound(rows, grads, shared_up, shared_down.T)
-    rows_in = rows_in.reshape(EXPERTS * CAP, model_width)
-    grads_in = grads_in.reshape(EXPERTS * CAP, model_width)
-    expert_pre = nn(rows_in, up_mine)
-    expert_act = gelu_tanh(expert_pre).astype(bf)
-    expert_out = nn(expert_act, down_mine).astype(bf)
-    d_act = nt(grads_in, down_mine)
-    d_pre = gelu_back(expert_pre, d_act).astype(bf)
-    d_rows = nt(d_pre, up_mine).astype(bf)
-    down_grad = tn(expert_act, grads_in).astype(bf)
-    up_grad = tn(rows_in, d_pre).astype(bf)
-    returned, d_returned, expert_up_grad, expert_down_grad = inbound(
-        expert_out.reshape(EXPERTS, CAP, model_width),
-        d_rows.reshape(EXPERTS, CAP, model_width),
-        up_grad,
-        down_grad,
+    rows_in, grads_in, shared_out, d_second, shared_first_grad, shared_second_grad = outbound(
+        rows, grads, shared_up, shared_down.T, second_input, d_mixed.astype(bf)
+    )
+    returned, d_returned, expert_up_grad, expert_down_grad = experts(
+        rows_in, grads_in, up_all, down_all
     )
     returned = returned.reshape(EXPERTS * CAP, model_width)
     d_returned = d_returned.reshape(EXPERTS * CAP, model_width)
-    shared_pre = nn(second_input, shared_first)
-    shared_act = gelu_tanh(shared_pre).astype(bf)
-    shared_out = nt(shared_act, shared_second)
-    d_shared = d_mixed.astype(bf)
-    shared_second_grad = tn(d_shared, shared_act).astype(bf)
-    d_shared_act = nn(d_shared, shared_second)
-    d_shared_pre = gelu_back(shared_pre, d_shared_act).astype(bf)
-    shared_first_grad = tn(second_input, d_shared_pre).astype(bf)
-    d_second = nt(d_shared_pre, shared_first)
     picked_0 = tn(send_0, returned)
     picked_1 = tn(send_1, returned)
     mixed = shared_out + (gate_share[:, 0:1] * picked_0 + gate_share[:, 1:2] * picked_1)
@@ -1237,22 +1454,23 @@
         ],
         axis=1,
     ).astype(bf)
-    shared_first_sum, shared_second_sum, qkvo_sum = dense_sums(
-        ("cols", "rows", "cols"), (shared_first_grad, shared_second_grad, qkvo_grad), 3
-    )
-    d_mod_all = lax.all_gather(d_modulation, ("dp", "fsdp"), axis=0)
-    d_mod_all = lax.dynamic_slice(d_mod_all, (0, 0, 1152 * d_index), (32, 2, 1152))
-    d_mod_all = d_mod_all.reshape(4, 8, 2, 1152).transpose(1, 0, 2, 3).reshape(64, 1152)
-    ada_grad = tn(activated_all, d_mod_all)
-    partial = nt(d_mod_all, ada_weight).reshape(8, 4, 2, 96)
-    partial_all = lax.all_gather(partial, ("dp", "fsdp"), axis=0)
-    partial_mine = lax.dynamic_slice(
-        partial_all, (0, f_index, d_index, 0, 0), (32, 1, 1, 2, 96)
-    ).reshape(4, 8, 2, 96)
-    d_activated = jnp.sum(partial_mine, axis=0).transpose(1, 0, 2).reshape(2, 768)
+    d_mod_rows = d_modulation.astype(jnp.float32).reshape(2, 4, 1152).transpose(1, 0, 2)
+    d_mod_rows = lax.dynamic_update_slice(
+        jnp.zeros((4, 8, 1152), jnp.float32), d_mod_rows, (0, 2 * d_index, 0)
+    )
+    router_tiles = jnp.pad(
+        router_grad.reshape(EXPERTS, 8, 96).transpose(1, 0, 2), ((0, 0), (0, 0), (0, 32))
+    )
+    shared_first_sum, shared_second_sum, qkvo_sum, ada_grad, d_act_tiles, router_sum = dense_sums(
+        ("cols", "rows", "cols"),
+        (shared_first_grad, shared_second_grad, qkvo_grad),
+        (d_mod_rows, router_tiles, seen[:64].astype(bf), ada_weight),
+        3,
+    )
+    d_activated = lax.dynamic_slice(d_act_tiles, (0, 2 * d_index, 0), (8, 2, 96))
+    d_activated = d_activated.transpose(1, 0, 2).reshape(2, model_width)
     condition_grad = jax.vjp(jax.nn.silu, cond_float)[1](d_activated)[0]
-    router_sum = lax.psum(router_grad, ("dp", "fsdp"))
-    router_out = lax.dynamic_slice(router_sum, (2 * d_index, 96 * f_index), (2, 96)).T
+    router_out = lax.dynamic_slice(router_sum, (2 * d_index, 0), (2, 96)).T
     return (
         output,
         tokens_grad,

time: 739 us -> 579 us (0.78)
  blocking collectives: 120 us -> 0 us
  matrix products: 179 us -> 76.2 us
  Pallas kernels: 330 us -> 389 us
    all_gather x2 -> x0, blocking collectives: 82.9 us -> none  [the longest x1 43.4 us: fitted_shards(): d_mod_all = lax.all_gather(d_modulation, ('dp', 'fsdp'), axis=0)]
    pallas_call x1, Pallas kernels: 95.7 us -> 140 us  [experts(): pl.pallas_call(expert_kernel, out_shape=(jax.ShapeDtypeStruct((8, 144, 76...]
    dot_general x8 -> x3, matrix products: 50.3 us -> 7.41 us  [nt(): lax.dot_general(left, right, (((1,), (1,)), ((), ())), preferred_element_...]
    psum x1 -> x0, blocking collectives: 37.1 us -> none  [fitted_shards(): router_sum = lax.psum(router_grad, ('dp', 'fsdp'))]
    dot_general x10 -> x6, matrix products: 46.3 us -> 12.1 us  [nn(): return jnp.dot(left, right, preferred_element_type=jnp.float32)]
    dot_general x11 -> x6, matrix products: 44.2 us -> 17.5 us  [tn(): lax.dot_general(left, right, (((0,), (0,)), ((), ())), preferred_element_...]
    pallas_call x1, Pallas kernels: 76.5 us -> 86.6 us  [dense_sums(): pl.pallas_call(functools.partial(dense_kernel, kinds), out_shape=tuple(ou...]
    unnamed x166 -> x164, local copies, waits for them, and re-layouts: 15 us -> 13.8 us
  transfers between devices with their start and end apart: 2 -> 2, of which waited for: 0 -> 0; matrix products, arithmetic and copies ran while one was open for 15% -> 12% of each run, Pallas kernels for 22% -> 28%
where the time goes in v2:
time: 579 us; the launch traced here: 575 us
  Pallas kernels  389 us (67%)
  matrix products  76.2 us (13%)
  local copies, waits for them, and re-layouts  61.4 us (11%)
  other arithmetic  31.2 us (5%)
  between operations  15.6 us (3%)
    pallas_call x1, Pallas kernels, experts(): pl.pallas_call(expert_kernel, out_shape=(jax.ShapeDtypeStruct((8, 144, 76...  140 us
    pallas_call x1, Pallas kernels, outbound(): pl.pallas_call(out_kernel, out_shape=(jax.ShapeDtypeStruct((8, 144, 768),...  105 us
    pallas_call x1, Pallas kernels, dense_sums(): pl.pallas_call(functools.partial(dense_kernel, kinds), out_shape=tuple(ou...  86.6 us
    pallas_call x1, Pallas kernels, opening(): pl.pallas_call(open_kernel, out_shape=(jax.ShapeDtypeStruct((768, 3072),...  57.9 us
    dot_general x6, matrix products, tn(): lax.dot_general(left, right, (((0,), (0,)), ((), ())), preferred_element_...  17.5 us
    unnamed x164, local copies, waits for them, and re-layouts  13.8 us
    dot_general x6, matrix products, nn(): return jnp.dot(left, right, preferred_element_type=jnp.float32)  12.1 us
    dot_general x1, matrix products, fitted_shards(): jnp.einsum('hqd,hkd->hqk', d_attended, values, preferred_element_type=jnp...  12 us
  transfers between devices with their start and end apart: 2, of which 0 were waited for; matrix products, arithmetic and copies ran while one was open for 12% of the time, Pallas kernels for 28%

profile of v2, /device:TPU:0, one launch (start us, length us, event | category | flops | bytes accessed | tf_op | source)
XLA Modules:
  0.0 574.7 jit_solution(6149419124977019626)
XLA Ops:
  12.7 57.9 %opening.1 = (bf16[768,3072]{1,0:T(8,128)(2,1)}, bf16[32,16,128]{2,1,0:T(8,128)(2,1)}, f32[72,128]{1,0:T(8,128)}, f32[4,8,1152]{2,1,0:T(8,128)}) custom-call(bf16[96,768]{1,0:T(8,128)(2,1)} %pad_maximum_fusion.4.shard, bf16[16,128]{1,0:T(8,128)(2,1)} %pad_bitcast_fusion.router, f32[8,8,128]{2,1,0:T(8,128)} %copy-done.32, bf16[128,1152]{1,0:T(8,128)(2,1)} %pad.26.ada_ref), custom_call_target="tpu_custom_call" | custom-call | tf_op jit(solution)/shard_map/opening/pallas_call | solution.py:649
  70.6 7.2 %copy.91 = bf16[768,3072]{0,1:T(8,128)(2,1)} copy(bf16[768,3072]{1,0:T(8,128)(2,1)} %get-tuple-element.45) | data formatting | bytes 9437184 | tf_op jit(solution)/shard_map/reshape | solution.py:1351
  77.8 4.0 slice.119
  87.6 4.2 copy-done.11
  96.7 2.6 copy.66
  105.1 11.1 %fusion.82 = (f32[12,512]{1,0:T(8,128)}, f32[12,512,512]{1,2,0:T(8,128)}) fusion(pred[512,512]{0,1:T(8,128)(4,1)} %broadcast_compare_fusion, bf16[12,512,64]{1,2,0:T(8,128)(2,1)} %bitcast.132, bf16[12,512,64]{1,2,0:T(8,128)(2,1)S(1)} %bitcast.121), kind=kOutput, calls=%fused_computation.171 | convolution fusion | flops 415236608 | bytes 14442496 | tf_op jit(solution)/shard_map/sub | solution.py:1371
  116.2 7.2 %fusion.33 = bf16[12,512,64]{1,2,0:T(8,128)(2,1)S(1)} fusion(bf16[12,512,64]{1,2,0:T(8,128)(2,1)S(1)} %bitcast.135, f32[12,512,512]{1,2,0:T(8,128)} %get-tuple-element.113, f32[12,512]{1,0:T(8,128)} %get-tuple-element.112), kind=kOutput, calls=%fused_computation.83 | convolution fusion | flops 409337856 | bytes 14180352 | tf_op jit(solution)/shard_map/hqk,hkd->hqd/dot_general | solution.py:1375
  123.4 3.7 fusion.77
  137.3 3.2 convolution_convert_fusion.2
  140.5 104.6 %outbound.1 = (bf16[8,144,768]{2,1,0:T(8,128)(2,1)}, bf16[8,144,768]{2,1,0:T(8,128)(2,1)}, f32[512,768]{1,0:T(8,128)}, f32[512,768]{1,0:T(8,128)}, bf16[768,3072]{1,0:T(8,128)(2,1)}, /*index=5*/bf16[768,3072]{1,0:T(8,128)(2,1)}) custom-call(bf16[8,144,768]{2,1,0:T(8,128)(2,1)} %bitcast.130, bf16[8,144,768]{2,1,0:T(8,128)(2,1)} %bitcast.131, ...), custom_call_target="tpu_custom_call" | custom-call | tf_op jit(solution)/shard_map/outbound/pallas_call | solution.py:804
  246.4 139.7 %experts.1 = (bf16[8,144,768]{2,1,0:T(8,128)(2,1)}, bf16[8,144,768]{2,1,0:T(8,128)(2,1)}, f32[2,96,3072]{2,1,0:T(8,128)}, f32[2,384,768]{2,1,0:T(8,128)}) custom-call(bf16[8,144,768]{2,1,0:T(8,128)(2,1)} %get-tuple-element.48.rows, bf16[8,144,768]{2,1,0:T(8,128)(2,1)} %get-tuple-element.49.grads, bf16[2,768,3072]{2,1,0:T(8,128)(2,1)} %all-gather.3.cloned.1.call-done.up_all, ...), custom_call_target="tpu_custom_call" | custom-call | tf_op jit(solution)/shard_map/experts/pallas_call | solution.py:996
  386.2 3.0 fusion.14
  389.3 4.9 multiply_reduce_fusion.2
  402.6 12.0 %multiply_reduce_fusion = (f32[12,512]{1,0:T(8,128)S(1)}, f32[12,512,512]{1,2,0:T(8,128)}) fusion(f32[12,512,512]{1,2,0:T(8,128)} %get-tuple-element.113, f32[12,512]{1,0:T(8,128)S(1)} %copy-done.47, bf16[12,512,64]{1,2,0:T(8,128)(2,1)} %bitcast.136, bf16[12,512,64]{1,2,0:T(8,128)(2,1)} %bitcast.134), kind=kOutput, calls=%fused_computation.2 | convolution fusion | flops 412084224 | bytes 26787840 | tf_op jit(solution)/shard_map/hqd,hkd->hqk/dot_general | solution.py:1425
  414.6 7.0 %multiply_convert_fusion = bf16[12,512,512]{1,2,0:T(8,128)(2,1)S(1)} fusion(f32[12,512,512]{1,2,0:T(8,128)} %get-tuple-element.117, f32[12,512]{1,0:T(8,128)S(1)} %get-tuple-element.116, f32[12,512,512]{1,2,0:T(8,128)S(1)} %bitcast.120, f32[12,512]{1,0:T(8,128)S(1)} %copy-done.47), kind=kLoop, calls=%fused_computation.1 | loop fusion | flops 12582912 | bytes 31506432 | tf_op jit(solution)/shard_map/convert_element_type | solution.py:1428
  423.6 2.9 multiply_convert_fusion.1
  426.5 4.1 fusion.36
  430.8 5.9 %convolution_convert_fusion = bf16[768,2304]{1,0:T(8,128)(2,1)} fusion(bf16[512,768]{1,0:T(8,128)(2,1)} %copy-done.25, bf16[512,768]{0,1:T(8,128)(2,1)} %bitcast.180, bf16[512,768]{0,1:T(8,128)(2,1)} %bitcast.178, bf16[512,768]{0,1:T(8,128)(2,1)} %bitcast.128), kind=kOutput, calls=%fused_computation.11 | convolution fusion | flops 1820786688 | bytes 6684672 | tf_op jit(solution)/shard_map/dot_general | solution.py:727
  436.7 5.1 fusion.75
  442.0 5.8 %copy.77 = bf16[768,2304]{0,1:T(8,128)(2,1)} copy(bf16[768,2304]{1,0:T(8,128)(2,1)} %convolution_convert_fusion) | data formatting | bytes 7077888 | tf_op jit(solution)/shard_map/convert.39
  452.3 4.5 pad_maximum_fusion
  456.7 6.9 %copy.90.refs_2_ = bf16[768,3072]{1,0:T(8,128)(2,1)} copy(bf16[768,3072]{0,1:T(8,128)(2,1)} %bitcast.117) | data formatting | bytes 9437184 | tf_op jit(solution)/shard_map/convert_element_type | solution.py:1447
  465.1 86.6 %dense_sums.1 = (f32[96,768]{1,0:T(8,128)}, f32[192,384]{1,0:T(8,128)}, f32[96,768]{1,0:T(8,128)}, f32[96,1152]{1,0:T(8,128)}, f32[8,8,128]{2,1,0:T(8,128)}, /*index=5*/f32[8,128]{1,0:T(8,128)}) custom-call(bf16[768,3072]{1,0:T(8,128)(2,1)} %get-tuple-element.53.refs_0_, bf16[768,3072]{1,0:T(8,128)(2,1)} %get-tuple-element.54.refs_1_, ...), custom_call_target="tpu_custom_call" | custom-call | tf_op jit(solution)/shard_map/dense_sums/pallas_call | solution.py:1288
  557.8 3.7 fusion.27
  (274 shorter events, 61.4 us)
Async XLA Ops:
  7.3 239.1 %all-gather.3.cloned.1.call-start = ((), (), s32[]{:S(2)}) async-start(), calls=%async_computation | async-start | bytes 10616832 | tf_op jit(solution)/shard_map/all_gather | solution.py:94
  8.0 238.4 %all-gather.5.cloned.1.call-start = ((), (), s32[]{:S(2)}) async-start(), calls=%async_computation.1 | async-start | bytes 10616832 | tf_op jit(solution)/shard_map/all_gather | solution.py:95
  83.2 40.2 %copy-start.9 = (bf16[768,4,192]{0,2,1:T(8,128)(2,1)}, bf16[768,4,192]{0,2,1:T(8,128)(2,1)S(1)}, u32[]{:S(2)}) copy-start(bf16[768,4,192]{0,2,1:T(8,128)(2,1)S(1)} %slice.123) | copy-start | bytes 3538948
  87.2 6.7 %copy-start = (f32[512,4608]{1,0:T(8,128)}, f32[512,4608]{1,0:T(8,128)S(1)}, u32[]{:S(2)}) copy-start(f32[512,4608]{1,0:T(8,128)S(1)} %multiply_add_fusion) | copy-start | bytes 28311556
  87.6 6.3 %copy-start.25 = (bf16[512,768]{1,0:T(8,128)(2,1)}, bf16[512,768]{1,0:T(8,128)(2,1)S(1)}, u32[]{:S(2)}) copy-start(bf16[512,768]{1,0:T(8,128)(2,1)S(1)} %fusion.23) | copy-start | bytes 2359300
  96.7 8.5 %copy-start.7 = (bf16[512,768]{0,1:T(8,128)(2,1)}, bf16[512,768]{0,1:T(8,128)(2,1)S(1)}, u32[]{:S(2)}) copy-start(bf16[512,768]{0,1:T(8,128)(2,1)S(1)} %copy.67) | copy-start | bytes 2359300
  102.1 28.6 %copy-start.34 = (bf16[768,8]{0,1:T(8,128)(2,1)}, bf16[768,8]{0,1:T(8,128)(2,1)S(1)}, u32[]{:S(2)}) copy-start(bf16[768,8]{0,1:T(8,128)(2,1)S(1)} %reshape.346) | copy-start | bytes 36868
  105.1 11.1 %copy-start.23 = (bf16[512,768]{0,1:T(8,128)(2,1)S(1)}, bf16[512,768]{0,1:T(8,128)(2,1)}, u32[]{:S(2)}) copy-start(bf16[512,768]{0,1:T(8,128)(2,1)} %copy.68) | copy-start | bytes 2359300
  386.2 9.8 %slice-start = ((s8[9437184]{0:T(1024)(128)(4,1)}), s8[4194304]{0:T(1024)(128)(4,1)S(1)}, s32[]{:S(2)}) async-start(s8[9437184]{0:T(1024)(128)(4,1)} %bitcast.113), calls=%async_computation.2 | async-start | bytes 8388608
  389.3 6.7 %slice-start.1 = ((s8[9437184]{0:T(1024)(128)(4,1)}), s8[4194304]{0:T(1024)(128)(4,1)S(1)}, s32[]{:S(2)}) async-start(s8[9437184]{0:T(1024)(128)(4,1)} %bitcast.113), calls=%async_computation.3 | async-start | bytes 8388608
  389.3 6.7 %slice-start.2 = ((s8[9437184]{0:T(1024)(128)(4,1)}), s8[1048576]{0:T(1024)(128)(4,1)S(1)}, s32[]{:S(2)}) async-start(s8[9437184]{0:T(1024)(128)(4,1)} %bitcast.113), calls=%async_computation.4 | async-start | bytes 2097152
  402.6 12.0 %slice-start.3 = ((s8[12582912]{0:T(1024)(128)(4,1)}), s8[4194304]{0:T(1024)(128)(4,1)S(1)}, s32[]{:S(2)}) async-start(s8[12582912]{0:T(1024)(128)(4,1)} %bitcast.119), calls=%async_computation.5 | async-start | bytes 8388608
  402.6 12.0 %slice-start.4 = ((s8[12582912]{0:T(1024)(128)(4,1)}), s8[4194304]{0:T(1024)(128)(4,1)S(1)}, s32[]{:S(2)}) async-start(s8[12582912]{0:T(1024)(128)(4,1)} %bitcast.119), calls=%async_computation.6 | async-start | bytes 8388608
  402.6 12.0 %slice-start.5 = ((s8[12582912]{0:T(1024)(128)(4,1)}), s8[4194304]{0:T(1024)(128)(4,1)S(1)}, s32[]{:S(2)}) async-start(s8[12582912]{0:T(1024)(128)(4,1)} %bitcast.119), calls=%async_computation.7 | async-start | bytes 8388608
  414.6 7.0 %copy-start.8 = (bf16[512,768]{0,1:T(8,128)(2,1)S(1)}, bf16[512,768]{0,1:T(8,128)(2,1)}, u32[]{:S(2)}) copy-start(bf16[512,768]{0,1:T(8,128)(2,1)} %copy-done.7) | copy-start | bytes 2359300
  430.7 6.0 %copy-start.4 = (bf16[512,768]{1,0:T(8,128)(2,1)S(1)}, bf16[512,768]{1,0:T(8,128)(2,1)}, u32[]{:S(2)}) copy-start(bf16[512,768]{1,0:T(8,128)(2,1)} %param.15) | copy-start | bytes 2359300
  430.7 6.0 %copy-start.12 = (bf16[768,4,576]{0,2,1:T(8,128)(2,1)S(1)}, bf16[768,4,576]{0,2,1:T(8,128)(2,1)}, u32[]{:S(2)}) copy-start(bf16[768,4,576]{0,2,1:T(8,128)(2,1)} %slice.119) | copy-start | bytes 10616836
  430.7 6.0 %copy-start.16 = (bf16[12,512,64]{1,2,0:T(8,128)(2,1)S(1)}, bf16[12,512,64]{1,2,0:T(8,128)(2,1)}, u32[]{:S(2)}) copy-start(bf16[12,512,64]{1,2,0:T(8,128)(2,1)} %multiply_convert_fusion.2) | copy-start | bytes 2359300
  430.7 5.9 %copy-start.19 = (f32[512,768]{1,0:T(8,128)S(1)}, f32[512,768]{1,0:T(8,128)}, u32[]{:S(2)}) copy-start(f32[512,768]{1,0:T(8,128)} %get-tuple-element.114) | copy-start | bytes 4718596
  430.7 5.9 %copy-start.49 = (f32[512]{0:T(512)S(1)}, f32[512]{0:T(512)}, u32[]{:S(2)}) copy-start(f32[512]{0:T(512)} %copy-done.48) | copy-start | bytes 6148
  430.7 5.9 %copy-start.55 = (f32[512]{0:T(512)S(1)}, f32[512]{0:T(512)}, u32[]{:S(2)}) copy-start(f32[512]{0:T(512)} %copy-done.54) | copy-start | bytes 6148
  430.8 5.9 %copy-start.71 = (bf16[12,512,64]{1,2,0:T(8,128)(2,1)S(1)}, bf16[12,512,64]{1,2,0:T(8,128)(2,1)}, u32[]{:S(2)}) copy-start(bf16[12,512,64]{1,2,0:T(8,128)(2,1)} %multiply_convert_fusion.1) | copy-start | bytes 2359300
  465.1 90.8 %copy-start.59 = (bf16[2,768]{1,0:T(2,128)(2,1)S(1)}, bf16[2,768]{1,0:T(2,128)(2,1)}, u32[]{:S(2)}) copy-start(bf16[2,768]{1,0:T(2,128)(2,1)} %param.16) | copy-start | bytes 9220
  557.8 6.0 %copy-start.18 = (f32[2,96,3072]{2,1,0:T(8,128)S(1)}, f32[2,96,3072]{2,1,0:T(8,128)}, u32[]{:S(2)}) copy-start(f32[2,96,3072]{2,1,0:T(8,128)} %get-tuple-element.142) | copy-start | bytes 7077892
  (57 other events, 164.5 us)
Sparse Core Ops, SparseCore 0:
  10.0 77.3 all-gather.2
  89.2 57.0 all-gather.4

commit v3 on v2

--- a/solution.py
+++ b/solution.py
@@ -519,6 +519,115 @@
             copy.wait_send()
 
 
+class Line:
+    def __init__(self, kind, shard, line, ssem, rsem, lsem):
+        self.kind, self.shard, self.line = kind, shard, line
+        self.ssem, self.rsem, self.lsem = ssem, rsem, lsem
+        self.d, self.s, self.c = place()
+
+    def block(self, d):
+        if self.kind == "cols":
+            return self.line.at[:, pl.ds(pl.multiple_of(768 * d, 768), 768)]
+        return self.line.at[pl.ds(pl.multiple_of(192 * d, 192), 192)]
+
+    def copy(self, index, src, source, target):
+        return push(
+            src, self.block(source), self.ssem.at[index], self.rsem.at[index], at(target, self.s, self.c)
+        )
+
+    def start(self):
+        d = self.d
+        self.own = pltpu.make_async_copy(self.shard, self.block(d), self.lsem)
+        self.own.start()
+        self.sent = [
+            self.copy(0, self.shard, d, flip(d, 2)),
+            self.copy(1, self.shard, d, flip(d, 1)),
+        ]
+        for copy in self.sent:
+            copy.start()
+
+    def relay(self):
+        d2 = flip(self.d, 2)
+        self.copy(0, self.shard, d2, d2).wait_recv()
+        copy = self.copy(2, self.block(d2), d2, flip(self.d, 1))
+        copy.start()
+        self.sent.append(copy)
+
+    def finish(self):
+        d1 = flip(self.d, 1)
+        self.own.wait()
+        self.copy(1, self.shard, d1, d1).wait_recv()
+        self.copy(2, self.shard, flip(d1, 2), d1).wait_recv()
+        for copy in self.sent:
+            copy.wait_send()
+
+
+class Spread:
+    def __init__(self, kind, line, full, ssem, rsem, lsem):
+        self.kind, self.line, self.full = kind, line, full
+        self.ssem, self.rsem, self.lsem = ssem, rsem, lsem
+        self.d, self.s, self.c = place()
+        self.sx, self.sy = flip(self.s, 1), flip(self.s, 2)
+        self.sd = flip(self.sx, 2)
+        self.mate = at(self.d, self.s, 1 - self.c)
+        self.to_x, self.to_y = at(self.d, self.sx, self.c), at(self.d, self.sy, self.c)
+        self.sent = []
+
+    def block(self, position, c, h=None):
+        f = 2 * position + c
+        if self.kind == "cols":
+            rows = pl.ds(pl.multiple_of(96 * f, 96), 96)
+            return self.full.at[rows] if h is None else self.full.at[rows, pl.ds(1536 * h, 1536)]
+        columns = pl.ds(pl.multiple_of(384 * f, 384), 384)
+        rows = pl.ds(0, 768) if h is None else pl.ds(384 * h, 384)
+        return self.full.at[rows, columns]
+
+    def go(self, index, ref, device, src=None):
+        copy = push(
+            ref if src is None else src, ref, self.ssem.at[index], self.rsem.at[index], device
+        )
+        copy.start()
+        self.sent.append(copy)
+
+    def arrived(self, index, ref):
+        push(ref, ref, self.ssem.at[index], self.rsem.at[index], self.mate).wait_recv()
+
+    def start(self):
+        mine = self.block(self.s, self.c)
+        self.own = pltpu.make_async_copy(self.line, mine, self.lsem)
+        self.own.start()
+        self.go(0, mine, self.to_x, self.line)
+        self.go(1, mine, self.to_y, self.line)
+        self.go(2, mine, self.mate, self.line)
+
+    def relay(self):
+        c = self.c
+        from_x, from_y = self.block(self.sx, c), self.block(self.sy, c)
+        self.arrived(0, from_x)
+        self.go(3, self.block(self.sx, c, 0), self.to_y)
+        self.go(5, from_x, self.mate)
+        self.arrived(1, from_y)
+        self.go(4, self.block(self.sy, c, 1), self.to_x)
+        self.go(6, from_y, self.mate)
+
+    def corner(self):
+        for h in range(2):
+            ref = self.block(self.sd, self.c, h)
+            self.arrived(3 + h, ref)
+            self.go(7 + h, ref, self.mate)
+
+    def finish(self):
+        c = 1 - self.c
+        self.own.wait()
+        self.arrived(2, self.block(self.s, c))
+        self.arrived(5, self.block(self.sx, c))
+        self.arrived(6, self.block(self.sy, c))
+        for h in range(2):
+            self.arrived(7 + h, self.block(self.sd, c, h))
+        for copy in self.sent:
+            copy.wait_send()
+
+
 def everyone_else():
     me = lax.axis_index("dp") * 8 + lax.axis_index("fsdp")
 
@@ -530,8 +639,10 @@
 
 
 def open_kernel(
-    shard, router, act_ref, ada_ref, full, routers, seen, rows_out,
+    shard, router, act_ref, ada_ref, up_shard, down_shard,
+    full, routers, seen, rows_out, up_line, down_line,
     heard, part, got, mixed, ssem, rsem, lsem, asem, brsem, rssem, rrsem, tssem, trsem, zssem, zrsem,
+    us, ur, ds, dr,
 ):
     me, other = everyone_else()
     d, s, c = place()
@@ -559,6 +670,12 @@
     lax.fori_loop(1, 32, send, 0)
     gather = Gather("cols", shard, full, ssem, rsem, lsem.at[0])
     gather.start()
+    lines = (
+        Line("cols", up_shard, up_line, us, ur, lsem.at[3]),
+        Line("rows", down_shard, down_line, ds, dr, lsem.at[4]),
+    )
+    for line in lines:
+        line.start()
     own_router = pltpu.make_async_copy(router, routers.at[me], lsem.at[1])
     own_router.start()
 
@@ -617,7 +734,11 @@
         gather.relay(k)
     for k in range(1, 4):
         gather.corner(k)
+    for line in lines:
+        line.relay()
     gather.finish()
+    for line in lines:
+        line.finish()
     own_router.wait()
     own_rows.wait()
     for k in range(1, 4):
@@ -645,7 +766,7 @@
 ONCHIP = pl.BlockSpec(memory_space=pltpu.VMEM)
 
 
-def opening(shard, router, act, ada):
+def opening(shard, router, act, ada, up_shard, down_shard):
     return pl.pallas_call(
         open_kernel,
         out_shape=(
@@ -653,21 +774,24 @@
             jax.ShapeDtypeStruct((32, 16, 128), jnp.bfloat16),
             jax.ShapeDtypeStruct((72, 128), jnp.float32),
             jax.ShapeDtypeStruct((4, 8, 1152), jnp.float32),
+            jax.ShapeDtypeStruct((96, 3072), jnp.bfloat16),
+            jax.ShapeDtypeStruct((768, 384), jnp.bfloat16),
         ),
-        in_specs=[ONCHIP] * 4,
-        out_specs=(ANYWHERE, ANYWHERE, ONCHIP, ANYWHERE),
+        in_specs=[ONCHIP] * 6,
+        out_specs=(ANYWHERE, ANYWHERE, ONCHIP, ANYWHERE, ANYWHERE, ANYWHERE),
         scratch_shapes=[
             pltpu.VMEM((32, 8, 128), jnp.float32),
             pltpu.VMEM((8, 8, 1152), jnp.float32),
             pltpu.VMEM((8, 8, 1152), jnp.float32),
             pltpu.VMEM((8, 1152), jnp.float32),
-            DMA((GATHER_SEMS,)), DMA((GATHER_SEMS,)), DMA((3,)),
+            DMA((GATHER_SEMS,)), DMA((GATHER_SEMS,)), DMA((5,)),
             DMA((32,)), DMA((32,)), DMA((32,)), DMA((32,)),
             DMA((8,)), DMA((8,)), DMA((4,)), DMA((4,)),
+            DMA((3,)), DMA((3,)), DMA((3,)), DMA((3,)),
         ],
         compiler_params=pltpu.CompilerParams(collective_id=0, has_side_effects=True),
         name="opening",
-    )(shard, router, act, ada)
+    )(shard, router, act, ada, up_shard, down_shard)
 
 
 def group_of(d, s, c):
@@ -748,39 +872,32 @@
 
 
 def out_kernel(
-    rows, grads, up_shard, down_shard, tokens, d_tokens,
+    rows, grads, up_line, down_line, tokens, d_tokens,
     rows_in, grads_in, mixed_out, d_tokens_out, up_grad, down_grad,
-    up_full, down_full, s1, r1, s2, r2, ssem, rsem, ssem2, rsem2, lsem,
+    up_full, down_full, tokens_t, d_tokens_t, s1, r1, s2, r2, ssem, rsem, ssem2, rsem2, lsem,
 ):
     d, s, c = place()
     greet([device for _, device in group_of(d, s, c)] + [at(d, flip(s, 1), c), at(d, flip(s, 2), c)])
-    first = Gather("cols", up_shard, up_full, ssem, rsem, lsem.at[0])
-    second = Gather("rows", down_shard, down_full, ssem2, rsem2, lsem.at[1])
+    both = (
+        Spread("cols", up_line, up_full, ssem, rsem, lsem.at[0]),
+        Spread("rows", down_line, down_full, ssem2, rsem2, lsem.at[1]),
+    )
     swap_a = Swap(rows, rows_in, s1, r1, lsem.at[2])
     swap_b = Swap(grads, grads_in, s2, r2, lsem.at[3])
-    both = (first, second)
     for g in both:
         g.start()
     swap_a.start()
     swap_b.start()
+    tokens_t[...] = tokens[...].T
+    d_tokens_t[...] = d_tokens[...].T
+    mixed_out[...] = jnp.zeros_like(mixed_out)
+    d_tokens_out[...] = jnp.zeros_like(d_tokens_out)
     for g in both:
-        g.relay(0)
-    for k in range(1, 4):
-        for g in both:
-            g.spread_z(k)
+        g.relay()
     for g in both:
-        g.corner(0)
-    for k in range(1, 4):
-        for g in both:
-            g.relay(k)
-    for k in range(1, 4):
-        for g in both:
-            g.corner(k)
+        g.corner()
     for g in both:
         g.finish()
-
-    mixed_out[...] = jnp.zeros_like(mixed_out)
-    d_tokens_out[...] = jnp.zeros_like(d_tokens_out)
 
     def block(b, carry):
         where = pl.ds(pl.multiple_of(b * HIDDEN, HIDDEN), HIDDEN)
@@ -788,10 +905,10 @@
         act, slope = gelu_pair(nn(tokens[...], up))
         act = act.astype(jnp.bfloat16)
         mixed_out[...] += nt(act, down)
-        down_grad[:, where] = tn(d_tokens[...], act).astype(jnp.bfloat16)
+        down_grad[:, where] = nn(d_tokens_t[...], act).astype(jnp.bfloat16)
         d_pre = (slope * nn(d_tokens[...], down)).astype(jnp.bfloat16)
         d_tokens_out[...] += nt(d_pre, up)
-        up_grad[:, where] = tn(tokens[...], d_pre).astype(jnp.bfloat16)
+        up_grad[:, where] = nn(tokens_t[...], d_pre).astype(jnp.bfloat16)
         return carry
 
     lax.fori_loop(0, 3072 // HIDDEN, block, 0)
@@ -799,7 +916,7 @@
     swap_b.finish()
 
 
-def outbound(rows, grads, up_shard, down_shard, tokens, d_tokens):
+def outbound(rows, grads, up_line, down_line, tokens, d_tokens):
     bf, f32 = jnp.bfloat16, jnp.float32
     return pl.pallas_call(
         out_kernel,
@@ -814,85 +931,53 @@
         in_specs=[ONCHIP] * 6,
         out_specs=(ANYWHERE,) * 2 + (ONCHIP,) * 4,
         scratch_shapes=[pltpu.VMEM((768, 3072), bf)] * 2
+        + [pltpu.VMEM((768, 512), bf)] * 2
         + [DMA((8,))] * 4
-        + [DMA((GATHER_SEMS,))] * 4
+        + [DMA((9,))] * 4
         + [DMA((4,))],
         compiler_params=pltpu.CompilerParams(
             collective_id=1, has_side_effects=True, vmem_limit_bytes=60 << 20
         ),
         name="outbound",
-    )(rows, grads, up_shard, down_shard, tokens, d_tokens)
+    )(rows, grads, up_line, down_line, tokens, d_tokens)
 
 
 def widened(ref):
     return ref[...].astype(jnp.float32)
 
 
-class ExpertSum:
-    def __init__(self, grad, out, near, far, last, outgoing, ssem, rsem):
-        self.grad, self.out, self.near = grad, out, near
-        self.far, self.last, self.outgoing = far, last, outgoing
-        self.ssem, self.rsem = ssem, rsem
-        self.d, self.s, self.c = place()
-        self.sx, self.sy = flip(self.s, 1), flip(self.s, 2)
-        self.sd = flip(self.sx, 2)
-        self.rows = grad.shape[0] // 8
-
-    def part(self, position, h):
-        return self.grad.at[pl.ds(pl.multiple_of((2 * position + h) * self.rows, 32), self.rows)]
-
-    def copy(self, index, src, dst, position):
-        copy = push(src, dst, self.ssem.at[index], self.rsem.at[index], at(self.d, position, self.c))
-        copy.start()
-        return copy
-
-    def send_corner(self):
-        self.one = [
-            self.copy(0, self.part(self.sd, 0), self.near.at[0], self.sx),
-            self.copy(1, self.part(self.sd, 1), self.near.at[1], self.sy),
+class Parts:
+    def __init__(self, grad, keep, send_x, send_y, sem):
+        s = lax.axis_index("fsdp") // 2
+        sx, sy = flip(s, 1), flip(s, 2)
+        sd = flip(sx, 2)
+        rows = grad.shape[0] // 8
+        slots = (
+            (s, 0, keep.at[0, 0]), (sy, 0, keep.at[0, 1]), (s, 1, keep.at[1, 0]), (sx, 1, keep.at[1, 1]),
+            (sx, 0, send_x.at[0]), (sd, 0, send_x.at[1]), (sy, 1, send_y.at[0]), (sd, 1, send_y.at[1]),
+        )
+        self.copies = [
+            pltpu.make_async_copy(
+                grad.at[pl.ds(pl.multiple_of((2 * position + h) * rows, 32), rows)], out, sem.at[i]
+            )
+            for i, (position, h, out) in enumerate(slots)
         ]
 
-    def send_y(self):
-        self.two_y = self.copy(3, self.part(self.sy, 1), self.far.at[1], self.sy)
-
-    def send_x(self):
-        self.two_x = self.copy(2, self.part(self.sx, 0), self.far.at[0], self.sx)
-
-    def join_y(self):
-        self.one[0].wait_recv()
-        self.outgoing[0] = (widened(self.part(self.sy, 0)) + widened(self.near.at[0])).astype(jnp.bfloat16)
-        self.three_y = self.copy(4, self.outgoing.at[0], self.far.at[2], self.sy)
-
-    def join_x(self):
-        self.one[1].wait_recv()
-        self.outgoing[1] = (widened(self.part(self.sx, 1)) + widened(self.near.at[1])).astype(jnp.bfloat16)
-        self.three_x = self.copy(5, self.outgoing.at[1], self.far.at[3], self.sx)
-
-    def close(self):
-        d, s, c = self.d, self.s, self.c
-        for copy in (self.two_x, self.two_y, self.three_x, self.three_y):
-            copy.wait_recv()
-        mine, theirs = c, 1 - c
-        self.outgoing[2] = (
-            widened(self.part(s, theirs)) + widened(self.far.at[theirs]) + widened(self.far.at[2 + theirs])
-        ).astype(jnp.bfloat16)
-        self.four = push(
-            self.outgoing.at[2], self.last, self.ssem.at[6], self.rsem.at[6], at(d, s, 1 - c)
-        )
-        self.four.start()
-        self.out[c] = widened(self.part(s, mine)) + widened(self.far.at[mine]) + widened(self.far.at[2 + mine])
+    def start(self):
+        for copy in self.copies:
+            copy.start()
 
     def finish(self):
-        self.four.wait_recv()
-        self.out[1 - self.c] = widened(self.last)
-        for copy in self.one + [self.two_x, self.two_y, self.three_x, self.three_y, self.four]:
-            copy.wait_send()
+        for copy in self.copies:
+            copy.wait()
 
 
 def expert_kernel(
-    rows, grads, up_all, down_all, rows_back, grads_back, up_out, down_out,
-    up, down, act, d_pre, made, d_made, total, d_total, up_grad, down_grad,
-    un, uf, ul, ug, dn, df, dl, dg, s1, r1, s2, r2, s3, r3, s4, r4, lsem, wsem,
+    rows, grads, up_all, down_all, first_grad, second_grad,
+    rows_back, grads_back, up_keep, up_x, up_y, down_keep, down_x, down_y, first_part, second_part,
+    up, down, act, d_pre, made, d_made, total, d_total, up_grad, down_grad, rows_t,
+    fo, fm, fn, ff, fs, fr, fl, so, sm, sn, sf, ss, sr, sl,
+    s1, r1, s2, r2, lsem, wsem, psem, qsem,
 ):
     bf = jnp.bfloat16
     d, s, c = place()
@@ -903,6 +988,12 @@
     for copy in weights:
         copy.start()
     greet([device for _, device in group_of(d, s, c)] + [at(d, flip(s, 1), c), at(d, flip(s, 2), c)])
+    sums = (
+        DenseSum("cols", first_grad, first_part, fo, fm, fn, ff, None, fs, fr, fl),
+        DenseSum("rows", second_grad, second_part, so, sm, sn, sf, None, ss, sr, sl),
+    )
+    for each in sums:
+        each.start()
     swap_a = Swap(made, rows_back, s1, r1, lsem.at[0])
     swap_b = Swap(d_made, grads_back, s2, r2, lsem.at[1])
     for copy in weights:
@@ -933,76 +1024,74 @@
         d_made[chunk] = d_total[...].astype(bf).reshape(2, 144, 768)
         swap_a.send(step)
         swap_b.send(step)
-    first = ExpertSum(up_grad, up_out, un, uf, ul, ug, s3, r3)
-    second = ExpertSum(down_grad, down_out, dn, df, dl, dg, s4, r4)
-    x_all = rows.reshape(1152, 768)
+        if step == 2:
+            for each in sums:
+                each.merge()
+        if step == 3:
+            for each in sums:
+                each.join()
+    rows_t[...] = rows.reshape(1152, 768)[...].T
     g_all = grads.reshape(1152, 768)
-    y = s // 2
-
-    def up_rows(side):
-        here = pl.ds(pl.multiple_of(384 * side, 384), 384)
-        x_part = x_all[:, here]
-
-        def block(b, carry):
-            where = pl.ds(pl.multiple_of(b * HIDDEN, HIDDEN), HIDDEN)
-            up_grad[here, where] = tn(x_part, d_pre[:, where]).astype(bf)
-            return carry
-
-        lax.fori_loop(0, 3072 // HIDDEN, block, 0)
-
-    def down_rows(position):
-        def block(b, carry):
-            where = pl.ds(pl.multiple_of(768 * position + 384 * b, 384), 384)
-            down_grad[where] = tn(act[:, where], g_all[...]).astype(bf)
-            return carry
-
-        lax.fori_loop(0, 2, block, 0)
-
-    up_rows(1 - y)
-    first.send_corner()
-    first.send_y()
-    down_rows(second.sd)
-    second.send_corner()
-    first.join_y()
-    down_rows(second.sy)
-    second.send_y()
-    second.join_y()
-    up_rows(y)
-    first.send_x()
-    first.join_x()
-    down_rows(second.sx)
-    second.send_x()
-    second.join_x()
-    down_rows(s)
-    first.close()
-    second.close()
-    first.finish()
-    second.finish()
+
+    def up_block(b, carry):
+        where = pl.ds(pl.multiple_of(b * HIDDEN, HIDDEN), HIDDEN)
+        up_grad[:, where] = nn(rows_t[...], d_pre[:, where]).astype(bf)
+        return carry
+
+    def down_block(b, carry):
+        where = pl.ds(pl.multiple_of(384 * b, 384), 384)
+        down_grad[where] = tn(act[:, where], g_all[...]).astype(bf)
+        return carry
+
+    up_parts = Parts(up_grad, up_keep, up_x, up_y, psem)
+    down_parts = Parts(down_grad, down_keep, down_x, down_y, qsem)
+    lax.fori_loop(0, 3072 // HIDDEN, up_block, 0)
+    up_parts.start()
+    lax.fori_loop(0, 8, down_block, 0)
+    down_parts.start()
+    for each in sums:
+        each.close()
     swap_a.finish()
     swap_b.finish()
-
-
-def experts(rows, grads, up_all, down_all):
+    up_parts.finish()
+    down_parts.finish()
+
+
+def experts(rows, grads, up_all, down_all, first_grad, second_grad):
     bf, f32 = jnp.bfloat16, jnp.float32
 
-    def rooms(r, n):
+    def rooms(piece, half):
         return [
-            pltpu.VMEM((2, r, n), bf),
-            pltpu.VMEM((4, r, n), bf),
-            pltpu.VMEM((r, n), bf),
-            pltpu.VMEM((3, r, n), bf),
+            pltpu.VMEM((4,) + piece, bf),
+            pltpu.VMEM((4,) + piece, bf),
+            pltpu.VMEM((2,) + half, bf),
+            pltpu.VMEM((2,) + piece, bf),
+            DMA((8,)),
+            DMA((8,)),
+            DMA((4,)),
         ]
+
+    def parts(r, n):
+        return (
+            jax.ShapeDtypeStruct((2, 2, r, n), bf),
+            jax.ShapeDtypeStruct((2, r, n), bf),
+            jax.ShapeDtypeStruct((2, r, n), bf),
+        )
 
     return pl.pallas_call(
         expert_kernel,
         out_shape=(
             jax.ShapeDtypeStruct((8, 144, 768), bf),
             jax.ShapeDtypeStruct((8, 144, 768), bf),
-            jax.ShapeDtypeStruct((2, 96, 3072), f32),
-            jax.ShapeDtypeStruct((2, 384, 768), f32),
+        )
+        + parts(96, 3072)
+        + parts(384, 768)
+        + (
+            jax.ShapeDtypeStruct((96, 3072), bf),
+            jax.ShapeDtypeStruct((768, 384), bf),
         ),
-        in_specs=[ONCHIP, ONCHIP, ANYWHERE, ANYWHERE],
-        out_specs=(ANYWHERE, ANYWHERE, ONCHIP, ONCHIP),
+        in_specs=[ONCHIP, ONCHIP, ANYWHERE, ANYWHERE, ANYWHERE, ANYWHERE],
+        out_specs=(ANYWHERE,) * 8 + (ONCHIP, ONCHIP),
         scratch_shapes=[
             pltpu.VMEM((768, 3072), bf),
             pltpu.VMEM((3072, 768), bf),
@@ -1014,16 +1103,43 @@
             pltpu.VMEM((288, 768), f32),
             pltpu.VMEM((768, 3072), bf),
             pltpu.VMEM((3072, 768), bf),
+            pltpu.VMEM((768, 1152), bf),
         ]
-        + rooms(96, 3072)
-        + rooms(384, 768)
-        + [DMA((8,))] * 8
-        + [DMA((2,)), DMA((2,))],
+        + rooms((96, 3072), (96, 1536))
+        + rooms((768, 384), (384, 384))
+        + [DMA((8,))] * 4
+        + [DMA((2,)), DMA((2,)), DMA((8,)), DMA((8,))],
         compiler_params=pltpu.CompilerParams(
             collective_id=2, has_side_effects=True, vmem_limit_bytes=67043328
         ),
         name="experts",
-    )(rows, grads, up_all, down_all)
+    )(rows, grads, up_all, down_all, first_grad, second_grad)
+
+
+def hop(values, bit):
+    return lax.ppermute(values, "fsdp", [(f, f ^ bit) for f in range(8)])
+
+
+def square_sum(keep, send_x, send_y):
+    f32, bf = jnp.float32, jnp.bfloat16
+    from_x, from_y = hop(send_x, 2), hop(send_y, 4)
+    low_next = hop((keep[0, 1].astype(f32) + from_x[1].astype(f32)).astype(bf), 4)
+    high_next = hop((keep[1, 1].astype(f32) + from_y[1].astype(f32)).astype(bf), 2)
+    low = keep[0, 0].astype(f32) + from_x[0].astype(f32) + low_next.astype(f32)
+    high = keep[1, 0].astype(f32) + from_y[0].astype(f32) + high_next.astype(f32)
+    first = lax.rem(lax.axis_index("fsdp"), 2) == 0
+    other = hop(jnp.where(first, high, low).astype(bf), 1).astype(f32)
+    return jnp.where(first, jnp.stack([low, other]), jnp.stack([other, high]))
+
+
+def line_sum(part, axis):
+    d, size = lax.axis_index("dp"), part.shape[axis] // 4
+    total = lax.dynamic_slice_in_dim(part, size * d, size, axis).astype(jnp.float32)
+    for k in range(1, 4):
+        block = lax.dynamic_slice_in_dim(part, size * lax.rem(d + k, 4), size, axis)
+        got = lax.ppermute(block, "dp", [(i, (i + k) % 4) for i in range(4)])
+        total = total + got.astype(jnp.float32)
+    return total
 
 
 class DenseSum:
@@ -1099,13 +1215,16 @@
             copy.start()
             self.two.append(copy)
 
+    def square(self):
+        for copy in self.two:
+            copy.wait_recv()
+        return (
+            widened(self.own.at[3]) + widened(self.far.at[0]) + widened(self.far.at[1])
+        ).astype(jnp.bfloat16)
+
     def along(self):
         d, s, c = self.d, self.s, self.c
-        for copy in self.two:
-            copy.wait_recv()
-        self.own[3] = (
-            widened(self.own.at[3]) + widened(self.far.at[0]) + widened(self.far.at[1])
-        ).astype(jnp.bfloat16)
+        self.own[3] = self.square()
         self.three = []
         for k in range(1, 4):
             target = lax.rem(d + k, 4)
@@ -1122,7 +1241,14 @@
             self.three[k - 1].wait_recv()
             total = total + widened(self.line.at[k - 1])
         self.out[...] = total
-        for copy in self.zero + self.one + self.two + self.three:
+        self.sent(self.three)
+
+    def close(self):
+        self.out[...] = self.square()
+        self.sent([])
+
+    def sent(self, more):
+        for copy in self.zero + self.one + self.two + more:
             copy.wait_send()
 
 
@@ -1316,7 +1442,6 @@
     model_width = tokens.shape[1]
     head_size = model_width // HEADS
     inside, segment = owners(image_sizes)
-    up_all, down_all = gather_experts(expert_up, expert_down)
     ids = jnp.arange(EXPERTS, dtype=jnp.int32)
     hot = routes[:, :, None] == ids[None, None, :]
     hot_any = jnp.any(hot, axis=1).astype(bf)
@@ -1338,7 +1463,11 @@
     ada_pad = jnp.pad(ada_weight, ((0, 32), (0, 0)))
     router_pack = jnp.pad(router_weight.reshape(192), (0, 2048 - 192)).reshape(16, 128)
     qkvo_shard = jnp.concatenate([qkv_weight, out_weight], axis=1)
-    qkvo, routers, seen, mod_rows = opening(qkvo_shard, router_pack, act_slices, ada_pad)
+    qkvo, routers, seen, mod_rows, up_line, down_line = opening(
+        qkvo_shard, router_pack, act_slices, ada_pad, shared_up, shared_down.T
+    )
+    expert_up, expert_down, seen = lax.optimization_barrier((expert_up, expert_down, seen))
+    up_all, down_all = gather_experts(expert_up, expert_down)
     expert_counts = seen[66, :EXPERTS].astype(jnp.int32)
     modulation = lax.dynamic_slice(mod_rows, (0, 2 * d_index, 0), (4, 2, 1152))
     modulation = modulation.transpose(1, 0, 2).reshape(2, 4608)
@@ -1394,11 +1523,13 @@
         .reshape(EXPERTS, CAP, model_width)
     )
     rows_in, grads_in, shared_out, d_second, shared_first_grad, shared_second_grad = outbound(
-        rows, grads, shared_up, shared_down.T, second_input, d_mixed.astype(bf)
-    )
-    returned, d_returned, expert_up_grad, expert_down_grad = experts(
-        rows_in, grads_in, up_all, down_all
-    )
+        rows, grads, up_line, down_line, second_input, d_mixed.astype(bf)
+    )
+    returned, d_returned, *parts, first_part, second_part = experts(
+        rows_in, grads_in, up_all, down_all, shared_first_grad, shared_second_grad
+    )
+    expert_up_grad, expert_down_grad = square_sum(*parts[:3]), square_sum(*parts[3:])
+    shared_first_sum, shared_second_sum = line_sum(first_part, 1), line_sum(second_part, 0)
     returned = returned.reshape(EXPERTS * CAP, model_width)
     d_returned = d_returned.reshape(EXPERTS * CAP, model_width)
     picked_0 = tn(send_0, returned)
@@ -1461,9 +1592,9 @@
     router_tiles = jnp.pad(
         router_grad.reshape(EXPERTS, 8, 96).transpose(1, 0, 2), ((0, 0), (0, 0), (0, 32))
     )
-    shared_first_sum, shared_second_sum, qkvo_sum, ada_grad, d_act_tiles, router_sum = dense_sums(
-        ("cols", "rows", "cols"),
-        (shared_first_grad, shared_second_grad, qkvo_grad),
+    qkvo_sum, ada_grad, d_act_tiles, router_sum = dense_sums(
+        ("cols",),
+        (qkvo_grad,),
         (d_mod_rows, router_tiles, seen[:64].astype(bf), ada_weight),
         3,
     )

time: 579 us -> 559 us (0.965)
  Pallas kernels: 389 us -> 294 us
  waiting for transfers between devices: 1.38 us -> 32.5 us
  starting transfers between devices: 0.08 us -> 30.2 us
  other arithmetic: 31.2 us -> 46.6 us
    pallas_call x1, Pallas kernels: 140 us -> 92.7 us  [experts(): pl.pallas_call(expert_kernel, out_shape=(jax.ShapeDtypeStruct((8, 144, 76...]
    pallas_call x1, Pallas kernels: 86.6 us -> 48.5 us  [dense_sums(): pl.pallas_call(functools.partial(dense_kernel, kinds), out_shape=tuple(ou...]
    ppermute x0 -> x16, waiting for transfers between devices: none -> 31.7 us  [the longest x10 31.7 us: hop(): return lax.ppermute(values, 'fsdp', [(f, f ^ bit) for f in range(8)])]
    ppermute x0 -> x16, starting transfers between devices: none -> 30.1 us  [the longest x6 20.2 us: line_sum(): got = lax.ppermute(block, 'dp', [(i, (i + k) % 4) for i in range(4)])]
    pallas_call x1, Pallas kernels: 105 us -> 98.4 us  [outbound(): pl.pallas_call(out_kernel, out_shape=(jax.ShapeDtypeStruct((8, 144, 768),...]
    unnamed x164 -> x152, local copies, waits for them, and re-layouts: 13.8 us -> 9.69 us
  transfers between devices with their start and end apart: 2 -> 18, of which waited for: 0 -> 4; matrix products, arithmetic and copies ran while one was open for 12% -> 15% of each run, Pallas kernels for 28% -> 18%
where the time goes in v3:
time: 559 us; the launch traced here: 552 us
  Pallas kernels  294 us (53%)
  matrix products  74.3 us (13%)
  local copies, waits for them, and re-layouts  58.7 us (11%)
  other arithmetic  46.6 us (8%)
  waiting for transfers between devices  32.5 us (6%)
  starting transfers between devices  30.2 us (5%)
  between operations  15.7 us (3%)
    pallas_call x1, Pallas kernels, outbound(): pl.pallas_call(out_kernel, out_shape=(jax.ShapeDtypeStruct((8, 144, 768),...  98.4 us
    pallas_call x1, Pallas kernels, experts(): pl.pallas_call(expert_kernel, out_shape=(jax.ShapeDtypeStruct((8, 144, 76...  92.7 us
    pallas_call x1, Pallas kernels, opening(): pl.pallas_call(open_kernel, out_shape=(jax.ShapeDtypeStruct((768, 3072),...  54.2 us
    pallas_call x1, Pallas kernels, dense_sums(): pl.pallas_call(functools.partial(dense_kernel, kinds), out_shape=tuple(ou...  48.5 us
    ppermute x10, waiting for transfers between devices, hop(): return lax.ppermute(values, 'fsdp', [(f, f ^ bit) for f in range(8)])  31.7 us
    ppermute x6, starting transfers between devices, line_sum(): got = lax.ppermute(block, 'dp', [(i, (i + k) % 4) for i in range(4)])  20.2 us
    dot_general x6, matrix products, tn(): lax.dot_general(left, right, (((0,), (0,)), ((), ())), preferred_element_...  17.2 us
    dot_general x1, matrix products, fitted_shards(): jnp.einsum('hqd,hkd->hqk', d_attended, values, preferred_element_type=jnp...  12 us
  transfers between devices with their start and end apart: 18, of which 4 were waited for; matrix products, arithmetic and copies ran while one was open for 15% of the time, Pallas kernels for 18%

profile of v3, /device:TPU:0, one launch (start us, length us, event | category | flops | bytes accessed | tf_op | source)
XLA Modules:
  0.0 551.9 jit_solution(2052861367568890775)
XLA Ops:
  16.3 54.2 %opening.1 = (bf16[768,3072]{1,0:T(8,128)(2,1)}, bf16[32,16,128]{2,1,0:T(8,128)(2,1)}, f32[72,128]{1,0:T(8,128)}, f32[4,8,1152]{2,1,0:T(8,128)}, bf16[96,3072]{1,0:T(8,128)(2,1)}, /*index=5*/bf16[768,384]{1,0:T(8,128)(2,1)}) custom-call(bf16[96,768]{1,0:T(8,128)(2,1)} %pad_maximum_fusion.4.shard, bf16[16,128]{1,0:T(8,128)(2,1)} %pad_bitcast_fusion.router, ...), custom_call_target="tpu_custom_call" | custom-call | tf_op jit(solution)/shard_map/opening/pallas_call | solution.py:770
  71.3 6.9 %copy.91 = bf16[768,3072]{0,1:T(8,128)(2,1)} copy(bf16[768,3072]{1,0:T(8,128)(2,1)} %get-tuple-element.54) | data formatting | bytes 9437184 | tf_op jit(solution)/shard_map/reshape | solution.py:1480
  78.1 4.1 slice.183
  103.2 10.9 %fusion.95 = (f32[12,512]{1,0:T(8,128)}, f32[12,512,512]{1,2,0:T(8,128)}) fusion(pred[512,512]{0,1:T(8,128)(4,1)} %broadcast_compare_fusion, bf16[12,512,64]{1,2,0:T(8,128)(2,1)} %bitcast.223, bf16[12,512,64]{1,2,0:T(8,128)(2,1)S(1)} %bitcast.212), kind=kOutput, calls=%fused_computation.214 | convolution fusion | flops 415236608 | bytes 14442496 | tf_op jit(solution)/shard_map/sub | solution.py:1500
  114.1 5.8 %fusion.33 = bf16[12,512,64]{1,2,0:T(8,128)(2,1)S(1)} fusion(bf16[12,512,64]{1,2,0:T(8,128)(2,1)S(1)} %bitcast.226, f32[12,512,512]{1,2,0:T(8,128)} %get-tuple-element.147, f32[12,512]{1,0:T(8,128)} %get-tuple-element.146), kind=kOutput, calls=%fused_computation.85 | convolution fusion | flops 409337856 | bytes 14180352 | tf_op jit(solution)/shard_map/hqk,hkd->hqd/dot_general | solution.py:1504
  120.0 3.7 fusion.90
  137.2 98.4 %outbound.1 = (bf16[8,144,768]{2,1,0:T(8,128)(2,1)}, bf16[8,144,768]{2,1,0:T(8,128)(2,1)}, f32[512,768]{1,0:T(8,128)}, f32[512,768]{1,0:T(8,128)}, bf16[768,3072]{1,0:T(8,128)(2,1)}, /*index=5*/bf16[768,3072]{1,0:T(8,128)(2,1)}) custom-call(bf16[8,144,768]{2,1,0:T(8,128)(2,1)} %bitcast.221, bf16[8,144,768]{2,1,0:T(8,128)(2,1)} %bitcast.222, ...), custom_call_target="tpu_custom_call" | custom-call | tf_op jit(solution)/shard_map/outbound/pallas_call | solution.py:921
  236.9 92.7 %experts.1 = (bf16[8,144,768]{2,1,0:T(8,128)(2,1)}, bf16[8,144,768]{2,1,0:T(8,128)(2,1)}, bf16[2,2,96,3072]{3,2,1,0:T(8,128)(2,1)}, bf16[2,96,3072]{2,1,0:T(8,12...) custom-call(bf16[8,144,768]{2,1,0:T(8,128)(2,1)} %get-tuple-element., ...), custom_call_target="tpu_custom_call" | custom-call | tf_op jit(solution)/shard_map/experts/pallas_call | solution.py:1081
  332.8 4.6 multiply_reduce_fusion.2
  346.0 12.0 %multiply_reduce_fusion = (f32[12,512]{1,0:T(8,128)S(1)}, f32[12,512,512]{1,2,0:T(8,128)}) fusion(f32[12,512,512]{1,2,0:T(8,128)} %get-tuple-element.147, f32[12,512]{1,0:T(8,128)S(1)} %copy-done.46, bf16[12,512,64]{1,2,0:T(8,128)(2,1)} %bitcast.227, bf16[12,512,64]{1,2,0:T(8,128)(2,1)} %bitcast.225), kind=kOutput, calls=%fused_computation.2 | convolution fusion | flops 412084224 | bytes 26787840 | tf_op jit(solution)/shard_map/hqd,hkd->hqk/dot_general | solution.py:1556
  358.0 7.0 %multiply_convert_fusion = bf16[12,512,512]{1,2,0:T(8,128)(2,1)S(1)} fusion(f32[12,512,512]{1,2,0:T(8,128)} %get-tuple-element.151, f32[12,512]{1,0:T(8,128)S(1)} %get-tuple-element.150, f32[12,512,512]{1,2,0:T(8,128)S(1)} %bitcast.211, f32[12,512]{1,0:T(8,128)S(1)} %copy-done.46), kind=kLoop, calls=%fused_computation.1 | loop fusion | flops 12582912 | bytes 31506432 | tf_op jit(solution)/shard_map/convert_element_type | solution.py:1559
  370.0 4.1 fusion.36
  374.3 5.8 %convolution_convert_fusion = bf16[768,2304]{1,0:T(8,128)(2,1)} fusion(bf16[512,768]{1,0:T(8,128)(2,1)} %copy-done.24, bf16[512,768]{0,1:T(8,128)(2,1)} %bitcast.270, bf16[512,768]{0,1:T(8,128)(2,1)} %bitcast.268, bf16[512,768]{0,1:T(8,128)(2,1)} %bitcast.219), kind=kOutput, calls=%fused_computation.11 | convolution fusion | flops 1820786688 | bytes 6684672 | tf_op jit(solution)/shard_map/dot_general | solution.py:851
  380.1 5.1 fusion.88
  385.4 5.8 %copy.77 = bf16[768,2304]{0,1:T(8,128)(2,1)} copy(bf16[768,2304]{1,0:T(8,128)(2,1)} %convolution_convert_fusion) | data formatting | bytes 7077888 | tf_op jit(solution)/shard_map/convert.57
  395.7 4.4 pad_maximum_fusion
  400.1 6.7 %copy.90.refs_0_ = bf16[768,3072]{1,0:T(8,128)(2,1)} copy(bf16[768,3072]{0,1:T(8,128)(2,1)} %bitcast.208) | data formatting | bytes 9437184 | tf_op jit(solution)/shard_map/convert_element_type | solution.py:1578
  408.3 48.5 %dense_sums.1 = (f32[96,768]{1,0:T(8,128)}, f32[96,1152]{1,0:T(8,128)}, f32[8,8,128]{2,1,0:T(8,128)}, f32[8,128]{1,0:T(8,128)}) custom-call(bf16[768,3072]{1,0:T(8,128)(2,1)} %copy.90.refs_0_, f32[4,8,1152]{2,1,0:T(8,128)} %copy-done.25, f32[8,8,128]{2,1,0:T(8,128)} %pad.27.refs_2_, bf16[64,128]{1,0:T(8,128)(2,1)} %slice.250.refs_3_, bf16[96,1152]{1,0:T(8,128)(2,1)} %refs_4_.1), custom_call_target="tpu_custom_call" | custom-call | tf_op jit(solution)/shard_map/dense_sums/pallas_call | solution.py:1414
  471.6 3.7 fusion.27
  475.3 14.0 %collective-permute-done.11 = bf16[2,384,768]{2,1,0:T(8,128)(2,1)} collective-permute-done((bf16[2,384,768]{2,1,0:T(8,128)(2,1)}, bf16[2,384,768]{2,1,0:T(8,128)(2,1)}, u32[]{:S(2)}, u32[]{:S(2)}) %collective-permute-start.11) | collective-permute-done | bytes 1179680 | tf_op jit(solution)/shard_map/ppermute | solution.py:1120
  490.4 5.1 collective-permute-start.5
  497.2 12.7 %collective-permute-done.6 = bf16[2,96,3072]{2,1,0:T(8,128)(2,1)} collective-permute-done((bf16[2,96,3072]{2,1,0:T(8,128)(2,1)}, bf16[2,96,3072]{2,1,0:T(8,128)(2,1)}, u32[]{:S(2)}, u32[]{:S(2)}) %collective-permute-start.6) | collective-permute-done | bytes 1179680 | tf_op jit(solution)/shard_map/ppermute | solution.py:1120
  522.2 4.4 collective-permute-done.12
  529.8 5.8 %collective-permute-start.2 = (bf16[96,768]{1,0:T(8,128)(2,1)S(1)}, bf16[96,768]{1,0:T(8,128)(2,1)S(1)}, u32[]{:S(2)}, u32[]{:S(2)}) collective-permute-start(bf16[96,768]{1,0:T(8,128)(2,1)S(1)} %get-tuple-element.136), channel_id=1, source_target_pairs={{0,24},{8,0},{16,8},{24,16},{1,25},{9,1},{17,9},{25,17},{2,26},{10... | collective-permute-start | bytes 442376 | tf_op jit(solution)/shard_map/ppermute | solution.py:1140
  (306 shorter events, 109.6 us)
Async XLA Ops:
  7.2 229.7 %all-gather.3.cloned.1.call-start = ((), (), s32[]{:S(2)}) async-start(), calls=%async_computation | async-start | bytes 10616832 | tf_op jit(solution)/shard_map/all_gather | solution.py:94
  9.6 61.7 %copy-start.55 = (pred[512,8]{0,1:T(8,128)(4,1)}, pred[512,8]{0,1:T(8,128)(4,1)S(1)}, u32[]{:S(2)}) copy-start(pred[512,8]{0,1:T(8,128)(4,1)S(1)} %fusion.67) | copy-start | bytes 12292
  70.5 166.4 %all-gather.5.cloned.1.call-start = ((), (), s32[]{:S(2)}) async-start(), calls=%async_computation.1 | async-start | bytes 10616832 | tf_op jit(solution)/shard_map/all_gather | solution.py:95
  83.6 36.3 %copy-start.9 = (bf16[768,4,192]{0,2,1:T(8,128)(2,1)}, bf16[768,4,192]{0,2,1:T(8,128)(2,1)S(1)}, u32[]{:S(2)}) copy-start(bf16[768,4,192]{0,2,1:T(8,128)(2,1)S(1)} %slice.187) | copy-start | bytes 3538948
  100.9 26.5 %copy-start.34 = (bf16[768,8]{0,1:T(8,128)(2,1)}, bf16[768,8]{0,1:T(8,128)(2,1)S(1)}, u32[]{:S(2)}) copy-start(bf16[768,8]{0,1:T(8,128)(2,1)S(1)} %reshape.378) | copy-start | bytes 36868
  460.1 29.2 %collective-permute-start.11 = (bf16[2,384,768]{2,1,0:T(8,128)(2,1)}, bf16[2,384,768]{2,1,0:T(8,128)(2,1)}, u32[]{:S(2)}, u32[]{:S(2)}) collective-permute-start(bf16[2,384,768]{2,1,0:T(8,128)(2,1)} %get-tuple-element.80), channel_id=1, source_target_pairs={{0,2},{1,3},{2,0},{3,1},{4,6},{5,7},{6,4},{7,5},{8,10},{9,11},{10,... | collective-permute-start | bytes 3538952 | tf_op jit(solution)/shard_map/ppermute | solution.py:1120
  460.9 29.5 %collective-permute-start.13 = (bf16[2,384,768]{2,1,0:T(8,128)(2,1)}, bf16[2,384,768]{2,1,0:T(8,128)(2,1)}, u32[]{:S(2)}, u32[]{:S(2)}) collective-permute-start(bf16[2,384,768]{2,1,0:T(8,128)(2,1)} %get-tuple-element.81), channel_id=1, source_target_pairs={{0,4},{1,5},{2,6},{3,7},{4,0},{5,1},{6,2},{7,3},{8,12},{9,13},{10,... | collective-permute-start | bytes 3538952 | tf_op jit(solution)/shard_map/ppermute | solution.py:1120
  462.1 47.8 %collective-permute-start.6 = (bf16[2,96,3072]{2,1,0:T(8,128)(2,1)}, bf16[2,96,3072]{2,1,0:T(8,128)(2,1)}, u32[]{:S(2)}, u32[]{:S(2)}) collective-permute-start(bf16[2,96,3072]{2,1,0:T(8,128)(2,1)} %get-tuple-element.77), channel_id=1, source_target_pairs={{0,2},{1,3},{2,0},{3,1},{4,6},{5,7},{6,4},{7,5},{8,10},{9,11},{10,... | collective-permute-start | bytes 3538952 | tf_op jit(solution)/shard_map/ppermute | solution.py:1120
  462.8 50.2 %collective-permute-start.8 = (bf16[2,96,3072]{2,1,0:T(8,128)(2,1)}, bf16[2,96,3072]{2,1,0:T(8,128)(2,1)}, u32[]{:S(2)}, u32[]{:S(2)}) collective-permute-start(bf16[2,96,3072]{2,1,0:T(8,128)(2,1)} %get-tuple-element.78), channel_id=1, source_target_pairs={{0,4},{1,5},{2,6},{3,7},{4,0},{5,1},{6,2},{7,3},{8,12},{9,13},{10,... | collective-permute-start | bytes 3538952 | tf_op jit(solution)/shard_map/ppermute | solution.py:1120
  466.0 49.5 %collective-permute-start.3 = (bf16[192,384]{1,0:T(8,128)(2,1)}, bf16[192,384]{1,0:T(8,128)(2,1)S(1)}, u32[]{:S(2)}, u32[]{:S(2)}) collective-permute-start(bf16[192,384]{1,0:T(8,128)(2,1)} %get-tuple-element.132), channel_id=1, source_target_pairs={{0,8},{8,16},{16,24},{24,0},{1,9},{9,17},{17,25},{25,1},{2,10},{10... | collective-permute-start | bytes 442376 | tf_op jit(solution)/shard_map/ppermute | solution.py:1140
  471.6 18.8 %copy-start.31 = (bf16[192,384]{1,0:T(8,128)(2,1)S(1)}, bf16[192,384]{1,0:T(8,128)(2,1)}, u32[]{:S(2)}) copy-start(bf16[192,384]{1,0:T(8,128)(2,1)} %get-tuple-element.133) | copy-start | bytes 442372
  471.6 23.9 %copy-start.18 = (bf16[2,2,384,768]{3,2,1,0:T(8,128)(2,1)S(1)}, bf16[2,2,384,768]{3,2,1,0:T(8,128)(2,1)}, u32[]{:S(2)}) copy-start(bf16[2,2,384,768]{3,2,1,0:T(8,128)(2,1)} %get-tuple-element.79) | copy-start | bytes 7077892
  489.3 29.2 %collective-permute-start.4 = (bf16[192,384]{1,0:T(8,128)(2,1)S(1)}, bf16[192,384]{1,0:T(8,128)(2,1)S(1)}, u32[]{:S(2)}, u32[]{:S(2)}) collective-permute-start(bf16[192,384]{1,0:T(8,128)(2,1)S(1)} %copy-done.32), channel_id=1, source_target_pairs={{0,16},{8,24},{16,0},{24,8},{1,17},{9,25},{17,1},{25,9},{2,18},{10... | collective-permute-start | bytes 442376 | tf_op jit(solution)/shard_map/ppermute | solution.py:1140
  490.4 29.9 %collective-permute-start.5 = (bf16[192,384]{1,0:T(8,128)(2,1)S(1)}, bf16[192,384]{1,0:T(8,128)(2,1)S(1)}, u32[]{:S(2)}, u32[]{:S(2)}) collective-permute-start(bf16[192,384]{1,0:T(8,128)(2,1)S(1)} %copy-done.31), channel_id=1, source_target_pairs={{0,24},{8,0},{16,8},{24,16},{1,25},{9,1},{17,9},{25,17},{2,26},{10... | collective-permute-start | bytes 442376 | tf_op jit(solution)/shard_map/ppermute | solution.py:1140
  495.5 18.3 %copy-start.17 = (bf16[2,2,96,3072]{3,2,1,0:T(8,128)(2,1)S(1)}, bf16[2,2,96,3072]{3,2,1,0:T(8,128)(2,1)}, u32[]{:S(2)}) copy-start(bf16[2,2,96,3072]{3,2,1,0:T(8,128)(2,1)} %get-tuple-element.76) | copy-start | bytes 7077892
  509.9 16.7 %collective-permute-start.12 = (bf16[384,768]{1,0:T(8,128)(2,1)S(1)}, bf16[384,768]{1,0:T(8,128)(2,1)S(1)}, u32[]{:S(2)}, u32[]{:S(2)}) collective-permute-start(bf16[384,768]{1,0:T(8,128)(2,1)S(1)} %get-tuple-element.126), channel_id=1, source_target_pairs={{0,4},{1,5},{2,6},{3,7},{4,0},{5,1},{6,2},{7,3},{8,12},{9,13},{10,... | collective-permute-start | bytes 1769480 | tf_op jit(solution)/shard_map/ppermute | solution.py:1120
  513.0 16.7 %collective-permute-start.14 = (bf16[384,768]{1,0:T(8,128)(2,1)S(1)}, bf16[384,768]{1,0:T(8,128)(2,1)S(1)}, u32[]{:S(2)}, u32[]{:S(2)}) collective-permute-start(bf16[384,768]{1,0:T(8,128)(2,1)S(1)} %get-tuple-element.125), channel_id=1, source_target_pairs={{0,2},{1,3},{2,0},{3,1},{4,6},{5,7},{6,4},{7,5},{8,10},{9,11},{10,... | collective-permute-start | bytes 1769480 | tf_op jit(solution)/shard_map/ppermute | solution.py:1120
  515.5 24.2 %collective-permute-start = (bf16[96,768]{1,0:T(8,128)(2,1)S(1)}, bf16[96,768]{1,0:T(8,128)(2,1)S(1)}, u32[]{:S(2)}, u32[]{:S(2)}) collective-permute-start(bf16[96,768]{1,0:T(8,128)(2,1)S(1)} %copy-done.30), channel_id=1, source_target_pairs={{0,8},{8,16},{16,24},{24,0},{1,9},{9,17},{17,25},{25,1},{2,10},{10... | collective-permute-start | bytes 442376 | tf_op jit(solution)/shard_map/ppermute | solution.py:1140
  518.5 18.7 %collective-permute-start.7 = (bf16[96,3072]{1,0:T(8,128)(2,1)S(1)}, bf16[96,3072]{1,0:T(8,128)(2,1)S(1)}, u32[]{:S(2)}, u32[]{:S(2)}) collective-permute-start(bf16[96,3072]{1,0:T(8,128)(2,1)S(1)} %get-tuple-element.128), channel_id=1, source_target_pairs={{0,4},{1,5},{2,6},{3,7},{4,0},{5,1},{6,2},{7,3},{8,12},{9,13},{10,... | collective-permute-start | bytes 1769480 | tf_op jit(solution)/shard_map/ppermute | solution.py:1120
  520.2 17.1 %collective-permute-start.9 = (bf16[96,3072]{1,0:T(8,128)(2,1)S(1)}, bf16[96,3072]{1,0:T(8,128)(2,1)S(1)}, u32[]{:S(2)}, u32[]{:S(2)}) collective-permute-start(bf16[96,3072]{1,0:T(8,128)(2,1)S(1)} %get-tuple-element.127), channel_id=1, source_target_pairs={{0,2},{1,3},{2,0},{3,1},{4,6},{5,7},{6,4},{7,5},{8,10},{9,11},{10,... | collective-permute-start | bytes 1769480 | tf_op jit(solution)/shard_map/ppermute | solution.py:1120
  526.6 13.1 %collective-permute-start.1 = (bf16[96,768]{1,0:T(8,128)(2,1)S(1)}, bf16[96,768]{1,0:T(8,128)(2,1)S(1)}, u32[]{:S(2)}, u32[]{:S(2)}) collective-permute-start(bf16[96,768]{1,0:T(8,128)(2,1)S(1)} %get-tuple-element.137), channel_id=1, source_target_pairs={{0,16},{8,24},{16,0},{24,8},{1,17},{9,25},{17,1},{25,9},{2,18},{10... | collective-permute-start | bytes 442376 | tf_op jit(solution)/shard_map/ppermute | solution.py:1140
  529.8 10.0 %collective-permute-start.2 = (bf16[96,768]{1,0:T(8,128)(2,1)S(1)}, bf16[96,768]{1,0:T(8,128)(2,1)S(1)}, u32[]{:S(2)}, u32[]{:S(2)}) collective-permute-start(bf16[96,768]{1,0:T(8,128)(2,1)S(1)} %get-tuple-element.136), channel_id=1, source_target_pairs={{0,24},{8,0},{16,8},{24,16},{1,25},{9,1},{17,9},{25,17},{2,26},{10... | collective-permute-start | bytes 442376 | tf_op jit(solution)/shard_map/ppermute | solution.py:1140
  537.2 3.3 collective-permute-start.15
  539.2 3.1 collective-permute-start.10
  (69 other events, 322.2 us)
Sparse Core Ops, SparseCore 0:
  70.6 55.8 all-gather.2
  128.4 89.0 all-gather.4

commit v4 on v3

--- a/solution.py
+++ b/solution.py
@@ -467,24 +467,28 @@
         mine = slot(self.kind, self.f(s), d)
         self.own = pltpu.make_async_copy(self.shard, self.full.at[mine], self.lsem)
         self.own.start()
-        for k in range(1, 4):
-            self.go(k - 1, mine, at(lax.rem(d + k, 4), s, c), self.shard)
+        self.go(1, mine, at(flip(d, 2), s, c), self.shard)
+        self.go(0, mine, at(flip(d, 1), s, c), self.shard)
         self.go(3, mine, at(d, flip(s, 1), c), self.shard)
         self.go(4, mine, at(d, flip(s, 2), c), self.shard)
         self.go(19, mine, at(d, s, 1 - c), self.shard)
 
+    def source(self, k):
+        return (self.d, flip(self.d, 1), flip(self.d, 2), flip(flip(self.d, 1), 2))[k]
+
     def spread_z(self, k):
         d, s, c = self.d, self.s, self.c
-        source = lax.rem(d + 4 - k, 4)
-        block = slot(self.kind, self.f(s), source)
+        block = slot(self.kind, self.f(s), self.source(k))
         self.arrived(k - 1, block)
+        if k == 2:
+            self.go(2, block, at(flip(d, 1), s, c))
         self.go(3 + 2 * k, block, at(d, flip(s, 1), c))
         self.go(4 + 2 * k, block, at(d, flip(s, 2), c))
         self.go(19 + 5 * k, block, at(d, s, 1 - c))
 
     def relay(self, k):
         d, s, c = self.d, self.s, self.c
-        source = lax.rem(d + 4 - k, 4)
+        source = self.source(k)
         sx, sy = flip(s, 1), flip(s, 2)
         from_x = slot(self.kind, self.f(sx), source)
         from_y = slot(self.kind, self.f(sy), source)
@@ -497,7 +501,7 @@
 
     def corner(self, k):
         d, s, c = self.d, self.s, self.c
-        source = lax.rem(d + 4 - k, 4)
+        source = self.source(k)
         sd = flip(flip(s, 1), 2)
         for h in range(2):
             where = half_slot(self.kind, self.f(sd), source, h)
@@ -510,7 +514,7 @@
         sd = flip(sx, 2)
         self.own.wait()
         for k in range(4):
-            source = lax.rem(d + 4 - k, 4)
+            source = self.source(k)
             for j, position in enumerate((s, sx, sy)):
                 self.arrived(19 + 5 * k + j, slot(self.kind, 2 * position + 1 - c, source))
             for h in range(2):
@@ -674,8 +678,6 @@
         Line("cols", up_shard, up_line, us, ur, lsem.at[3]),
         Line("rows", down_shard, down_line, ds, dr, lsem.at[4]),
     )
-    for line in lines:
-        line.start()
     own_router = pltpu.make_async_copy(router, routers.at[me], lsem.at[1])
     own_router.start()
 
@@ -713,6 +715,8 @@
 
     for k in range(1, 8):
         tile_copy(k).start()
+    gather.spread_z(1)
+    gather.spread_z(2)
     gather.relay(0)
     for k in range(1, 8):
         tile_copy(k).wait_recv()
@@ -727,15 +731,18 @@
         zs.append(copy)
     own_rows = pltpu.make_async_copy(mixed, rows_out.at[d], lsem.at[2])
     own_rows.start()
+    gather.spread_z(3)
+    for line in lines:
+        line.start()
+    gather.relay(1)
     gather.corner(0)
-    for k in range(1, 4):
-        gather.spread_z(k)
-    for k in range(1, 4):
-        gather.relay(k)
-    for k in range(1, 4):
-        gather.corner(k)
+    gather.relay(2)
+    gather.corner(1)
+    gather.relay(3)
+    gather.corner(2)
     for line in lines:
         line.relay()
+    gather.corner(3)
     gather.finish()
     for line in lines:
         line.finish()
@@ -1120,11 +1127,16 @@
     return lax.ppermute(values, "fsdp", [(f, f ^ bit) for f in range(8)])
 
 
-def square_sum(keep, send_x, send_y):
+def square_next(keep, from_x, from_y):
     f32, bf = jnp.float32, jnp.bfloat16
-    from_x, from_y = hop(send_x, 2), hop(send_y, 4)
-    low_next = hop((keep[0, 1].astype(f32) + from_x[1].astype(f32)).astype(bf), 4)
-    high_next = hop((keep[1, 1].astype(f32) + from_y[1].astype(f32)).astype(bf), 2)
+    return (
+        hop((keep[0, 1].astype(f32) + from_x[1].astype(f32)).astype(bf), 4),
+        hop((keep[1, 1].astype(f32) + from_y[1].astype(f32)).astype(bf), 2),
+    )
+
+
+def square_last(keep, from_x, from_y, low_next, high_next):
+    f32, bf = jnp.float32, jnp.bfloat16
     low = keep[0, 0].astype(f32) + from_x[0].astype(f32) + low_next.astype(f32)
     high = keep[1, 0].astype(f32) + from_y[0].astype(f32) + high_next.astype(f32)
     first = lax.rem(lax.axis_index("fsdp"), 2) == 0
@@ -1422,6 +1434,259 @@
     )(*grads, *small)
 
 
+def layer_stats(values_in):
+    centred = values_in - jnp.mean(values_in, axis=-1, keepdims=True)
+    inv_std = lax.rsqrt(jnp.mean(centred * centred, axis=-1, keepdims=True) + 1e-06)
+    return centred * inv_std, inv_std
+
+
+def modulated(inside, mod, part):
+    columns = slice(768 * part, 768 * part + 768)
+    return inside[:, 0:1] * mod[0:1, columns] + inside[:, 1:2] * mod[1:2, columns]
+
+
+def head_column(g):
+    return 768 * (g // 9) + 64 * (g % 9)
+
+
+QUERY_ROWS = 256
+
+
+def front_kernel(
+    tokens, mod, inside, seg_col, seg_row, qkvo, router, cotangent, routes, target,
+    heads, totals, attended, projected, residual, second, d_mixed, gates, rows, grads,
+    bias, made, weighted,
+):
+    bf, f32 = jnp.bfloat16, jnp.float32
+    token_float = tokens[...].astype(f32)
+    normed, _ = layer_stats(token_float)
+    first = (normed * (1.0 + modulated(inside, mod, 1)) + modulated(inside, mod, 0)).astype(bf)
+    for j in range(4):
+        piece = nn(first, qkvo[:, 768 * j : 768 * j + 640]).astype(bf)
+        for i in range(9):
+            heads[9 * j + i] = piece[:, 64 * i : 64 * i + 64]
+    bias[...] = jnp.where(seg_col[...] == seg_row[...], 0.0, -1e30)
+
+    def block(n, carry):
+        h, part = n // (512 // QUERY_ROWS), lax.rem(n, 512 // QUERY_ROWS)
+        lines = pl.ds(pl.multiple_of(part * QUERY_ROWS, QUERY_ROWS), QUERY_ROWS)
+        scores = nt(heads[h, lines], heads[12 + h]) * 0.125 + bias[lines]
+        row_max = jnp.max(scores, axis=-1, keepdims=True)
+        weight = jnp.exp(scores - row_max)
+        running = jnp.sum(weight, axis=-1, keepdims=True)
+        probability = (weight * (1.0 / running)).astype(bf)
+        made[h, lines] = nn(probability, heads[24 + h]).astype(bf)
+        totals[h, lines] = row_max + jnp.log(running)
+        return carry
+
+    lax.fori_loop(0, 12 * (512 // QUERY_ROWS), block, 0)
+    for h in range(12):
+        attended[:, 64 * h : 64 * h + 64] = made[h]
+    for j in range(4):
+        piece = nn(attended[...], qkvo[:, 768 * j + 512 : 768 * j + 768])
+        projected[:, 192 * j : 192 * j + 192] = piece[:, 64:256]
+    residual[...] = token_float + modulated(inside, mod, 2) * projected[...]
+    normed, _ = layer_stats(residual[...])
+    second[...] = (normed * (1.0 + modulated(inside, mod, 4)) + modulated(inside, mod, 3)).astype(bf)
+    logits = nn(second[...], router[...])
+    ids = lax.broadcasted_iota(jnp.int32, (512, 8), 1)
+    chosen = [
+        jnp.sum(jnp.where(ids == routes[:, k : k + 1], logits, 0.0), axis=-1, keepdims=True)
+        for k in range(2)
+    ]
+    top = jnp.maximum(chosen[0], chosen[1])
+    raised = [jnp.exp(each - top) for each in chosen]
+    share = [each / (raised[0] + raised[1]) for each in raised]
+    pair = lax.broadcasted_iota(jnp.int32, (512, 2), 1)
+    gates[...] = jnp.where(pair == 0, share[0], share[1])
+    mixed_grad = modulated(inside, mod, 5) * cotangent[...].astype(f32)
+    d_mixed[...] = mixed_grad.astype(bf)
+    for k in range(2):
+        weighted[k] = (share[k] * mixed_grad).astype(bf)
+
+    def send(b, carry):
+        lines = pl.ds(pl.multiple_of(288 * b, 288), 288)
+        places = lax.broadcasted_iota(jnp.int32, (288, 512), 0) + 288 * b
+        first_hot = (places == target[0:1]).astype(f32)
+        second_hot = (places == target[1:2]).astype(f32)
+        rows[lines] = nn((first_hot + second_hot).astype(bf), second[...]).astype(bf)
+        grads[lines] = (
+            nn(first_hot.astype(bf), weighted[0]) + nn(second_hot.astype(bf), weighted[1])
+        ).astype(bf)
+        return carry
+
+    lax.fori_loop(0, 4, send, 0)
+
+
+def front(tokens, mod, inside, seg_col, seg_row, qkvo, router, cotangent, routes, target):
+    bf, f32 = jnp.bfloat16, jnp.float32
+    return pl.pallas_call(
+        front_kernel,
+        out_shape=(
+            jax.ShapeDtypeStruct((36, 512, 64), bf),
+            jax.ShapeDtypeStruct((12, 512, 1), f32),
+            jax.ShapeDtypeStruct((512, 768), bf),
+            jax.ShapeDtypeStruct((512, 768), f32),
+            jax.ShapeDtypeStruct((512, 768), f32),
+            jax.ShapeDtypeStruct((512, 768), bf),
+            jax.ShapeDtypeStruct((512, 768), bf),
+            jax.ShapeDtypeStruct((512, 2), f32),
+            jax.ShapeDtypeStruct((1152, 768), bf),
+            jax.ShapeDtypeStruct((1152, 768), bf),
+        ),
+        in_specs=[ONCHIP] * 10,
+        out_specs=(ONCHIP,) * 10,
+        scratch_shapes=[
+            pltpu.VMEM((512, 512), f32),
+            pltpu.VMEM((12, 512, 64), bf),
+            pltpu.VMEM((2, 512, 768), bf),
+        ],
+        compiler_params=pltpu.CompilerParams(vmem_limit_bytes=60 << 20),
+        name="front",
+    )(tokens, mod, inside, seg_col, seg_row, qkvo, router, cotangent, routes, target)
+
+
+def norm_grad(upstream, normed, inv_std):
+    return (
+        upstream
+        - jnp.mean(upstream, axis=-1, keepdims=True)
+        - normed * jnp.mean(upstream * normed, axis=-1, keepdims=True)
+    ) * inv_std
+
+
+def rear_kernel(
+    tokens, mod, inside, seg_col, seg_row, qkvo, router, cotangent, routes, target,
+    heads, totals, attended, projected, residual, second, gates,
+    returned, d_returned, shared_out, d_shared,
+    output, tokens_grad, qkvo_grad, d_mod, router_grad,
+    bias, rows_t, d_heads, d_att, d_att_t, d_rows_t, d_rows, d_residual, d_proj,
+):
+    bf, f32 = jnp.bfloat16, jnp.float32
+    upstream = cotangent[...].astype(f32)
+
+    def image_sums(part, values):
+        for j in range(2):
+            d_mod[j : j + 1, 768 * part : 768 * part + 768] = jnp.sum(
+                inside[:, j : j + 1] * values, axis=0, keepdims=True
+            )
+
+    share = [gates[:, k : k + 1] for k in range(2)]
+    places = lax.broadcasted_iota(jnp.int32, (512, 1152), 1)
+    hot = [(places == target[:, k : k + 1]).astype(f32).astype(bf) for k in range(2)]
+    picked = [nn(each, returned[...]) for each in hot]
+    mixed = shared_out[...] + (share[0] * picked[0] + share[1] * picked[1])
+    gate_two = modulated(inside, mod, 5)
+    output[...] = (residual[...] + gate_two * mixed).astype(bf)
+    image_sums(5, upstream * mixed)
+    mixed_grad = gate_two * upstream
+    d_share = [jnp.sum(mixed_grad * each, axis=-1, keepdims=True) for each in picked]
+    inner = share[0] * d_share[0] + share[1] * d_share[1]
+    ids = lax.broadcasted_iota(jnp.int32, (512, 8), 1)
+    d_logits = sum(
+        jnp.where(ids == routes[:, k : k + 1], share[k] * (d_share[k] - inner), 0.0) for k in range(2)
+    ).astype(bf)
+    router_grad[...] = tn(d_logits, second[...])
+    d_second = (
+        d_shared[...] + nt(d_logits, router[...]) + (nn(hot[0], d_returned[...]) + nn(hot[1], d_returned[...]))
+    )
+    normed, inv_std = layer_stats(residual[...])
+    image_sums(3, d_second)
+    image_sums(4, d_second * normed)
+    d_residual[...] = upstream + norm_grad(d_second * (1.0 + modulated(inside, mod, 4)), normed, inv_std)
+    gate_one = modulated(inside, mod, 2)
+    image_sums(2, d_residual[...] * projected[...])
+    d_proj[...] = (gate_one * d_residual[...]).astype(bf)
+    d_attended = jnp.zeros((512, 768), f32)
+    for j in range(4):
+        piece = jnp.concatenate(
+            [jnp.zeros((512, 64), bf), d_proj[:, 192 * j : 192 * j + 192]], axis=1
+        )
+        d_attended += nt(piece, qkvo[:, 768 * j + 512 : 768 * j + 768])
+    d_attended = d_attended.astype(bf)
+    d_att_t[...] = d_attended.T
+    for h in range(12):
+        d_att[h] = d_attended[:, 64 * h : 64 * h + 64]
+    for j in range(18):
+        pair = jnp.concatenate([heads[2 * j], heads[2 * j + 1]], axis=1)
+        rows_t[128 * j : 128 * j + 128] = pair.T
+    bias[...] = jnp.where(seg_col[...] == seg_row[...], 0.0, -1e30)
+
+    def head(h, carry):
+        def at_head(g):
+            return pl.ds(pl.multiple_of(64 * g, 64), 64)
+
+        d_key, d_value = jnp.zeros((64, 512), f32), jnp.zeros((64, 512), f32)
+        for part in range(512 // QUERY_ROWS):
+            lines = slice(part * QUERY_ROWS, (part + 1) * QUERY_ROWS)
+            scores = nn(heads[h, lines], rows_t[at_head(12 + h)]) * 0.125 + bias[lines]
+            probability = jnp.exp(scores - totals[h, lines])
+            d_prob = nn(d_att[h, lines], rows_t[at_head(24 + h)])
+            inner = jnp.sum(probability * d_prob, axis=-1, keepdims=True)
+            d_scores = (probability * (d_prob - inner)).astype(bf)
+            d_heads[h, lines] = (nn(d_scores, heads[12 + h]) * 0.125).astype(bf)
+            d_key += nn(rows_t[at_head(h), lines], d_scores)
+            d_value += nn(d_att_t[at_head(h), lines], probability.astype(bf))
+        d_rows_t[at_head(h)] = (d_key * 0.125).astype(bf)
+        d_rows_t[at_head(12 + h)] = d_value.astype(bf)
+        return carry
+
+    lax.fori_loop(0, 12, head, 0)
+    for g in range(12):
+        column = head_column(g)
+        d_rows[:, column : column + 64] = d_heads[g]
+    for j in range(12):
+        pair = d_rows_t[128 * j : 128 * j + 128].T
+        for i in range(2):
+            column = head_column(12 + 2 * j + i)
+            d_rows[:, column : column + 64] = pair[:, 64 * i : 64 * i + 64]
+    for j in range(4):
+        d_rows[:, 768 * j + 576 : 768 * j + 768] = jnp.zeros((512, 192), bf)
+    token_float = tokens[...].astype(f32)
+    normed, inv_std = layer_stats(token_float)
+    scale_one = 1.0 + modulated(inside, mod, 1)
+    first_t = (normed * scale_one + modulated(inside, mod, 0)).astype(bf).T
+    attended_t = attended[...].T
+    for j in range(4):
+        qkvo_grad[:, 768 * j : 768 * j + 640] = nn(first_t, d_rows[:, 768 * j : 768 * j + 640]).astype(bf)
+        qkvo_grad[:, 768 * j + 576 : 768 * j + 768] = nn(
+            attended_t, d_proj[:, 192 * j : 192 * j + 192]
+        ).astype(bf)
+    d_first = nt(d_rows[...], qkvo[...])
+    image_sums(0, d_first)
+    image_sums(1, d_first * normed)
+    tokens_grad[...] = d_residual[...] + norm_grad(d_first * scale_one, normed, inv_std)
+
+
+def rear(*operands):
+    bf, f32 = jnp.bfloat16, jnp.float32
+    return pl.pallas_call(
+        rear_kernel,
+        out_shape=(
+            jax.ShapeDtypeStruct((512, 768), bf),
+            jax.ShapeDtypeStruct((512, 768), f32),
+            jax.ShapeDtypeStruct((768, 3072), bf),
+            jax.ShapeDtypeStruct((2, 4608), f32),
+            jax.ShapeDtypeStruct((8, 768), f32),
+        ),
+        in_specs=[ONCHIP] * len(operands),
+        out_specs=(ONCHIP,) * 5,
+        scratch_shapes=[
+            pltpu.VMEM((512, 512), f32),
+            pltpu.VMEM((2304, 512), bf),
+            pltpu.VMEM((12, 512, 64), bf),
+            pltpu.VMEM((12, 512, 64), bf),
+            pltpu.VMEM((768, 512), bf),
+            pltpu.VMEM((1536, 512), bf),
+            pltpu.VMEM((512, 3072), bf),
+            pltpu.VMEM((512, 768), f32),
+            pltpu.VMEM((512, 768), bf),
+        ],
+        compiler_params=pltpu.CompilerParams(vmem_limit_bytes=67043328),
+        cost_estimate=pl.CostEstimate(flops=60_000_000_000, bytes_accessed=30_000_000, transcendentals=0),
+        name="rear",
+    )(*operands)
+
+
 def fitted_shards(
     tokens,
     condition,
@@ -1442,6 +1707,7 @@
     model_width = tokens.shape[1]
     head_size = model_width // HEADS
     inside, segment = owners(image_sizes)
+    up_all, down_all = gather_experts(expert_up, expert_down)
     ids = jnp.arange(EXPERTS, dtype=jnp.int32)
     hot = routes[:, :, None] == ids[None, None, :]
     hot_any = jnp.any(hot, axis=1).astype(bf)
@@ -1450,9 +1716,6 @@
     before = nn(earlier, hot_any)
     position = jnp.sum(jnp.where(hot, before[:, None, :], 0.0), axis=-1).astype(jnp.int32)
     target = routes * CAP + position
-    places = jnp.arange(EXPERTS * CAP, dtype=jnp.int32)
-    send_0 = (places[:, None] == target[None, :, 0]).astype(bf)
-    send_1 = (places[:, None] == target[None, :, 1]).astype(bf)
     live = (segment < IMG_DEV).astype(jnp.float32)
     counts = jnp.sum(live[:, None] * hot_any.astype(jnp.float32), axis=0)
     cond_float = condition.astype(jnp.float32)
@@ -1466,8 +1729,6 @@
     qkvo, routers, seen, mod_rows, up_line, down_line = opening(
         qkvo_shard, router_pack, act_slices, ada_pad, shared_up, shared_down.T
     )
-    expert_up, expert_down, seen = lax.optimization_barrier((expert_up, expert_down, seen))
-    up_all, down_all = gather_experts(expert_up, expert_down)
     expert_counts = seen[66, :EXPERTS].astype(jnp.int32)
     modulation = lax.dynamic_slice(mod_rows, (0, 2 * d_index, 0), (4, 2, 1152))
     modulation = modulation.transpose(1, 0, 2).reshape(2, 4608)
@@ -1477,114 +1738,33 @@
         .transpose(1, 2, 0, 3)
         .reshape(model_width, EXPERTS)
     )
-    qkvo = qkvo.reshape(model_width, 4, 768)
-    qkv_full = qkvo[:, :, :576].reshape(model_width, 2304)
-    out_full = qkvo[:, :, 576:].reshape(model_width, 768)
-    per_row = inside[:, 0:1] * modulation[0:1] + inside[:, 1:2] * modulation[1:2]
-    shift_one, scale_one, gate_one, shift_two, scale_two, gate_two = jnp.split(per_row, 6, axis=1)
-    token_float = tokens.astype(jnp.float32)
-    normed_one, inv_one = layer_norm(token_float)
-    first_input = (normed_one * (1.0 + scale_one) + shift_one).astype(bf)
-    qkv_rows = nn(first_input, qkv_full).astype(bf)
-    queries, keys, values = (
-        qkv_rows[:, i * model_width : (i + 1) * model_width]
-        .reshape(LONG, HEADS, head_size)
-        .transpose(1, 0, 2)
-        for i in range(3)
-    )
-    scale = head_size**-0.5
-    allowed = (segment[:, None] == segment[None, :])[None]
-    scores = jnp.einsum("hqd,hkd->hqk", queries, keys, preferred_element_type=jnp.float32) * scale
-    scores = jnp.where(allowed, scores, -1e30)
-    row_max = jnp.max(scores, axis=-1, keepdims=True)
-    weight = jnp.exp(scores - row_max)
-    running = jnp.sum(weight, axis=-1, keepdims=True)
-    probability = weight / running
-    prob_low = probability.astype(bf)
-    attended = jnp.einsum("hqk,hkd->hqd", prob_low, values, preferred_element_type=jnp.float32)
-    attended = attended.astype(bf).transpose(1, 0, 2).reshape(LONG, model_width)
-    projected = nn(attended, out_full)
-    residual_one = token_float + gate_one * projected
-    normed_two, inv_two = layer_norm(residual_one)
-    second_input = (normed_two * (1.0 + scale_two) + shift_two).astype(bf)
-    logits = nn(second_input, router_full)
-    route_hot = hot.astype(jnp.float32)
-    chosen = jnp.sum(logits[:, None, :] * route_hot, axis=-1)
-    gate_share = jax.nn.softmax(chosen, axis=-1)
-    upstream = cotangent.astype(jnp.float32)
-    d_mixed = gate_two * upstream
-    rows = nn(send_0 + send_1, second_input).astype(bf).reshape(EXPERTS, CAP, model_width)
-    weighted = jnp.concatenate(
-        [(gate_share[:, k : k + 1] * d_mixed).astype(bf) for k in range(2)], axis=0
-    )
-    grads = (
-        nn(jnp.concatenate([send_0, send_1], axis=1), weighted)
-        .astype(bf)
-        .reshape(EXPERTS, CAP, model_width)
-    )
+    segments = (segment[:, None], segment[None, :])
+    heads, totals, attended, projected, residual, second_input, d_mixed, gates, rows, grads = front(
+        tokens, modulation, inside, *segments, qkvo, router_full, cotangent, routes, target.T
+    )
+    rows = rows.reshape(EXPERTS, CAP, model_width)
+    grads = grads.reshape(EXPERTS, CAP, model_width)
     rows_in, grads_in, shared_out, d_second, shared_first_grad, shared_second_grad = outbound(
-        rows, grads, up_line, down_line, second_input, d_mixed.astype(bf)
+        rows, grads, up_line, down_line, second_input, d_mixed
     )
     returned, d_returned, *parts, first_part, second_part = experts(
         rows_in, grads_in, up_all, down_all, shared_first_grad, shared_second_grad
     )
-    expert_up_grad, expert_down_grad = square_sum(*parts[:3]), square_sum(*parts[3:])
+    up_keep, up_x, up_y, down_keep, down_x, down_y = parts
+    up_near, down_near = (hop(up_x, 2), hop(up_y, 4)), (hop(down_x, 2), hop(down_y, 4))
     shared_first_sum, shared_second_sum = line_sum(first_part, 1), line_sum(second_part, 0)
     returned = returned.reshape(EXPERTS * CAP, model_width)
     d_returned = d_returned.reshape(EXPERTS * CAP, model_width)
-    picked_0 = tn(send_0, returned)
-    picked_1 = tn(send_1, returned)
-    mixed = shared_out + (gate_share[:, 0:1] * picked_0 + gate_share[:, 1:2] * picked_1)
-    output = (residual_one + gate_two * mixed).astype(bf)
-    d_gate_two = upstream * mixed
-    d_gate_share = jnp.stack(
-        [jnp.sum(d_mixed * picked_0, axis=-1), jnp.sum(d_mixed * picked_1, axis=-1)], axis=1
-    )
-    d_chosen = gate_share * (
-        d_gate_share - jnp.sum(gate_share * d_gate_share, axis=-1, keepdims=True)
-    )
-    d_logits = jnp.sum(d_chosen[:, :, None] * route_hot, axis=1).astype(bf)
-    router_grad = tn(d_logits, second_input)
-    d_second = d_second + nt(d_logits, router_full) + tn(send_0 + send_1, d_returned)
-    d_scale_two = d_second * normed_two
-    d_residual = upstream + norm_back(d_second * (1.0 + scale_two), normed_two, inv_two)
-    d_projected = (gate_one * d_residual).astype(bf)
-    d_gate_one = d_residual * projected
-    out_grad = tn(attended, d_projected)
-    d_attended = nt(d_projected, out_full).astype(bf)
-    d_attended = d_attended.reshape(LONG, HEADS, head_size).transpose(1, 0, 2)
-    d_prob = jnp.einsum("hqd,hkd->hqk", d_attended, values, preferred_element_type=jnp.float32)
-    d_scores = (
-        probability * (d_prob - jnp.sum(probability * d_prob, axis=-1, keepdims=True))
-    ).astype(bf)
-    d_queries = jnp.einsum("hqk,hkd->hqd", d_scores, keys, preferred_element_type=jnp.float32) * scale
-    d_keys = jnp.einsum("hqk,hqd->hkd", d_scores, queries, preferred_element_type=jnp.float32) * scale
-    d_values = jnp.einsum("hqk,hqd->hkd", prob_low, d_attended, preferred_element_type=jnp.float32)
-    d_qkv = jnp.concatenate(
-        [
-            piece.astype(bf).transpose(1, 0, 2).reshape(LONG, model_width)
-            for piece in (d_queries, d_keys, d_values)
-        ],
-        axis=1,
-    )
-    qkv_grad = tn(first_input, d_qkv)
-    d_first = nt(d_qkv, qkv_full)
-    d_scale_one = d_first * normed_one
-    tokens_grad = d_residual + norm_back(d_first * (1.0 + scale_one), normed_one, inv_one)
-    qkvo_grad = (
-        jnp.concatenate(
-            [qkv_grad.reshape(model_width, 4, 576), out_grad.reshape(model_width, 4, 192)], axis=2
-        )
-        .astype(bf)
-        .reshape(model_width, 3072)
-    )
-    d_modulation = jnp.concatenate(
-        [
-            jnp.stack([jnp.sum(inside[:, j : j + 1] * piece, axis=0) for j in range(IMG_DEV)])
-            for piece in (d_first, d_scale_one, d_gate_one, d_second, d_scale_two, d_gate_two)
-        ],
-        axis=1,
-    ).astype(bf)
+    output, tokens_grad, qkvo_grad, d_modulation, router_grad = rear(
+        tokens, modulation, inside, *segments, qkvo, router_full, cotangent, routes, target,
+        heads, totals, attended, projected, residual, second_input, gates,
+        returned, d_returned, shared_out, d_second,
+    )
+    qkvo_grad, up_near, down_near, shared_first_sum, shared_second_sum = lax.optimization_barrier(
+        (qkvo_grad, up_near, down_near, shared_first_sum, shared_second_sum)
+    )
+    up_next, down_next = square_next(up_keep, *up_near), square_next(down_keep, *down_near)
+    d_modulation = d_modulation.astype(bf)
     d_mod_rows = d_modulation.astype(jnp.float32).reshape(2, 4, 1152).transpose(1, 0, 2)
     d_mod_rows = lax.dynamic_update_slice(
         jnp.zeros((4, 8, 1152), jnp.float32), d_mod_rows, (0, 2 * d_index, 0)
@@ -1598,6 +1778,9 @@
         (d_mod_rows, router_tiles, seen[:64].astype(bf), ada_weight),
         3,
     )
+    qkvo_sum, up_next, down_next = lax.optimization_barrier((qkvo_sum, up_next, down_next))
+    expert_up_grad = square_last(up_keep, *up_near, *up_next)
+    expert_down_grad = square_last(down_keep, *down_near, *down_next)
     d_activated = lax.dynamic_slice(d_act_tiles, (0, 2 * d_index, 0), (8, 2, 96))
     d_activated = d_activated.transpose(1, 0, 2).reshape(2, model_width)
     condition_grad = jax.vjp(jax.nn.silu, cond_float)[1](d_activated)[0]

time: 559 us -> 466 us (0.83)
  matrix products: 74.3 us -> 0.22 us
  Pallas kernels: 294 us -> 366 us
  local copies, waits for them, and re-layouts: 58.7 us -> 19.6 us
  other arithmetic: 46.6 us -> 24.3 us
  waiting for transfers between devices: 32.5 us -> 10.6 us
  starting transfers between devices: 30.2 us -> 22.4 us
    pallas_call x0 -> x2, Pallas kernels: none -> 76 us  [the longest x1 43.7 us: rear(): pl.pallas_call(rear_kernel, out_shape=(jax.ShapeDtypeStruct((512, 768), b...]
    dot_general x14 -> x0, matrix products: 51.5 us -> none  [the longest x6 17.2 us: tn(): lax.dot_general(left, right, (((0,), (0,)), ((), ())), preferred_element_...]
    ppermute x10, waiting for transfers between devices: 31.7 us -> 0.03 us  [hop(): return lax.ppermute(values, 'fsdp', [(f, f ^ bit) for f in range(8)])]
    dot_general x6 -> x1, matrix products: 11.9 us -> 0.22 us  [nn(): return jnp.dot(left, right, preferred_element_type=jnp.float32)]
    convert_element_type x8 -> x3, other arithmetic: 18.6 us -> 7.12 us  [the longest x2 5.74 us: square_next(): (keep[1, 1].astype(f32) + from_y[1].astype(f32)).astype(bf)]
    sub x1 -> x0, matrix products: 10.9 us -> none  [fitted_shards(): weight = jnp.exp(scores - row_max)]
    slice x10 -> x0, local copies, waits for them, and re-layouts: 10.6 us -> none  [the longest x4 4.99 us: fitted_shards(): qkv_rows[:, i * model_width:(i + 1) * model_width]]
    ppermute x6, waiting for transfers between devices: 0.02 us -> 9.15 us  [line_sum(): got = lax.ppermute(block, 'dp', [(i, (i + k) % 4) for i in range(4)])]
  transfers between devices with their start and end apart: 18 -> 18, of which waited for: 4 -> 3; matrix products, arithmetic and copies ran while one was open for 15% -> 8% of each run, Pallas kernels for 18% -> 60%
where the time goes in v4:
time: 466 us; the launch traced here: 458 us
  Pallas kernels  366 us (79%)
  other arithmetic  24.3 us (5%)
  starting transfers between devices  22.4 us (5%)
  local copies, waits for them, and re-layouts  19.6 us (4%)
  between operations  14.9 us (3%)
  waiting for transfers between devices  10.6 us (2%)
    pallas_call x1, Pallas kernels, outbound(): pl.pallas_call(out_kernel, out_shape=(jax.ShapeDtypeStruct((8, 144, 768),...  94.7 us
    pallas_call x1, Pallas kernels, experts(): pl.pallas_call(expert_kernel, out_shape=(jax.ShapeDtypeStruct((8, 144, 76...  91.8 us
    pallas_call x1, Pallas kernels, opening(): pl.pallas_call(open_kernel, out_shape=(jax.ShapeDtypeStruct((768, 3072),...  57.1 us
    pallas_call x1, Pallas kernels, dense_sums(): pl.pallas_call(functools.partial(dense_kernel, kinds), out_shape=tuple(ou...  45.9 us
    pallas_call x1, Pallas kernels, rear(): pl.pallas_call(rear_kernel, out_shape=(jax.ShapeDtypeStruct((512, 768), b...  43.7 us
    pallas_call x1, Pallas kernels, front(): pl.pallas_call(front_kernel, out_shape=(jax.ShapeDtypeStruct((36, 512, 64...  32.3 us
    ppermute x6, starting transfers between devices, line_sum(): got = lax.ppermute(block, 'dp', [(i, (i + k) % 4) for i in range(4)])  13.8 us
  transfers between devices with their start and end apart: 18, of which 3 were waited for; matrix products, arithmetic and copies ran while one was open for 8% of the time, Pallas kernels for 60%

profile of v4, /device:TPU:0, one launch (start us, length us, event | category | flops | bytes accessed | tf_op | source)
XLA Modules:
  0.0 457.5 jit_solution(4459587300385232623)
XLA Ops:
  13.7 57.1 %opening.1 = (bf16[768,3072]{1,0:T(8,128)(2,1)}, bf16[32,16,128]{2,1,0:T(8,128)(2,1)}, f32[72,128]{1,0:T(8,128)}, f32[4,8,1152]{2,1,0:T(8,128)}, bf16[96,3072]{1,0:T(8,128)(2,1)}, /*index=5*/bf16[768,384]{1,0:T(8,128)(2,1)}) custom-call(bf16[96,768]{1,0:T(8,128)(2,1)} %pad_maximum_fusion.shard, bf16[16,128]{1,0:T(8,128)(2,1)} %pad_bitcast_fusion.router, ...), custom_call_target="tpu_custom_call" | custom-call | tf_op jit(solution)/shard_map/opening/pallas_call | solution.py:777
  75.0 1.5 constant_dynamic-slice_fusion.7
  76.5 32.3 %front.1 = (bf16[36,512,64]{2,1,0:T(8,128)(2,1)}, f32[12,512,1]{2,1,0:T(8,128)}, bf16[512,768]{1,0:T(8,128)(2,1)}, f32[512,768]{1,0:T(8,128)}, f32[512,768]{1,0:...) custom-call(bf16[512,768]{1,0:T(8,128)(2,1)} %tokens.3, ...), custom_call_target="tpu_custom_call" | custom-call | tf_op jit(solution)/shard_map/front/pallas_call | solution.py:1523
  108.8 94.7 %outbound.1 = (bf16[8,144,768]{2,1,0:T(8,128)(2,1)}, bf16[8,144,768]{2,1,0:T(8,128)(2,1)}, f32[512,768]{1,0:T(8,128)}, f32[512,768]{1,0:T(8,128)}, bf16[768,3072]{1,0:T(8,128)(2,1)}, /*index=5*/bf16[768,3072]{1,0:T(8,128)(2,1)}) custom-call(bf16[8,144,768]{2,1,0:T(8,128)(2,1)} %bitcast.114, bf16[8,144,768]{2,1,0:T(8,128)(2,1)} %bitcast.115, ...), custom_call_target="tpu_custom_call" | custom-call | tf_op jit(solution)/shard_map/outbound/pallas_call | solution.py:928
  203.6 91.8 %experts.1 = (bf16[8,144,768]{2,1,0:T(8,128)(2,1)}, bf16[8,144,768]{2,1,0:T(8,128)(2,1)}, bf16[2,2,96,3072]{3,2,1,0:T(8,128)(2,1)}, bf16[2,96,3072]{2,1,0:T(8,12...) custom-call(bf16[8,144,768]{2,1,0:T(8,128)(2,1)} %get-tuple-element., ...), custom_call_target="tpu_custom_call" | custom-call | tf_op jit(solution)/shard_map/experts/pallas_call | solution.py:1088
  296.6 3.4 collective-permute-start.7
  300.1 2.8 collective-permute-start.9
  304.6 2.0 collective-permute-start.5
  307.4 4.3 collective-permute-done.8
  315.8 43.7 %rear.1 = (bf16[512,768]{1,0:T(8,128)(2,1)}, f32[512,768]{1,0:T(8,128)}, bf16[768,3072]{1,0:T(8,128)(2,1)}, f32[2,4608]{1,0:T(2,128)}, f32[8,768]{1,0:T(8,128)}) custom-call(bf16[512,768]{1,0:T(8,128)(2,1)} %tokens.3, f32[2,4608]{1,0:T(2,128)} %bitcast.120, f32[512,2]{1,0:T(8,128)} %get-tuple-element.148.inside, s32[512,1]{1,0:T(8,128)} %copy.72.seg_col, ...), custom_call_target="tpu_custom_call" | custom-call | flops 60000002048 | bytes 30000000 | tf_op jit(solution)/shard_map/rear/pallas_call | solution.py:1662
  359.4 5.5 %collective-permute-start.6 = (bf16[96,768]{1,0:T(8,128)(2,1)}, bf16[96,768]{1,0:T(8,128)(2,1)S(1)}, u32[]{:S(2)}, u32[]{:S(2)}) collective-permute-start(bf16[96,768]{1,0:T(8,128)(2,1)} %get-tuple-element.146), channel_id=1, source_target_pairs={{0,24},{8,0},{16,8},{24,16},{1,25},{9,1},{17,9},{25,17},{2,26},{10... | collective-permute-start | bytes 442376 | tf_op jit(solution)/shard_map/ppermute | solution.py:1152
  364.9 1.9 convert_add_fusion.8
  366.8 3.8 collective-permute-done.6
  370.6 1.8 convert_add_fusion.9
  372.4 3.1 fusion.4
  377.5 2.7 fusion.6
  383.4 1.4 slice.139.refs_3_
  384.8 1.4 convert_element_type.213
  386.2 1.4 reshape.217
  391.0 45.9 %dense_sums.1 = (f32[96,768]{1,0:T(8,128)}, f32[96,1152]{1,0:T(8,128)}, f32[8,8,128]{2,1,0:T(8,128)}, f32[8,128]{1,0:T(8,128)}) custom-call(bf16[768,3072]{1,0:T(8,128)(2,1)} %get-tuple-element.109.refs_0_, f32[4,8,1152]{2,1,0:T(8,128)} %fusion.16.refs_1_, f32[8,8,128]{2,1,0:T(8,128)} %pad.27.refs_2_, bf16[64,128]{1,0:T(8,128)(2,1)} %slice.139.refs_3_, ...), custom_call_target="tpu_custom_call" | custom-call | tf_op jit(solution)/shard_map/dense_sums/pallas_call | solution.py:1426
  437.8 2.2 fusion.12
  440.2 2.0 fusion.10
  446.1 1.6 maximum_select_fusion.1
  447.9 1.6 maximum_select_fusion
  (109 shorter events, 32.6 us)
Async XLA Ops:
  7.2 196.3 %all-gather.3.cloned.1.call-start = ((), (), s32[]{:S(2)}) async-start(), calls=%async_computation | async-start | bytes 10616832 | tf_op jit(solution)/shard_map/all_gather | solution.py:94
  8.0 5.0 %copy-start.6 = (bf16[96,576]{1,0:T(8,128)(2,1)S(1)}, bf16[96,576]{1,0:T(8,128)(2,1)}, u32[]{:S(2)}) copy-start(bf16[96,576]{1,0:T(8,128)(2,1)} %param.18) | copy-start | bytes 331780
  8.0 5.0 %copy-start.8 = (bf16[96,192]{1,0:T(8,128)(2,1)S(1)}, bf16[96,192]{1,0:T(8,128)(2,1)}, u32[]{:S(2)}) copy-start(bf16[96,192]{1,0:T(8,128)(2,1)} %param.19) | copy-start | bytes 110596
  8.0 195.6 %all-gather.5.cloned.1.call-start = ((), (), s32[]{:S(2)}) async-start(), calls=%async_computation.1 | async-start | bytes 10616832 | tf_op jit(solution)/shard_map/all_gather | solution.py:95
  11.2 62.0 %copy-start.10 = (s32[512]{0:T(512)}, s32[512]{0:T(512)S(1)}, u32[]{:S(2)}) copy-start(s32[512]{0:T(512)S(1)} %get-tuple-element.131) | copy-start | bytes 6148
  295.4 7.5 %copy-start.2 = (bf16[96,3072]{1,0:T(8,128)(2,1)S(1)}, bf16[96,3072]{1,0:T(8,128)(2,1)}, u32[]{:S(2)}) copy-start(bf16[96,3072]{1,0:T(8,128)(2,1)} %get-tuple-element.107) | copy-start | bytes 1769476
  295.4 8.3 %copy-start.9 = (s32[512,2]{0,1:T(2,128)S(1)}, s32[512,2]{0,1:T(2,128)}, u32[]{:S(2)}) copy-start(s32[512,2]{0,1:T(2,128)} %convert_add_fusion.10) | copy-start | bytes 12292
  296.6 10.0 %collective-permute-start.7 = (bf16[192,384]{1,0:T(8,128)(2,1)S(1)}, bf16[192,384]{1,0:T(8,128)(2,1)}, u32[]{:S(2)}, u32[]{:S(2)}) collective-permute-start(bf16[192,384]{1,0:T(8,128)(2,1)S(1)} %get-tuple-element.142), channel_id=1, source_target_pairs={{0,8},{8,16},{16,24},{24,0},{1,9},{9,17},{17,25},{25,1},{2,10},{10... | collective-permute-start | bytes 442376 | tf_op jit(solution)/shard_map/ppermute | solution.py:1152
  300.0 11.7 %collective-permute-start.8 = (bf16[192,384]{1,0:T(8,128)(2,1)S(1)}, bf16[192,384]{1,0:T(8,128)(2,1)}, u32[]{:S(2)}, u32[]{:S(2)}) collective-permute-start(bf16[192,384]{1,0:T(8,128)(2,1)S(1)} %get-tuple-element.144), channel_id=1, source_target_pairs={{0,16},{8,24},{16,0},{24,8},{1,17},{9,25},{17,1},{25,9},{2,18},{10... | collective-permute-start | bytes 442376 | tf_op jit(solution)/shard_map/ppermute | solution.py:1152
  300.1 12.5 %collective-permute-start.9 = (bf16[192,384]{1,0:T(8,128)(2,1)S(1)}, bf16[192,384]{1,0:T(8,128)(2,1)}, u32[]{:S(2)}, u32[]{:S(2)}) collective-permute-start(bf16[192,384]{1,0:T(8,128)(2,1)S(1)} %get-tuple-element.143), channel_id=1, source_target_pairs={{0,24},{8,0},{16,8},{24,16},{1,25},{9,1},{17,9},{25,17},{2,26},{10... | collective-permute-start | bytes 442376 | tf_op jit(solution)/shard_map/ppermute | solution.py:1152
  303.7 11.2 %collective-permute-start.4 = (bf16[96,768]{1,0:T(8,128)(2,1)S(1)}, bf16[96,768]{1,0:T(8,128)(2,1)}, u32[]{:S(2)}, u32[]{:S(2)}) collective-permute-start(bf16[96,768]{1,0:T(8,128)(2,1)S(1)} %get-tuple-element.145), channel_id=1, source_target_pairs={{0,8},{8,16},{16,24},{24,0},{1,9},{9,17},{17,25},{25,1},{2,10},{10... | collective-permute-start | bytes 442376 | tf_op jit(solution)/shard_map/ppermute | solution.py:1152
  304.6 54.9 %collective-permute-start.5 = (bf16[96,768]{1,0:T(8,128)(2,1)}, bf16[96,768]{1,0:T(8,128)(2,1)}, u32[]{:S(2)}, u32[]{:S(2)}) collective-permute-start(bf16[96,768]{1,0:T(8,128)(2,1)} %get-tuple-element.147), channel_id=1, source_target_pairs={{0,16},{8,24},{16,0},{24,8},{1,17},{9,25},{17,1},{25,9},{2,18},{10... | collective-permute-start | bytes 442376 | tf_op jit(solution)/shard_map/ppermute | solution.py:1152
  306.6 65.8 %collective-permute-start = (bf16[2,96,3072]{2,1,0:T(8,128)(2,1)}, bf16[2,96,3072]{2,1,0:T(8,128)(2,1)}, u32[]{:S(2)}, u32[]{:S(2)}) collective-permute-start(bf16[2,96,3072]{2,1,0:T(8,128)(2,1)} %get-tuple-element.103), channel_id=1, source_target_pairs={{0,2},{1,3},{2,0},{3,1},{4,6},{5,7},{6,4},{7,5},{8,10},{9,11},{10,... | collective-permute-start | bytes 3538952 | tf_op jit(solution)/shard_map/ppermute | solution.py:1127
  311.7 60.7 %collective-permute-start.1 = (bf16[2,96,3072]{2,1,0:T(8,128)(2,1)}, bf16[2,96,3072]{2,1,0:T(8,128)(2,1)}, u32[]{:S(2)}, u32[]{:S(2)}) collective-permute-start(bf16[2,96,3072]{2,1,0:T(8,128)(2,1)} %get-tuple-element.104), channel_id=1, source_target_pairs={{0,4},{1,5},{2,6},{3,7},{4,0},{5,1},{6,2},{7,3},{8,12},{9,13},{10,... | collective-permute-start | bytes 3538952 | tf_op jit(solution)/shard_map/ppermute | solution.py:1127
  312.6 59.8 %collective-permute-start.2 = (bf16[2,384,768]{2,1,0:T(8,128)(2,1)}, bf16[2,384,768]{2,1,0:T(8,128)(2,1)}, u32[]{:S(2)}, u32[]{:S(2)}) collective-permute-start(bf16[2,384,768]{2,1,0:T(8,128)(2,1)} %get-tuple-element.105), channel_id=1, source_target_pairs={{0,2},{1,3},{2,0},{3,1},{4,6},{5,7},{6,4},{7,5},{8,10},{9,11},{10,... | collective-permute-start | bytes 3538952 | tf_op jit(solution)/shard_map/ppermute | solution.py:1127
  314.9 57.5 %collective-permute-start.3 = (bf16[2,384,768]{2,1,0:T(8,128)(2,1)}, bf16[2,384,768]{2,1,0:T(8,128)(2,1)}, u32[]{:S(2)}, u32[]{:S(2)}) collective-permute-start(bf16[2,384,768]{2,1,0:T(8,128)(2,1)} %get-tuple-element.106), channel_id=1, source_target_pairs={{0,4},{1,5},{2,6},{3,7},{4,0},{5,1},{6,2},{7,3},{8,12},{9,13},{10,... | collective-permute-start | bytes 3538952 | tf_op jit(solution)/shard_map/ppermute | solution.py:1127
  359.4 11.1 %collective-permute-start.6 = (bf16[96,768]{1,0:T(8,128)(2,1)}, bf16[96,768]{1,0:T(8,128)(2,1)S(1)}, u32[]{:S(2)}, u32[]{:S(2)}) collective-permute-start(bf16[96,768]{1,0:T(8,128)(2,1)} %get-tuple-element.146), channel_id=1, source_target_pairs={{0,24},{8,0},{16,8},{24,16},{1,25},{9,1},{17,9},{25,17},{2,26},{10... | collective-permute-start | bytes 442376 | tf_op jit(solution)/shard_map/ppermute | solution.py:1152
  372.4 5.0 %copy-start = (bf16[2,2,96,3072]{3,2,1,0:T(8,128)(2,1)S(1)}, bf16[2,2,96,3072]{3,2,1,0:T(8,128)(2,1)}, u32[]{:S(2)}) copy-start(bf16[2,2,96,3072]{3,2,1,0:T(8,128)(2,1)} %get-tuple-element.116) | copy-start | bytes 7077892
  375.5 62.3 %collective-permute-start.12 = (bf16[384,768]{1,0:T(8,128)(2,1)}, bf16[384,768]{1,0:T(8,128)(2,1)S(1)}, u32[]{:S(2)}, u32[]{:S(2)}) collective-permute-start(bf16[384,768]{1,0:T(8,128)(2,1)} %get-tuple-element.139), channel_id=1, source_target_pairs={{0,4},{1,5},{2,6},{3,7},{4,0},{5,1},{6,2},{7,3},{8,12},{9,13},{10,... | collective-permute-start | bytes 1769480 | tf_op jit(solution)/shard_map/ppermute | solution.py:1127
  376.3 61.5 %collective-permute-start.13 = (bf16[384,768]{1,0:T(8,128)(2,1)}, bf16[384,768]{1,0:T(8,128)(2,1)}, u32[]{:S(2)}, u32[]{:S(2)}) collective-permute-start(bf16[384,768]{1,0:T(8,128)(2,1)} %get-tuple-element.138), channel_id=1, source_target_pairs={{0,2},{1,3},{2,0},{3,1},{4,6},{5,7},{6,4},{7,5},{8,10},{9,11},{10,... | collective-permute-start | bytes 1769480 | tf_op jit(solution)/shard_map/ppermute | solution.py:1127
  380.1 57.7 %collective-permute-start.10 = (bf16[96,3072]{1,0:T(8,128)(2,1)}, bf16[96,3072]{1,0:T(8,128)(2,1)S(1)}, u32[]{:S(2)}, u32[]{:S(2)}) collective-permute-start(bf16[96,3072]{1,0:T(8,128)(2,1)} %get-tuple-element.141), channel_id=1, source_target_pairs={{0,4},{1,5},{2,6},{3,7},{4,0},{5,1},{6,2},{7,3},{8,12},{9,13},{10,... | collective-permute-start | bytes 1769480 | tf_op jit(solution)/shard_map/ppermute | solution.py:1127
  381.0 56.9 %collective-permute-start.11 = (bf16[96,3072]{1,0:T(8,128)(2,1)}, bf16[96,3072]{1,0:T(8,128)(2,1)}, u32[]{:S(2)}, u32[]{:S(2)}) collective-permute-start(bf16[96,3072]{1,0:T(8,128)(2,1)} %get-tuple-element.140), channel_id=1, source_target_pairs={{0,2},{1,3},{2,0},{3,1},{4,6},{5,7},{6,4},{7,5},{8,10},{9,11},{10,... | collective-permute-start | bytes 1769480 | tf_op jit(solution)/shard_map/ppermute | solution.py:1127
  440.1 6.0 %collective-permute-start.15 = (bf16[384,768]{1,0:T(8,128)(2,1)S(1)}, bf16[384,768]{1,0:T(8,128)(2,1)S(1)}, u32[]{:S(2)}, u32[]{:S(2)}) collective-permute-start(bf16[384,768]{1,0:T(8,128)(2,1)S(1)} %get-tuple-element.133), channel_id=1, source_target_pairs={{0,1},{1,0},{2,3},{3,2},{4,5},{5,4},{6,7},{7,6},{8,9},{9,8},{10,11... | collective-permute-start | bytes 1769480 | tf_op jit(solution)/shard_map/ppermute | solution.py:1127
  442.2 5.6 %collective-permute-start.14 = (bf16[96,3072]{1,0:T(8,128)(2,1)S(1)}, bf16[96,3072]{1,0:T(8,128)(2,1)S(1)}, u32[]{:S(2)}, u32[]{:S(2)}) collective-permute-start(bf16[96,3072]{1,0:T(8,128)(2,1)S(1)} %get-tuple-element.136), channel_id=1, source_target_pairs={{0,1},{1,0},{2,3},{3,2},{4,5},{5,4},{6,7},{7,6},{8,9},{9,8},{10,11... | collective-permute-start | bytes 1769480 | tf_op jit(solution)/shard_map/ppermute | solution.py:1127
  (9 other events, 22.0 us)
Sparse Core Ops, SparseCore 0:
  9.9 78.2 all-gather.2
  90.2 83.0 all-gather.4
